TPU v7x, 32 devices: a whole 2x2x4 slice. The times are simulated.
32 devices in a mesh: dp: 8 (over y, x, core), stream: 4 (over z).
Axes of the slice: x: 2, y: 2, z: 4, core: 2. Of those that a mesh axis runs over, the one named last changes fastest.
Arguments:
- history: bfloat16 [8, 4096, 2048], P(None, 'dp'), may hold values from -6 to 6
- mixing: float32 [4096, 4, 8], P('dp', 'stream'), may hold values from -2 to 2
- shard_offset: int32 [8], P('dp'), may hold values from 0 to 3584, as said below
- norm_gain: bfloat16 [4, 2048], P('stream'), may hold values from 0.099609375 to 1.8984375
- norm_bias: bfloat16 [4, 2048], P('stream'), may hold values from -1.75 to 1.75
- w_heads: bfloat16 [3, 2048, 2048], P(None, 'dp', 'stream'), may hold values from -0.125 to 0.125
- w_merge: bfloat16 [2048, 2048], P('stream', 'dp'), may hold values from -3 to 3
- w_up: bfloat16 [2048, 8192], P('dp', 'stream'), may hold values from -0.125 to 0.125
- w_down: bfloat16 [8192, 2048], P('stream', 'dp'), may hold values from -0.0625 to 0.0625
- mixer_first: bfloat16 [2048, 36], P('stream'), may hold values from -0.125 to 0.125
- mixer_second: bfloat16 [36, 4, 9], P(None, 'stream'), may hold values from -1 to 1
- out_cotangent: bfloat16 [4096, 2048], P('dp', 'stream'), may hold values from -6 to 6
- next_cotangent: float32 [4096, 4, 9], P('dp', 'stream'), may hold values from -6 to 6
Outputs:
- block_out: bfloat16 [4096, 2048], P('dp', 'stream')
- next_mixing: float32 [4096, 4, 9], P('dp', 'stream')
- grad_history: float32 [8, 4096, 2048], P('stream', 'dp')
- grad_mixing: float32 [4096, 4, 8], P('dp', 'stream')
- grad_gain: float32 [4, 2048], P('stream')
- grad_bias: float32 [4, 2048], P('stream')
- grad_heads: float32 [3, 2048, 2048], P(None, 'dp', 'stream')
- grad_merge: float32 [2048, 2048], P('stream', 'dp')
- grad_up: float32 [2048, 8192], P('dp', 'stream')
- grad_down: float32 [8192, 2048], P('stream', 'dp')
- grad_first: float32 [2048, 36], P('stream')
- grad_second: float32 [36, 4, 9], P(None, 'stream')
Inputs may be any that keep to these rules, and one draw needn't show every extreme that they name: `shard_offset`: sequences of 2048 and 4096 tokens are packed end to end, each new one starting at the first token of a shard; the first may have begun before the first token and the last may be cut off at the end. Entry i is the position, within its sequence, of the first token of shard i.
All inputs are finite; a program needn't handle non-finite values.
Results may differ from a plain program's by a relative error of at most 0.012.
Values may be sent and summed in bfloat16 or wider, within the bound.
No kernel may reach another device: no remote copies, remote signals or barrier semaphores. Data moves between devices by JAX's collectives and lax.ppermute only.
A program may use at most 256 MiB of HBM per device.

v0:
```python
import math

import jax
import jax.numpy as jnp
from jax import lax
from jax.experimental import pallas as pl
from jax.experimental.pallas import tpu as pltpu
from jax.sharding import PartitionSpec as P

HD = 128
ROT = 32
SEQ = 2048


def passed_along(shard, axis, by):
    peers = lax.axis_size(axis)
    pairs = [(i, i + by) for i in range(peers) if 0 <= i + by < peers]
    return lax.ppermute(shard, axis, pairs)


def rotate(vectors, positions, sign):
    half = ROT // 2
    counter = jnp.arange(half, dtype=jnp.float32)
    freqs = jnp.exp(counter * (-2.0 * math.log(10000.0) / ROT))
    angles = positions.astype(jnp.float32)[:, None] * freqs[None, :]
    cosine = jnp.cos(angles)[:, None, :]
    sine = sign * jnp.sin(angles)[:, None, :]
    first = vectors[..., :half]
    second = vectors[..., half:ROT]
    return jnp.concatenate(
        [first * cosine - second * sine, second * cosine + first * sine, vectors[..., ROT:]],
        axis=-1,
    )


def exact_gelu(vectors):
    return jax.nn.gelu(vectors, approximate=False)


def block_logits(queries, keys_block, diagonal):
    logits = jnp.einsum("qhd,khd->hqk", queries, keys_block, preferred_element_type=jnp.float32) * (
        1.0 / math.sqrt(queries.shape[-1])
    )
    if diagonal:
        counter = jnp.arange(queries.shape[0], dtype=jnp.int32)
        allowed = counter[None, :] <= counter[:, None]
        logits = jnp.where(allowed[None], logits, -1e30)
    return logits


def keep_same(state):
    return state


BF = jnp.bfloat16
SHARE = 1.0
F32 = jnp.float32
OUTWARD = [(0, 1), (3, 2)]
MIDDLE = [(1, 2), (2, 1)]
INWARD = [(1, 0), (2, 3)]


def dot(left, right):
    return jnp.dot(left, right, preferred_element_type=F32)


def dot_rows(left, right):
    return lax.dot_general(left, right, (((0,), (0,)), ((), ())), preferred_element_type=F32)


def dot_cols(left, right):
    return lax.dot_general(left, right, (((1,), (1,)), ((), ())), preferred_element_type=F32)


def partner(shard, bit):
    peers = lax.axis_size("dp")
    return lax.ppermute(shard, "dp", [(i, i ^ bit) for i in range(peers)])


def line_hop(shard, pairs):
    return lax.ppermute(shard, "stream", pairs)


def cost(microseconds):
    return pl.CostEstimate(
        flops=int(microseconds * SHARE * 0.9e9),
        bytes_accessed=int(microseconds * SHARE * 3e6),
        transcendentals=0,
    )


def after(value, *others):
    return lax.optimization_barrier((value, *others))[0]


class Gathered:
    def __init__(self, shard, direct=False):
        self.shard = shard
        self.peers = lax.axis_size("dp")
        if self.peers != 8:
            self.by_x = self.by_y = shard
            return
        self.cut = max(range(shard.ndim - 1), key=lambda dim: shard.shape[dim])
        self.by_x = partner(shard, 2)
        self.by_y = partner(shard, 4)
        self.across = partner(shard, 6) if direct else None

    def whole(self, *earlier):
        shard = self.shard
        if self.peers != 8:
            return lax.all_gather(shard, "dp", axis=0)
        index = lax.axis_index("dp")
        cut = self.cut
        half = shard.shape[cut] // 2
        shard, by_x, by_y = [gated(item, earlier) for item in (shard, self.by_x, self.by_y)]
        pieces = [(shard, 0, 0), (by_x, 2, 0), (by_y, 4, 0)]
        if self.across is None:
            low = lax.slice_in_dim(by_y, 0, half, axis=cut)
            high = lax.slice_in_dim(by_x, half, 2 * half, axis=cut)
            pieces += [(partner(low, 2), 6, 0), (partner(high, 4), 6, half)]
        else:
            pieces.append((gated(self.across, earlier), 6, 0))
        pieces += [(partner(piece, 1), code ^ 1, start) for piece, code, start in pieces]
        return put_together(pieces, shard, self.peers, cut, index)


def put_together(pieces, shard, peers, cut, index):
    codes = [(code, start) for _, code, start in pieces]
    arrays = [piece for piece, _, _ in pieces]

    def kernel(place, *refs):
        out, held, sems, sent = refs[-4:]
        owners = {}
        for n, (code, start) in enumerate(codes):
            size = refs[n].shape[cut]
            span = tuple(
                pl.ds(start, size) if dim == cut else slice(None) for dim in range(shard.ndim)
            )
            copy = pltpu.make_async_copy(refs[n], held.at[(code, *span)], sems.at[n])
            copy.start()
            owners.setdefault(code, []).append(copy)
        leaving = []
        for code, copies in owners.items():
            for copy in copies:
                copy.wait()
            copy = pltpu.make_async_copy(held.at[code], out.at[place[0] ^ code], sent.at[code])
            copy.start()
            leaving.append(copy)
        for copy in leaving:
            copy.wait()

    anywhere = pl.BlockSpec(memory_space=pl.ANY)
    size = peers * shard.size * shard.dtype.itemsize
    return pl.pallas_call(
        kernel,
        in_specs=[pl.BlockSpec(memory_space=pltpu.SMEM)] + [anywhere] * len(arrays),
        out_specs=anywhere,
        out_shape=jax.ShapeDtypeStruct((peers, *shard.shape), shard.dtype),
        scratch_shapes=[
            pltpu.VMEM((peers, *shard.shape), shard.dtype),
            pltpu.SemaphoreType.DMA((len(arrays),)),
            pltpu.SemaphoreType.DMA((peers,)),
        ],
        cost_estimate=cost(2 * size / 3e6),
        name="put_together",
    )(index.astype(jnp.int32).reshape(1), *arrays)


def block_spans(tokens):
    sizes = [tokens // 4] * 3 + [tokens // 8] * 2
    return [(sum(sizes[:i]), size) for i, size in enumerate(sizes)]


def along_line(count, first, second, third, finish=None):
    ones, twos, threes, ends = [], [], [], []
    for step in range(count + 2):
        old = []
        if step >= 4:
            old.append(threes[step - 4] if finish is None else ends[step - 4])
        if step < count:
            gates = list(old)
            if step >= 2:
                gates.append(ones[step - 2])
            if step >= 3:
                gates.append(twos[step - 3])
            ones.append(line_hop(first(step, gates), OUTWARD))
        if 0 <= step - 1 < count:
            load = second(step - 1, ones[step - 1])
            twos.append(line_hop(gated(load, old), MIDDLE))
        if 0 <= step - 2 < count:
            back = step - 2
            load = third(back, ones[back], twos[back])
            threes.append(line_hop(gated(load, old), INWARD))
            if finish is not None:
                ends.append(finish(back, ones[back], twos[back], threes[back]))
    return ones, twos, threes


def gated(value, gates):
    return after(value, *gates) if gates else value


def rope_tables(positions, sign):
    half = ROT // 2
    lane = jnp.arange(HD, dtype=jnp.int32)
    counter = (lane % half).astype(F32)
    freqs = jnp.exp(counter * (-2.0 * math.log(10000.0) / ROT))
    angles = positions.astype(F32)[:, None] * freqs[None, :]
    cosine = jnp.where(lane < ROT, jnp.cos(angles), 1.0)
    sine = sign * jnp.sin(angles)
    up = jnp.where(lane < half, -sine, 0.0)
    down = jnp.where((lane >= half) & (lane < ROT), sine, 0.0)
    return jnp.stack([cosine, up, down])


def turned(block, tables):
    half = ROT // 2
    return (
        block * tables[0]
        + pltpu.roll(block, HD - half, 1) * tables[1]
        + pltpu.roll(block, half, 1) * tables[2]
    )


def make_streams(history, mix_rows, gains, biases):
    entries, tokens, width = history.shape
    streams = gains.shape[0]
    rows, sub, lanes = min(64, tokens), 16, 512

    def kernel(hist, mix, gain, bias, normed, unit, inv, last, scratch):
        def step(r, carry):
            here = pl.ds(pl.multiple_of(r * sub, sub), sub)
            weights = mix[here, :]
            columns = [
                [weights[:, s * entries + j : s * entries + j + 1] for j in range(entries)]
                for s in range(streams)
            ]
            for lane in range(0, width, lanes):
                span = slice(lane, lane + lanes)
                sums = [None] * streams
                for j in range(entries):
                    part = hist[j, here, span].astype(F32)
                    for s in range(streams):
                        term = columns[s][j] * part
                        sums[s] = term if j == 0 else sums[s] + term
                for s in range(streams):
                    scratch[s, :, span] = sums[s]
            stds = []
            for s in range(streams):
                values = scratch[s]
                center = values - jnp.sum(values, axis=-1, keepdims=True) * (1.0 / width)
                var = jnp.sum(center * center, axis=-1, keepdims=True) * (1.0 / width)
                std = lax.rsqrt(var + 1e-05)
                stds.append(std)
                scaled = center * std
                unit[s, here, :] = scaled.astype(BF)
                normed[s, here, :] = (scaled * gain[s : s + 1] + bias[s : s + 1]).astype(BF)
            last[here, :] = scratch[streams - 1]
            inv[here, :] = jnp.concatenate(stds, axis=-1)
            return carry

        lax.fori_loop(0, rows // sub, step, 0)

    wide = jax.ShapeDtypeStruct((streams, tokens, width), BF)
    return pl.pallas_call(
        kernel,
        grid=(tokens // rows,),
        in_specs=[
            pl.BlockSpec((entries, rows, width), lambda i: (0, i, 0)),
            pl.BlockSpec((rows, streams * entries), lambda i: (i, 0)),
            pl.BlockSpec((streams, width), lambda i: (0, 0)),
            pl.BlockSpec((streams, width), lambda i: (0, 0)),
        ],
        out_specs=[
            pl.BlockSpec((streams, rows, width), lambda i: (0, i, 0)),
            pl.BlockSpec((streams, rows, width), lambda i: (0, i, 0)),
            pl.BlockSpec((rows, streams), lambda i: (i, 0)),
            pl.BlockSpec((rows, width), lambda i: (i, 0)),
        ],
        out_shape=[
            wide,
            wide,
            jax.ShapeDtypeStruct((tokens, streams), F32),
            jax.ShapeDtypeStruct((tokens, width), F32),
        ],
        scratch_shapes=[pltpu.VMEM((streams, sub, width), F32)],
        cost_estimate=cost(22),
        name="make_streams",
    )(history, mix_rows, gains, biases)


def project(normed, w_heads, tables):
    _, tokens, width = normed.shape
    columns = w_heads.shape[3]
    heads, half = columns // HD, tokens // 2

    def kernel(x, w, table, out):
        flat = dot(x[0], w[...].reshape(width, columns))
        turn = pl.program_id(0) < 2

        def put(head, block):
            out[2 * head, 0] = block[:half].astype(BF)
            out[2 * head + 1, 0] = block[half:].astype(BF)

        @pl.when(turn)
        def _():
            for head in range(heads):
                put(head, turned(flat[:, head * HD : (head + 1) * HD], table[...]))

        @pl.when(jnp.logical_not(turn))
        def _():
            for head in range(heads):
                put(head, flat[:, head * HD : (head + 1) * HD])

    return pl.pallas_call(
        kernel,
        grid=(3,),
        in_specs=[
            pl.BlockSpec((1, tokens, width), lambda c: (c, 0, 0)),
            pl.BlockSpec((w_heads.shape[0], 1, w_heads.shape[2], columns), lambda c: (0, c, 0, 0)),
            pl.BlockSpec((3, tokens, HD), lambda c: (0, 0, 0)),
        ],
        out_specs=pl.BlockSpec((2 * heads, 1, half, HD), lambda c: (0, c, 0, 0)),
        out_shape=jax.ShapeDtypeStruct((2 * heads, 3, half, HD), BF),
        cost_estimate=cost(9),
        name="project",
    )(normed, w_heads, tables)


def attend(own, other, first_key, side):
    shards, _, half, _ = own.shape
    factor = 1.0 / math.sqrt(HD)

    def kernel(first, part, mine, theirs, out, exact, norm):
        s = pl.program_id(0)
        query = mine[s, 0]

        def fold(state, keys, values, mask):
            top, total, acc = state
            logits = dot_cols(query, keys) * factor
            if mask is not None:
                logits = jnp.where(mask, logits, -1e30)
            new_top = jnp.maximum(top, jnp.max(logits, axis=-1, keepdims=True))
            probs = jnp.exp(logits - new_top)
            keep = jnp.exp(top - new_top)
            return (
                new_top,
                total * keep + jnp.sum(probs, axis=-1, keepdims=True),
                acc * keep + dot(probs.astype(BF), values),
            )

        row = lax.broadcasted_iota(jnp.int32, (half, half), 0)
        col = lax.broadcasted_iota(jnp.int32, (half, half), 1)
        state = (
            jnp.full((half, 1), -1e30, F32),
            jnp.zeros((half, 1), F32),
            jnp.zeros((half, HD), F32),
        )
        state = fold(state, mine[s, 1], mine[s, 2], col <= row)
        state = lax.fori_loop(
            0, part[0], lambda i, st: fold(st, theirs[s, 0], theirs[s, 1], None), state
        )

        def shard_step(b, st):
            st = fold(st, mine[b, 1], mine[b, 2], None)
            return fold(st, theirs[b, 0], theirs[b, 1], None)

        top, total, acc = lax.fori_loop(first[s], s, shard_step, state)
        result = acc / total
        out[0] = result.astype(BF)
        exact[0] = result
        norm[0] = top + jnp.log(total)

    return pl.pallas_call(
        kernel,
        grid_spec=pltpu.PrefetchScalarGridSpec(
            num_scalar_prefetch=2,
            grid=(shards,),
            in_specs=[
                pl.BlockSpec((shards, 3, half, HD), lambda s, *_: (0, 0, 0, 0)),
                pl.BlockSpec((shards, 2, half, HD), lambda s, *_: (0, 0, 0, 0)),
            ],
            out_specs=[
                pl.BlockSpec((1, half, HD), lambda s, *_: (s, 0, 0)),
                pl.BlockSpec((1, half, HD), lambda s, *_: (s, 0, 0)),
                pl.BlockSpec((1, half, 1), lambda s, *_: (s, 0, 0)),
            ],
        ),
        out_shape=[
            jax.ShapeDtypeStruct((shards, half, HD), BF),
            jax.ShapeDtypeStruct((shards, half, HD), F32),
            jax.ShapeDtypeStruct((shards, half, 1), F32),
        ],
        cost_estimate=cost(16),
        name="attend",
    )(first_key, side, own, other)


def attend_back(own, other, grads, exact, norm, first_key, side):
    shards, _, half, _ = own.shape
    factor = 1.0 / math.sqrt(HD)

    def kernel(first, part, mine, theirs, grad_ref, exact_ref, norm_ref, kept, given, sums):
        s = pl.program_id(0)
        query = mine[s, 0]
        grad = grad_ref[s]
        delta = jnp.sum(grad.astype(F32) * exact_ref[0], axis=-1, keepdims=True)
        level = norm_ref[0]
        lowered = grad

        @pl.when(s == 0)
        def _():
            sums[...] = jnp.zeros_like(sums)

        def fold(query_grad, keys, values, mask, slot, b):
            logits = dot_cols(query, keys) * factor
            probs = jnp.exp(logits - level)
            if mask is not None:
                probs = jnp.where(mask, probs, 0.0)
            score = (probs * (dot_cols(grad, values) - delta)).astype(BF)
            sums[slot, b] += dot_rows(score, query)
            sums[slot + 1, b] += dot_rows(probs.astype(BF), lowered)
            return query_grad + dot(score, keys)

        row = lax.broadcasted_iota(jnp.int32, (half, half), 0)
        col = lax.broadcasted_iota(jnp.int32, (half, half), 1)
        total = fold(jnp.zeros((half, HD), F32), mine[s, 1], mine[s, 2], col <= row, 0, s)
        total = lax.fori_loop(
            0, part[0], lambda i, q: fold(q, theirs[s, 0], theirs[s, 1], None, 2, s), total
        )

        def shard_step(b, q):
            q = fold(q, mine[b, 1], mine[b, 2], None, 0, b)
            return fold(q, theirs[b, 0], theirs[b, 1], None, 2, b)

        total = lax.fori_loop(first[s], s, shard_step, total)
        kept[s, 0] = (total * factor).astype(BF)

        @pl.when(s == shards - 1)
        def _():
            for b in range(shards):
                kept[b, 1] = (sums[0, b] * factor).astype(BF)
                kept[b, 2] = sums[1, b].astype(BF)
                given[b, 0] = (sums[2, b] * factor).astype(BF)
                given[b, 1] = sums[3, b].astype(BF)

    whole = lambda n: pl.BlockSpec((shards, n, half, HD), lambda s, *_: (0, 0, 0, 0))
    return pl.pallas_call(
        kernel,
        grid_spec=pltpu.PrefetchScalarGridSpec(
            num_scalar_prefetch=2,
            grid=(shards,),
            in_specs=[
                whole(3),
                whole(2),
                pl.BlockSpec((shards, half, HD), lambda s, *_: (0, 0, 0)),
                pl.BlockSpec((1, half, HD), lambda s, *_: (s, 0, 0)),
                pl.BlockSpec((1, half, 1), lambda s, *_: (s, 0, 0)),
            ],
            out_specs=[whole(3), whole(2)],
            scratch_shapes=[pltpu.VMEM((4, shards, half, HD), F32)],
        ),
        out_shape=[
            jax.ShapeDtypeStruct((shards, 3, half, HD), BF),
            jax.ShapeDtypeStruct((shards, 2, half, HD), BF),
        ],
        cost_estimate=cost(22),
        name="attend_back",
    )(first_key, side, own, other, grads, exact, norm)


def norm_back(grad, unit, inv, gain, extra):
    width = grad.shape[1]
    scaled = grad * gain
    mean = jnp.sum(scaled, axis=-1, keepdims=True) * (1.0 / width)
    slope = jnp.sum(scaled * unit, axis=-1, keepdims=True) * (1.0 / width)
    result = inv * (scaled - mean - unit * slope)
    return result if extra is None else result + extra


def heads_back(parts, w_heads, normed, unit, inv, gains, tables, spans):
    _, tokens, width = normed.shape
    columns = w_heads.shape[3]
    heads, half = columns // HD, tokens // 2
    count = len(spans)

    def kernel(part, w, x, u, istd, gain, table, *refs):
        pieces, (stream, weight, stats, grad, wide) = refs[:count], refs[count:]
        c = pl.program_id(0)
        turn = c < 2

        def take(head):
            return jnp.concatenate([part[2 * head, 0], part[2 * head + 1, 0]], axis=0).astype(F32)

        @pl.when(turn)
        def _():
            for head in range(heads):
                grad[:, head * HD : (head + 1) * HD] = turned(take(head), table[...]).astype(BF)

        @pl.when(jnp.logical_not(turn))
        def _():
            for head in range(heads):
                grad[:, head * HD : (head + 1) * HD] = take(head).astype(BF)

        wide[...] = dot_cols(grad[...], w[...].reshape(width, columns))
        weight[0] = dot_rows(x[0], grad[...]).astype(BF)
        stats[...] = jnp.zeros_like(stats)
        for r, (start, block) in enumerate(spans):
            column = lax.broadcasted_iota(jnp.int32, (block, istd.shape[1]), 1)
            here = slice(start, start + block)
            values = wide[here, :]
            units = u[0, here, :].astype(F32)
            std = jnp.sum(jnp.where(column == c, istd[here, :], 0.0), axis=-1, keepdims=True)
            result = norm_back(values, units, std, gain[0], None).astype(BF)
            stream[0, here, :] = result
            pieces[r][0] = result
            stats[0, 0:1] += jnp.sum(values * units, axis=0, keepdims=True)
            stats[0, 1:2] += jnp.sum(values, axis=0, keepdims=True)

    return pl.pallas_call(
        kernel,
        grid=(3,),
        in_specs=[
            pl.BlockSpec((2 * heads, 1, half, HD), lambda c: (0, c, 0, 0)),
            pl.BlockSpec((w_heads.shape[0], 1, w_heads.shape[2], columns), lambda c: (0, c, 0, 0)),
            pl.BlockSpec((1, tokens, width), lambda c: (c, 0, 0)),
            pl.BlockSpec((1, tokens, width), lambda c: (c, 0, 0)),
            pl.BlockSpec((tokens, inv.shape[1]), lambda c: (0, 0)),
            pl.BlockSpec((1, 1, width), lambda c: (c, 0, 0)),
            pl.BlockSpec((3, tokens, HD), lambda c: (0, 0, 0)),
        ],
        out_specs=[pl.BlockSpec((1, block, width), lambda c: (c, 0, 0)) for _, block in spans]
        + [
            pl.BlockSpec((1, tokens, width), lambda c: (c, 0, 0)),
            pl.BlockSpec((1, width, columns), lambda c: (c, 0, 0)),
            pl.BlockSpec((1, 2, width), lambda c: (c, 0, 0)),
        ],
        out_shape=[jax.ShapeDtypeStruct((3, block, width), BF) for _, block in spans]
        + [
            jax.ShapeDtypeStruct((3, tokens, width), BF),
            jax.ShapeDtypeStruct((3, width, columns), BF),
            jax.ShapeDtypeStruct((3, 2, width), F32),
        ],
        scratch_shapes=[pltpu.VMEM((tokens, columns), BF), pltpu.VMEM((tokens, width), F32)],
        cost_estimate=cost(3),
        name="heads_back",
    )(parts, w_heads, normed, unit, inv, gains[:, None, :], tables)


def last_back(grad, unit, inv, gain, extra, flag):
    tokens, width = grad.shape
    block = min(128, tokens)

    def kernel(g, u, istd, gain_ref, e, flag_ref, stream, stats):
        @pl.when(pl.program_id(0) == 0)
        def _():
            stats[...] = jnp.zeros_like(stats)

        values = g[...]
        units = u[...].astype(F32)
        std = istd[...][:, -1:]
        added = e[...].astype(F32) * flag_ref[0]
        stream[...] = norm_back(values, units, std, gain_ref[...], added).astype(BF)
        stats[0:1] += jnp.sum(values * units, axis=0, keepdims=True)
        stats[1:2] += jnp.sum(values, axis=0, keepdims=True)

    row = lambda n: pl.BlockSpec((block, n), lambda i: (i, 0))
    return pl.pallas_call(
        kernel,
        grid=(tokens // block,),
        in_specs=[
            row(width),
            row(width),
            row(inv.shape[1]),
            pl.BlockSpec((1, width), lambda i: (0, 0)),
            row(width),
            pl.BlockSpec(memory_space=pltpu.SMEM),
        ],
        out_specs=[row(width), pl.BlockSpec((2, width), lambda i: (0, 0))],
        out_shape=[
            jax.ShapeDtypeStruct((tokens, width), BF),
            jax.ShapeDtypeStruct((2, width), F32),
        ],
        cost_estimate=cost(7),
        name="last_back",
    )(grad, unit, inv, gain, extra, flag)


def mixing_back(heads_part, last_part, history, which, of):
    entries, tokens, width = history.shape
    streams = heads_part.shape[0] + 1
    rows, sub, lanes = min(64, tokens // of), 16, 256
    steps = tokens // of // rows
    base = which * steps

    def kernel(first, last, hist, out):
        def step(r, carry):
            here = pl.ds(pl.multiple_of(r * sub, sub), sub)
            for s in range(streams):
                sums = [None] * entries
                for lane in range(0, width, lanes):
                    span = slice(lane, lane + lanes)
                    part = first[s, here, span] if s < streams - 1 else last[here, span]
                    part = part.astype(F32)
                    for j in range(entries):
                        term = part * hist[j, here, span].astype(F32)
                        sums[j] = term if lane == 0 else sums[j] + term
                columns = [jnp.sum(item, axis=-1, keepdims=True) for item in sums]
                out[s, here, :] = jnp.concatenate(columns, axis=-1)
            return carry

        lax.fori_loop(0, rows // sub, step, 0)

    return pl.pallas_call(
        kernel,
        grid=(steps,),
        in_specs=[
            pl.BlockSpec((streams - 1, rows, width), lambda i: (0, base + i, 0)),
            pl.BlockSpec((rows, width), lambda i: (base + i, 0)),
            pl.BlockSpec((entries, rows, width), lambda i: (0, base + i, 0)),
        ],
        out_specs=pl.BlockSpec((streams, rows, entries), lambda i: (0, i, 0)),
        out_shape=jax.ShapeDtypeStruct((streams, tokens // of, entries), F32),
        cost_estimate=cost(0.4),
        name="mixing_back",
    )(heads_part, last_part, history)


def far_attend(queries, keys, values, shard_offset):
    tokens, heads_here, head_size = queries.shape
    data_index = lax.axis_index("dp")
    pairs = [jnp.stack([keys, values])]
    reach = 2 * SEQ // tokens
    for back in range(1, reach):
        pairs.append(passed_along(pairs[0], "dp", back))
    usable = [(shard_offset[0] >= back * tokens) & (data_index >= back) for back in range(reach)]
    first_logits = block_logits(queries, keys, True)
    top = jnp.max(first_logits, axis=-1)
    total = jnp.sum(jnp.exp(first_logits - top[..., None]), axis=-1)
    for back in range(1, reach):

        def widen(state, block=pairs[back][0]):
            logits = block_logits(queries, block, False)
            new_top = jnp.maximum(state[0], jnp.max(logits, axis=-1))
            summed = state[1] * jnp.exp(state[0] - new_top) + jnp.sum(
                jnp.exp(logits - new_top[..., None]), axis=-1
            )
            return (new_top, summed)

        top, total = lax.cond(usable[back], widen, keep_same, (top, total))
    log_total = top + jnp.log(total)
    attended = jnp.zeros((tokens, heads_here, head_size), F32)
    for back in range(reach):

        def accumulate(current, block=pairs[back], diagonal=back == 0):
            probs = jnp.exp(block_logits(queries, block[0], diagonal) - log_total[..., None])
            return current + jnp.einsum(
                "hqk,khd->qhd", probs.astype(BF), block[1], preferred_element_type=F32
            )

        attended = lax.cond(usable[back], accumulate, keep_same, attended)
    return attended, (pairs, usable, log_total)


def far_attend_back(queries, attended_grad, kept):
    tokens, heads_here, head_size = queries.shape
    factor = 1.0 / math.sqrt(head_size)
    pairs, usable, log_total = kept
    reach = len(pairs)

    def weights_of(block, diagonal):
        return jnp.exp(block_logits(queries, block, diagonal) - log_total[..., None])

    def prob_grads(block):
        return jnp.einsum("qhd,khd->hqk", attended_grad, block[1], preferred_element_type=F32)

    delta = jnp.zeros((heads_here, tokens), F32)
    for back in range(reach):

        def gather_delta(current, block=pairs[back], diagonal=back == 0):
            return current + jnp.sum(weights_of(block[0], diagonal) * prob_grads(block), axis=-1)

        delta = lax.cond(usable[back], gather_delta, keep_same, delta)

    def skip_block(current):
        return (current, jnp.zeros((2, tokens, heads_here, head_size), F32))

    query_grad = jnp.zeros((tokens, heads_here, head_size), F32)
    key_value_grad = jnp.zeros((2, tokens, heads_here, head_size), F32)
    for back in range(reach):

        def spread(current, block=pairs[back], diagonal=back == 0):
            probs = weights_of(block[0], diagonal)
            score_grad = (probs * (prob_grads(block) - delta[..., None])).astype(BF)
            query_part = (
                current
                + jnp.einsum("hqk,khd->qhd", score_grad, block[0], preferred_element_type=F32)
                * factor
            )
            key_part = (
                jnp.einsum("hqk,qhd->khd", score_grad, queries, preferred_element_type=F32)
                * factor
            )
            value_part = jnp.einsum(
                "hqk,qhd->khd", probs.astype(BF), attended_grad, preferred_element_type=F32
            )
            return (query_part, jnp.stack([key_part, value_part]))

        query_grad, pair_grad = lax.cond(usable[back], spread, skip_block, query_grad)
        if back == 0:
            key_value_grad = pair_grad
        else:
            key_value_grad = key_value_grad + passed_along(pair_grad, "dp", -back)
    return jnp.concatenate([query_grad[None], key_value_grad])


def mix_block(start, coefficients, shares, last_share, extras, last_extras, arrived, whole):
    streams, block, width = shares.shape
    each = coefficients.shape[1] // (streams + 1)
    groups = 1 + len(extras)
    final = arrived is not None
    lanes = 512

    def kernel(*refs):
        weights = refs[0][...]
        heads, lasts = refs[1 : 1 + groups], refs[1 + groups : 1 + 2 * groups]
        out = refs[-2] if final else refs[-1]
        if final:
            refs[-1][...] = jnp.zeros_like(refs[-1])
        columns = [weights[:, n : n + 1] for n in range(weights.shape[1])]
        for lane in range(0, width, lanes):
            span = slice(lane, lane + lanes)
            values = []
            for s in range(streams + 1):
                picks = [r[s, :, span] if s < streams else l[:, span] for r, l in zip(heads, lasts)]
                total = picks[0].astype(F32)
                for pick in picks[1:]:
                    total = total + pick.astype(F32)
                values.append(total)
            for e in range(each):
                total = columns[e * (streams + 1)] * values[0]
                for s in range(1, streams + 1):
                    total = total + columns[e * (streams + 1) + s] * values[s]
                if final:
                    total = total + refs[1 + 2 * groups][e, :, span].astype(F32)
                out[e, :, span] = total.astype(out.dtype)

    i = start // block
    piece = pl.BlockSpec((streams, block, width), lambda n: (0, 0, 0))
    rows = [
        pl.BlockSpec((block, width), lambda n, at=start % item.shape[0] // block: (at, 0))
        for item in (last_share, *last_extras)
    ]
    small = pl.BlockSpec((each, block, width), lambda n: (0, 0, 0))
    specs = [pl.BlockSpec((block, coefficients.shape[1]), lambda n: (i, 0))]
    specs += [piece] * groups + rows
    args = [coefficients, shares, *extras, last_share, *last_extras]
    alias = {}
    if final:
        specs.append(small)
        args.append(arrived)
        if whole is not None:
            specs.append(pl.BlockSpec(memory_space=pl.ANY))
            args.append(whole)
            alias = {len(args) - 1: 0}
        out_spec = [
            pl.BlockSpec((each, block, width), lambda n: (0, i, 0)),
            pl.BlockSpec((8, 128), lambda n: (0, 0)),
        ]
        out_shape = [
            jax.ShapeDtypeStruct((each, coefficients.shape[0], width), F32),
            jax.ShapeDtypeStruct((8, 128), F32),
        ]
    else:
        out_spec, out_shape = small, jax.ShapeDtypeStruct((each, block, width), BF)
    return pl.pallas_call(
        kernel,
        grid=(1,),
        in_specs=specs,
        out_specs=out_spec,
        out_shape=out_shape,
        input_output_aliases=alias,
        cost_estimate=cost(0.4),
        name="mix_final" if final else "mix_inward",
    )(*args)


def hidden_units(x, w_up):
    tokens, width = x.shape
    units = w_up.shape[1]
    block = min(512, units)

    def kernel(x_ref, w, out, slope):
        up = dot(x_ref[...], w[...])
        inside = 0.5 * (1.0 + lax.erf(up * math.sqrt(0.5)))
        out[...] = (up * inside).astype(BF)
        bell = jnp.exp(-0.5 * up * up) * (1.0 / math.sqrt(2.0 * math.pi))
        slope[...] = (inside + up * bell).astype(BF)

    column = pl.BlockSpec((tokens, block), lambda i: (0, i))
    return pl.pallas_call(
        kernel,
        grid=(units // block,),
        in_specs=[
            pl.BlockSpec((tokens, width), lambda i: (0, 0)),
            pl.BlockSpec((width, block), lambda i: (0, i)),
        ],
        out_specs=[column, column],
        out_shape=[jax.ShapeDtypeStruct((tokens, units), BF)] * 2,
        cost_estimate=cost(9),
        name="hidden_units",
    )(x, w_up)


def merge_branches(attended, hidden, w_merge, w_down, stream, flag):
    tokens, inner = attended.shape
    shards, units, cols = w_down.shape
    members = lax.axis_size("stream")
    each = shards // members
    if cols % 128:
        merged = jnp.einsum("te,ned->tnd", attended, w_merge, preferred_element_type=F32)
        merged = merged + jnp.einsum("tf,nfd->tnd", hidden, w_down, preferred_element_type=F32)
        merged = merged.reshape(tokens, -1) + flag * stream
        return jnp.transpose(merged.reshape(tokens, members, -1), (1, 0, 2)).astype(BF)

    def kernel(a, h, wm, wd, st, flag_ref, out):
        out[0] = (dot(a[...], wm[0]) + dot(h[...], wd[0]) + flag_ref[0] * st[...]).astype(BF)

    return pl.pallas_call(
        kernel,
        grid=(shards,),
        in_specs=[
            pl.BlockSpec((tokens, inner), lambda n: (0, 0)),
            pl.BlockSpec((tokens, units), lambda n: (0, 0)),
            pl.BlockSpec((1, inner, cols), lambda n: (n, 0, 0)),
            pl.BlockSpec((1, units, cols), lambda n: (n, 0, 0)),
            pl.BlockSpec((tokens, cols), lambda n: (0, n)),
            pl.BlockSpec(memory_space=pltpu.SMEM),
        ],
        out_specs=pl.BlockSpec((1, tokens, cols), lambda n: (n // each, 0, n % each)),
        out_shape=jax.ShapeDtypeStruct((members, tokens, each * cols), BF),
        cost_estimate=cost(13),
        name="merge_branches",
    )(attended, hidden, w_merge, w_down, stream, flag)


def back_through(grad, stacked, slope):
    tokens = grad.shape[0]
    shards, units, cols = stacked.shape
    if cols % 128:
        split = grad.reshape(tokens, shards, cols)
        total = jnp.einsum("tnd,nfd->tf", split, stacked, preferred_element_type=F32)
        return (total if slope is None else total * slope.astype(F32)).astype(BF)

    def kernel(*refs):
        g, w = refs[:2]
        out, acc = refs[-2:]
        n = pl.program_id(0)
        part = dot_cols(g[...], w[0])

        @pl.when(n == 0)
        def _():
            acc[...] = part

        @pl.when(n > 0)
        def _():
            acc[...] += part

        @pl.when(n == shards - 1)
        def _():
            total = acc[...]
            if slope is not None:
                total = total * refs[2][...].astype(F32)
            out[...] = total.astype(BF)

    specs = [
        pl.BlockSpec((tokens, cols), lambda n: (0, n)),
        pl.BlockSpec((1, units, cols), lambda n: (n, 0, 0)),
    ]
    args = [grad, stacked]
    if slope is not None:
        specs.append(pl.BlockSpec((tokens, units), lambda n: (0, 0)))
        args.append(slope)
    return pl.pallas_call(
        kernel,
        grid=(shards,),
        in_specs=specs,
        out_specs=pl.BlockSpec((tokens, units), lambda n: (0, 0)),
        out_shape=jax.ShapeDtypeStruct((tokens, units), BF),
        scratch_shapes=[pltpu.VMEM((tokens, units), F32)],
        cost_estimate=cost(13 if slope is not None else 7),
        name="back_through",
    )(*args)


def body(
    history,
    mixing,
    shard_offset,
    norm_gain,
    norm_bias,
    w_heads,
    w_merge,
    w_up,
    w_down,
    mixer_first,
    mixer_second,
    out_cotangent,
    next_cotangent,
):
    member = lax.axis_index("stream")
    members = lax.axis_size("stream")
    shards = lax.axis_size("dp")
    index = lax.axis_index("dp")
    entries, tokens, width = history.shape
    heads_here = w_heads.shape[2] // HD
    half = tokens // 2
    highest = lax.Precision.HIGHEST
    flag = (member == members - 1).astype(F32)
    flags = flag.reshape(1)
    near = shards == 8 and heads_here * 2 == shards and tokens * shards == 2 * SEQ

    if near:
        spread = jnp.broadcast_to(shard_offset[:, None], (8, 128))
        offsets = lax.all_gather(spread, "dp", axis=0)[:, 0, 0]
        w_heads = after(w_heads, offsets)
    got_heads = Gathered(w_heads, direct=near)
    lanes = jnp.concatenate([norm_gain, norm_bias]).astype(F32).reshape(tokens, -1)
    first_rows = mixer_first.astype(F32).reshape(tokens, -1)
    second_flat = mixer_second[:, 0, :].astype(F32).reshape(-1)
    hidden_count = mixer_second.shape[0]
    lines = -(-second_flat.shape[0] // tokens)
    second_rows = jnp.pad(second_flat, (0, lines * tokens - second_flat.shape[0]))
    outputs = next_cotangent.shape[2]
    arrays = [mixing[:, 0, :], lanes, next_cotangent[:, 0, :], first_rows]
    arrays.append(second_rows.reshape(tokens, lines))
    packed = lax.all_gather(jnp.concatenate(arrays, axis=1), "stream", axis=0)
    parts, place = [], 0
    for array in arrays:
        parts.append(packed[:, :, place : place + array.shape[1]])
        place += array.shape[1]
    mix_all, norms, next_full, first_full, second_full = parts
    norms = norms.reshape(members, 2, width)
    first_full = first_full.astype(BF).reshape(width, -1)
    second_full = second_full.reshape(members, -1)[:, : second_flat.shape[0]]
    second_full = second_full.reshape(members, hidden_count, outputs)
    if near:
        early = (got_heads.by_x, got_heads.by_y, got_heads.across)
        history = after(history, *early)
        w_up, w_merge = after(w_up, *early[:2]), after(w_merge, *early[:2])
    got_up = Gathered(w_up)
    got_merge = Gathered(w_merge, direct=near)
    gains, biases = norms[:, 0], norms[:, 1]
    mix_rows = jnp.transpose(mix_all, (1, 0, 2)).reshape(tokens, members * entries)

    normed, unit, inv, stream = make_streams(history, mix_rows, gains, biases)
    full_heads = got_heads.whole()
    cotangent = lax.all_gather(after(out_cotangent, inv), "stream", axis=1, tiled=True)
    positions = shard_offset[0] + jnp.arange(tokens, dtype=jnp.int32)
    projected = project(after(normed, got_up.by_x, got_up.by_y), full_heads, rope_tables(positions, 1.0))

    if near:
        side = (index % 2).astype(jnp.int32).reshape(1)
        place = jnp.arange(shards, dtype=jnp.int32)
        first_key = jnp.maximum(place - offsets // tokens, 0).astype(jnp.int32)
        own = lax.all_to_all(projected, "dp", 0, 0, tiled=True)
        got_down = Gathered(after(w_down, own))
        other = partner(own[:, 1:], 1)
        result, exact, level = attend(own, other, first_key, side)
        full_up = got_up.whole(result)
        full_merge = got_merge.whole(result)
        back = lax.all_to_all(result, "dp", 0, 0, tiled=True)
        attended = jnp.transpose(back.reshape(heads_here, tokens, HD), (1, 0, 2)).reshape(tokens, -1)
    else:
        got_down = Gathered(w_down)
        full_up = got_up.whole()
        full_merge = got_merge.whole()
        split = projected.reshape(heads_here, 2, 3, half, HD)
        split = jnp.transpose(split, (2, 1, 3, 0, 4)).reshape(3, tokens, heads_here, HD)
        result, kept = far_attend(split[0], split[1], split[2], shard_offset)
        attended = result.reshape(tokens, -1).astype(BF)
    full_down = got_down.whole(result)
    flat_up = full_up.reshape(width, -1)
    hidden, slope = hidden_units(normed[members - 1], flat_up)
    attended = after(attended, hidden)
    hidden = after(hidden, cotangent)
    share = merge_branches(attended, hidden, full_merge, full_down, stream, flags)

    columns = lax.all_to_all(share, "stream", 0, 0, tiled=True)
    block_out = jnp.sum(columns.astype(F32), axis=0).astype(BF)
    block_full = lax.all_gather(block_out, "stream", axis=1, tiled=True)
    out_float = block_full.astype(F32)
    scale = lax.rsqrt(jnp.sum(out_float * out_float, axis=-1) / width + 1e-06)
    proj = dot(block_full, first_full)
    mixer, mixer_back = jax.vjp(exact_gelu, scale[:, None] * proj)
    second_here = mixer_second[:, 0, :].astype(F32)
    next_here = jnp.dot(mixer, second_here, precision=highest, preferred_element_type=F32)
    mixer_grad = jnp.einsum(
        "stn,scn->tc", next_full, second_full, precision=highest, preferred_element_type=F32
    )
    pre_grad = mixer_back(mixer_grad)[0]
    proj_grad = (scale[:, None] * pre_grad).astype(BF)
    scale_grad = jnp.sum(pre_grad * proj, axis=-1)
    second_local = jnp.dot(
        mixer.T, next_cotangent[:, 0, :], precision=highest, preferred_element_type=F32
    )
    first_local = dot_rows(block_out, proj_grad)
    grad_out = (
        cotangent.astype(F32)
        + dot_cols(proj_grad, first_full)
        - (scale * scale * scale * scale_grad)[:, None] * out_float / width
    ).astype(BF)

    attended_grad = back_through(grad_out, full_merge, None)
    up_grad = back_through(grad_out, full_down, slope)
    down_grad = dot_rows(hidden, grad_out).astype(BF)
    grad_down = lax.psum_scatter(down_grad, "dp", scatter_dimension=1, tiled=True).astype(F32)
    last_normed = dot_cols(after(up_grad, down_grad), flat_up)
    last_share, last_stats = last_back(
        last_normed, unit[members - 1], inv, gains[members - 1 :], grad_out, flags
    )
    last_hop = line_hop(last_share, OUTWARD)
    last_sum = (last_share.astype(F32) + last_hop.astype(F32)).astype(BF)
    last_next = line_hop(last_sum, MIDDLE)
    if near:
        sent = attended_grad.reshape(tokens, heads_here, HD)
        sent = jnp.transpose(sent, (1, 0, 2)).reshape(shards, half, HD)
        grads = lax.all_to_all(sent, "dp", 0, 0, tiled=True)
        grads = after(grads, last_share)
        kept_grads, given = attend_back(own, other, grads, exact, level, first_key, side)
        taken = partner(given, 1)
        summed = kept_grads[:, 1:].astype(F32) + taken.astype(F32)
        pair = jnp.concatenate([kept_grads[:, :1], summed.astype(BF)], axis=1)
        pair = after(pair, last_hop)
        late_grad, late_up = after(grad_out, pair), after(up_grad, pair)
        up_back = dot_rows(normed[members - 1], late_up).astype(BF)
        merge_grad = dot_rows(attended, late_grad).astype(BF)
        parts = lax.all_to_all(pair, "dp", 0, 0, tiled=True)
    else:
        up_back = dot_rows(normed[members - 1], up_grad).astype(BF)
        merge_grad = dot_rows(attended, grad_out).astype(BF)
        grads = far_attend_back(split[0], attended_grad.reshape(tokens, heads_here, HD), kept)
        parts = grads.reshape(3, 2, half, heads_here, HD)
        parts = jnp.transpose(parts, (3, 1, 0, 2, 4)).reshape(2 * heads_here, 3, half, HD)

    parts = after(parts, last_sum, grad_down, up_back, merge_grad)
    spans = block_spans(tokens)
    *pieces, heads_share, heads_grad, heads_stats = heads_back(
        parts, full_heads, normed, unit, inv, gains, rope_tables(positions, -1.0), spans
    )

    grad_merge = lax.psum_scatter(merge_grad, "dp", scatter_dimension=1, tiled=True).astype(F32)
    grad_heads = lax.psum_scatter(heads_grad, "dp", scatter_dimension=1, tiled=True).astype(F32)
    grad_up = lax.psum_scatter(up_back, "dp", scatter_dimension=0, tiled=True).astype(F32)

    each = entries // members

    def weights_for(owner):
        block = lax.dynamic_slice_in_dim(mix_all, owner * each, each, axis=2)
        return jnp.transpose(block, (1, 2, 0)).reshape(tokens, each * members)

    there = weights_for(jnp.where(member == 1, 0, members - 1))
    here = weights_for(member)
    extra = {}

    last_one = lambda i: last_hop
    last_two = lambda i: last_next

    def first_hop(i, gates):
        gates = list(gates)
        if i == 3:
            gates.append(grad_merge)
        return gated(pieces[i], gates)

    def small_sums():
        stats = jnp.concatenate([heads_stats, last_stats[None]]).reshape(members, tokens, -1)
        both = jnp.concatenate([jnp.concatenate(mixes, axis=1), stats], axis=2)
        both = jnp.sum(lax.all_to_all(both, "stream", 0, 0, tiled=True), axis=0)
        second_sums = jnp.pad(second_local.reshape(-1), (0, lines * tokens - second_flat.shape[0]))
        local = [both[:, entries:], first_local.reshape(tokens, -1), second_sums.reshape(tokens, lines)]
        everyone = lax.all_gather(jnp.concatenate(local, axis=1), "dp", axis=0)
        return both[:, :entries], jnp.sum(everyone, axis=0)

    mixes = []

    def second_hop(i, one):
        return (pieces[i].astype(F32) + one.astype(F32)).astype(BF)

    def third_hop(i, one, two):
        return mix_block(spans[i][0], there, pieces[i], last_share, [two], [last_two(i)], None, None)

    def finish(i, one, two, three):
        if i in (0, 1):
            mixes.append(mixing_back(heads_share, last_share, after(history, two), i, 2))
        if i == 1:
            extra["both"], extra["all"] = small_sums()
        if i == 3:
            three = after(three, extra["both"], grad_heads)
        if i == 4:
            three = after(three, extra["all"])
        extra["history"], token = mix_block(
            spans[i][0],
            here,
            pieces[i],
            last_share,
            [one, two],
            [last_one(i), last_two(i)],
            three,
            extra.get("history"),
        )
        return token

    along_line(len(spans), first_hop, second_hop, third_hop, finish)
    grad_history = extra["history"]

    grad_mixing = extra["both"][:, None, :]
    sums = extra["all"]
    columns = 2 * width // tokens
    stats = sums[:, :columns].reshape(2, width)
    grad_first = sums[:, columns:-lines].reshape(mixer_first.shape)
    grad_second = sums[:, -lines:].reshape(-1)[: second_flat.shape[0]].reshape(hidden_count, outputs)
    return (
        block_out,
        next_here[:, None, :],
        grad_history,
        grad_mixing,
        stats[:1],
        stats[1:],
        grad_heads,
        grad_merge,
        grad_up,
        grad_down,
        grad_first,
        grad_second[:, None, :],
    )


def solution(mesh):
    in_specs = (
        P(None, "dp", None),
        P("dp", "stream", None),
        P("dp"),
        P("stream", None),
        P("stream", None),
        P(None, "dp", "stream"),
        P("stream", "dp"),
        P("dp", "stream"),
        P("stream", "dp"),
        P("stream", None),
        P(None, "stream", None),
        P("dp", "stream"),
        P("dp", "stream", None),
    )
    out_specs = (
        P("dp", "stream"),
        P("dp", "stream", None),
        P("stream", "dp", None),
        P("dp", "stream", None),
        P("stream", None),
        P("stream", None),
        P(None, "dp", "stream"),
        P("stream", "dp"),
        P("dp", "stream"),
        P("stream", "dp"),
        P("stream", None),
        P(None, "stream", None),
    )
    return jax.shard_map(body, mesh=mesh, in_specs=in_specs, out_specs=out_specs, check_vma=False)
```

profile of v0, /device:TPU:0, one launch (start us, length us, event | category | flops | bytes accessed | tf_op | source)
XLA Modules:
  0.0 767.2 jit_solution(12274118684608282408)
XLA Ops:
  9.9 9.5 %all-reduce.2 = s32[8]{0:T(128)S(1)} all-reduce(s32[8]{0:T(128)S(1)} %dynamic-update-slice), channel_id=3, replica_groups=mesh['dp'=8,'stream'=4] {'dp'}, use_global_device_ids=true, to_apply=%add.2 | all-reduce | flops 8 | bytes 64
  27.2 16.5 %all-gather.1 = f32[2048,62]{0,1:T(8,128)S(1)} all-gather(f32[512,62]{0,1:T(8,128)S(1)} %concatenate.27), channel_id=4, replica_groups=mesh['dp'=8,'stream'=4] {'stream'}, dimensions={0}, use_global_device_ids=true | all-gather | bytes 634880 | tf_op jit(solution)/shard_map/all_gather | solution.py:937
  49.5 2.6 collective-permute-done.1.refs_2_
  52.1 4.0 collective-permute-start.3
  57.5 22.6 %make_streams.1 = (bf16[4,512,2048]{2,1,0:T(8,128)(2,1)}, bf16[4,512,2048]{2,1,0:T(8,128)(2,1)}, f32[512,4]{1,0:T(8,128)}, f32[512,2048]{1,0:T(8,128)}) custom-call(bf16[8,512,2048]{2,1,0:T(8,128)(2,1)} %hist.2, f32[512,32]{1,0:T(8,128)} %copy.66.mix, f32[4,2048]{1,0:T(4,128)} %get-tuple-element.201.gain, f32[4,2048]{1,0:T(4,128)} %get-tuple-element.200.bias), custom_call_target="tpu_custom_call" | custom-call | flops 19800000512 | bytes 66000000 | tf_op jit(solution)/shard_map/make_streams/pallas_call | solution.py:265
  81.0 5.5 put_together.4.w
  86.5 8.8 %project.1 = bf16[8,3,256,128]{3,2,1,0:T(8,128)(2,1)} custom-call(bf16[4,512,2048]{2,1,0:T(8,128)(2,1)} %get-tuple-element.80.x, bf16[8,3,256,512]{3,2,1,0:T(8,128)(2,1)} %put_together.4.w, f32[3,512,128]{2,1,0:T(8,128)} %get-tuple-element.180.table), custom_call_target="tpu_custom_call" | custom-call | flops 8099999744 | bytes 27000000 | tf_op jit(solution)/shard_map/project/pallas_call | solution.py:315
  95.3 24.6 %all_to_all.30.mine = bf16[8,3,256,128]{3,2,1,0:T(8,128)(2,1)S(1)} all-to-all(bf16[8,3,256,128]{3,2,1,0:T(8,128)(2,1)} %project.1), channel_id=1, replica_groups=mesh['dp'=8,'stream'=4] {'dp'}, dimensions={0} | all-to-all | bytes 3145728 | tf_op jit(solution)/shard_map/all_to_all | solution.py:966
  122.7 2.4 collective-permute-start.19
  126.2 27.5 %attend.1 = (bf16[8,256,128]{2,1,0:T(8,128)(2,1)}, f32[8,256,128]{2,1,0:T(8,128)}, f32[8,256,1]{2,1,0:T(8,128)}) custom-call(s32[8]{0:T(128)} %subtract_maximum_fusion.first, s32[1]{0:T(128)} %bitcast.1.part, bf16[8,3,256,128]{3,2,1,0:T(8,128)(2,1)} %copy-done.8, bf16[8,2,256,128]{3,2,1,0:T(8,128)(2,1)} %collective-permute-done.9.theirs), custom_call_target="tpu_custom_call" | custom-call | flops 14400000000 | bytes 48000000 | tf_op jit(solution)/shard_map/attend/pallas_call | solution.py:374
  153.7 5.0 collective-permute-done.25.refs_2_
  168.8 5.9 collective-permute-done.26.refs_3_
  174.7 2.7 collective-permute-done.27.refs_4_
  178.2 3.5 all-to-all-start.1
  184.4 7.1 collective-permute-done.11.refs_4_
  191.6 3.2 slice_bitcast_fusion.1.x_ref
  194.7 2.4 put_together.6.wm.refs_1_
  200.0 6.5 put_together.5
  206.5 10.1 %hidden_units.1 = (bf16[512,2048]{1,0:T(8,128)(2,1)}, bf16[512,2048]{1,0:T(8,128)(2,1)}) custom-call(bf16[512,2048]{1,0:T(8,128)(2,1)} %slice_bitcast_fusion.1.x_ref, bf16[2048,2048]{1,0:T(8,128)(2,1)} %bitcast.107), custom_call_target="tpu_custom_call" | custom-call | flops 8099999744 | bytes 27000000 | tf_op jit(solution)/shard_map/hidden_units/pallas_call | solution.py:801
  217.4 6.5 put_together.7.wd.refs_1_
  223.9 12.6 %merge_branches.1 = bf16[4,512,512]{2,1,0:T(8,128)(2,1)} custom-call(bf16[512,512]{1,0:T(8,128)(2,1)} %bitcast.98, bf16[512,2048]{1,0:T(8,128)(2,1)} %get-tuple-element.89.h, bf16[8,512,256]{2,1,0:T(8,128)(2,1)} %put_together.6.wm.refs_1_, bf16[8,2048,256]{2,1,0:T(8,128)(2,1)} %put_together.7.wd.refs_1_, f32[512,2048]{1,0:T(8,128)} %get-tuple-element.99.st, ...), custom_call_target="tpu_custom_call" | custom-call | flops 11699999744 | bytes 39000000 | tf_op jit(solution)/shard_map/merge_branches/pallas_call | solution.py:829
  236.5 53.2 %all_to_all.31 = bf16[4,512,512]{2,1,0:T(8,128)(2,1)S(1)} all-to-all(bf16[4,512,512]{2,1,0:T(8,128)(2,1)} %merge_branches.1), channel_id=1, replica_groups=mesh['dp'=8,'stream'=4] {'stream'}, dimensions={0} | all-to-all | bytes 4194304 | tf_op jit(solution)/shard_map/all_to_all | solution.py:989
  291.3 42.8 %all-gather.8.cloned.1.call-done = bf16[512,2048]{1,0:T(8,128)(2,1)} async-done(((bf16[512,512]{1,0:T(8,128)(2,1)}), bf16[512,2048]{1,0:T(8,128)(2,1)}) %all-gather.8.cloned.1.call-update) | async-done | bytes 2097168 | tf_op jit(solution)/shard_map/all_gather | solution.py:991
  340.4 6.9 convolution_convert_fusion.1
  348.0 3.2 slice_bitcast_fusion.u
  351.2 14.3 %back_through.3 = bf16[512,2048]{1,0:T(8,128)(2,1)} custom-call(bf16[512,2048]{1,0:T(8,128)(2,1)} %copy-done.40, bf16[8,2048,256]{2,1,0:T(8,128)(2,1)} %put_together.7.wd.refs_1_, bf16[512,2048]{1,0:T(8,128)(2,1)} %get-tuple-element.100.refs_2_), custom_call_target="tpu_custom_call" | custom-call | flops 11699999744 | bytes 39000000 | tf_op jit(solution)/shard_map/back_through/pallas_call | solution.py:884
  365.5 7.2 back_through.2
  374.8 4.0 all-to-all-start.3
  379.0 9.8 %fusion.37.g = f32[512,2048]{1,0:T(8,128)} fusion(bf16[512,2048]{1,0:T(8,128)(2,1)S(1)} %copy-done.43, bf16[2048,2048]{1,0:T(8,128)(2,1)} %bitcast.108), kind=kOutput, calls=%fused_computation.99 | convolution fusion | flops 4294967296 | bytes 14680064 | tf_op jit(solution)/shard_map/dot_general | solution.py:72
  388.8 6.4 last_back.1
  398.1 35.8 %attend_back.1 = (bf16[8,3,256,128]{3,2,1,0:T(8,128)(2,1)}, bf16[8,2,256,128]{3,2,1,0:T(8,128)(2,1)}) custom-call(s32[8]{0:T(128)} %subtract_maximum_fusion.first, s32[1]{0:T(128)} %bitcast.1.part, bf16[8,3,256,128]{3,2,1,0:T(8,128)(2,1)} %copy-done.8, bf16[8,2,256,128]{3,2,1,0:T(8,128)(2,1)} %collective-permute-done.9.theirs, ...), custom_call_target="tpu_custom_call" | custom-call | flops 19800000512 | bytes 66000000 | tf_op jit(solution)/shard_map/attend_back/pallas_call | solution.py:448
  433.9 4.6 collective-permute-start.33
  444.9 2.6 convolution_convert_fusion.2
  449.1 8.4 %convolution_convert_fusion = bf16[2048,2048]{1,0:T(8,128)(2,1)} fusion(bf16[512,2048]{1,0:T(8,128)(2,1)S(1)} %copy-done.44, bf16[4,512,2048]{2,1,0:T(8,128)(2,1)} %get-tuple-element.80.x), kind=kOutput, calls=%fused_computation | convolution fusion | flops 4299161600 | bytes 12582912 | tf_op jit(solution)/shard_map/dot_general | solution.py:68
  457.5 4.5 all-to-all-start.4
  462.3 3.7 add_convert_fusion
  466.0 2.7 convert_element_type.152
  468.7 20.0 %all-to-all-done.4.part = bf16[8,3,256,128]{3,2,1,0:T(8,128)(2,1)} async-done(((bf16[8,3,256,128]{3,2,1,0:T(8,128)(2,1)}), bf16[8,3,256,128]{3,2,1,0:T(8,128)(2,1)}, u32[]{:S(2)}, u32[]{:S(2)}) %all-to-all-start.4) | async-done | bytes 1572896 | tf_op jit(solution)/shard_map/all_to_all | solution.py:1038
  488.6 17.1 %heads_back.1 = (bf16[3,128,2048]{2,1,0:T(8,128)(2,1)}, bf16[3,128,2048]{2,1,0:T(8,128)(2,1)}, bf16[3,128,2048]{2,1,0:T(8,128)(2,1)}, bf16[3,64,2048]{2,1,0:T(8,...) custom-call(bf16[8,3,256,128]{3,2,1,0:T(8,128)(2,1)} %all-to-all-don, ...), custom_call_target="tpu_custom_call" | custom-call | flops 2700000000 | bytes 9000000 | tf_op jit(solution)/shard_map/heads_back/pallas_call | solution.py:520
  510.3 32.8 %collective-permute-done.35.refs_2_ = bf16[3,128,2048]{2,1,0:T(8,128)(2,1)S(1)} collective-permute-done((bf16[3,128,2048]{2,1,0:T(8,128)(2,1)}, bf16[3,128,2048]{2,1,0:T(8,128)(2,1)S(1)}, u32[]{:S(2)}, u32[]{:S(2)}) %collective-permute-start.35) | collective-permute-done | bytes 1572896 | tf_op jit(solution)/shard_map/ppermute | solution.py:81
  543.1 3.8 add_convert_fusion.3
  548.8 23.9 %collective-permute-done.40.refs_2_ = bf16[3,128,2048]{2,1,0:T(8,128)(2,1)S(1)} collective-permute-done((bf16[3,128,2048]{2,1,0:T(8,128)(2,1)}, bf16[3,128,2048]{2,1,0:T(8,128)(2,1)S(1)}, u32[]{:S(2)}, u32[]{:S(2)}) %collective-permute-start.40) | collective-permute-done | bytes 1572896 | tf_op jit(solution)/shard_map/ppermute | solution.py:81
  572.6 3.8 add_convert_fusion.2
  578.2 7.0 collective-permute-start.39
  587.4 4.7 mix_inward.5
  596.0 4.3 mix_inward.6
  601.6 30.4 %collective-permute-start.46 = (bf16[3,64,2048]{2,1,0:T(8,128)(2,1)S(1)}, bf16[3,64,2048]{2,1,0:T(8,128)(2,1)}, u32[]{:S(2)}, u32[]{:S(2)}) collective-permute-start(bf16[3,64,2048]{2,1,0:T(8,128)(2,1)S(1)} %copy-done.4), channel_id=1, source_target_pairs={{0,1},{3,2},{4,5},{7,6},{8,9},{11,10},{12,13},{15,14},{16,17},{19,... | collective-permute-start | bytes 2359304 | tf_op jit(solution)/shard_map/ppermute | solution.py:81
  632.0 3.7 add_convert_fusion.1
  636.6 5.9 mix_final.5
  642.5 4.2 collective-permute-start.42
  652.4 9.7 %mixing_back.2 = f32[4,256,8]{2,1,0:T(8,128)} custom-call(bf16[3,512,2048]{2,1,0:T(8,128)(2,1)} %get-tuple-element.123.first, bf16[512,2048]{1,0:T(8,128)(2,1)} %get-tuple-element.103.refs_3_.refs_4_.last, bf16[8,512,2048]{2,1,0:T(8,128)(2,1)} %hist.2), custom_call_target="tpu_custom_call" | custom-call | flops 360000000 | bytes 1200000 | tf_op jit(solution)/shard_map/mixing_back/pallas_call | solution.py:614
  663.3 9.7 %mixing_back.3 = f32[4,256,8]{2,1,0:T(8,128)} custom-call(bf16[3,512,2048]{2,1,0:T(8,128)(2,1)} %get-tuple-element.123.first, bf16[512,2048]{1,0:T(8,128)(2,1)} %get-tuple-element.103.refs_3_.refs_4_.last, bf16[8,512,2048]{2,1,0:T(8,128)(2,1)} %hist.2), custom_call_target="tpu_custom_call" | custom-call | flops 360000000 | bytes 1200000 | tf_op jit(solution)/shard_map/mixing_back/pallas_call | solution.py:614
  677.3 5.8 mix_final.6
  686.8 4.1 all-to-all-start.5
  692.3 4.1 mix_inward.9
  698.8 2.8 convert_element_type.172
  701.6 9.8 %all-to-all-done.5 = f32[4,512,16]{1,2,0:T(8,128)S(1)} async-done(((f32[4,512,16]{1,2,0:T(8,128)}), f32[4,512,16]{1,2,0:T(8,128)S(1)}, u32[]{:S(2)}, u32[]{:S(2)}) %all-to-all-start.5) | async-done | bytes 131104 | tf_op jit(solution)/shard_map/all_to_all | solution.py:1078
  712.3 2.8 mix_inward.8
  717.4 2.8 mix_inward.7
  721.5 16.1 %all-gather.2 = f32[4096,45]{0,1:T(8,128)S(1)} all-gather(f32[512,45]{0,1:T(8,128)S(1)} %pad_maximum_fusion.3), channel_id=5, replica_groups=mesh['dp'=8,'stream'=4] {'dp'}, dimensions={0}, use_global_device_ids=true | all-gather | bytes 829440 | tf_op jit(solution)/shard_map/all_gather | solution.py:1081
  743.2 5.8 mix_final.7
  749.1 2.7 convert_element_type.168
  752.5 3.6 mix_final.8
  756.2 3.6 mix_final.9
  (288 shorter events, 106.6 us)
Async XLA Ops:
  7.2 209.4 %all-gather.6.cloned.1.call-start = ((), (), s32[]{:S(2)}) async-start(), calls=%async_computation.10 | async-start | bytes 2621440 | tf_op jit(solution)/shard_map/all_gather | solution.py:958
  19.4 30.1 %collective-permute-start = (bf16[3,256,512]{2,1,0:T(8,128)(2,1)}, bf16[3,256,512]{2,1,0:T(8,128)(2,1)S(1)}, u32[]{:S(2)}, u32[]{:S(2)}) collective-permute-start(bf16[3,256,512]{2,1,0:T(8,128)(2,1)} %refs_0_), channel_id=1, source_target_pairs={{0,8},{4,12},{8,0},{12,4},{16,24},{20,28},{24,16},{28,20},{1,9},{5... | collective-permute-start | bytes 2359304 | tf_op jit(solution)/shard_map/ppermute | solution.py:77
  20.2 31.9 %collective-permute-start.1 = (bf16[3,256,512]{2,1,0:T(8,128)(2,1)}, bf16[3,256,512]{2,1,0:T(8,128)(2,1)}, u32[]{:S(2)}, u32[]{:S(2)}) collective-permute-start(bf16[3,256,512]{2,1,0:T(8,128)(2,1)} %refs_0_), channel_id=1, source_target_pairs={{0,16},{4,20},{8,24},{12,28},{16,0},{20,4},{24,8},{28,12},{1,17},{... | collective-permute-start | bytes 2359304 | tf_op jit(solution)/shard_map/ppermute | solution.py:77
  20.7 36.2 %collective-permute-start.2 = (bf16[3,256,512]{2,1,0:T(8,128)(2,1)}, bf16[3,256,512]{2,1,0:T(8,128)(2,1)}, u32[]{:S(2)}, u32[]{:S(2)}) collective-permute-start(bf16[3,256,512]{2,1,0:T(8,128)(2,1)} %refs_0_), channel_id=1, source_target_pairs={{0,24},{4,28},{8,16},{12,20},{16,8},{20,12},{24,0},{28,4},{1,25},{... | collective-permute-start | bytes 2359304 | tf_op jit(solution)/shard_map/ppermute | solution.py:77
  22.9 34.6 %collective-permute-start.5 = (bf16[3,256,512]{2,1,0:T(8,128)(2,1)}, bf16[3,256,512]{2,1,0:T(8,128)(2,1)}, u32[]{:S(2)}, u32[]{:S(2)}) collective-permute-start(bf16[3,256,512]{2,1,0:T(8,128)(2,1)} %refs_0_), channel_id=1, source_target_pairs={{0,4},{4,0},{8,12},{12,8},{16,20},{20,16},{24,28},{28,24},{1,5},{5... | collective-permute-start | bytes 2359304 | tf_op jit(solution)/shard_map/ppermute | solution.py:77
  44.0 247.2 %copy-start.12 = (f32[4,512,62]{1,0,2:T(4,128)}, f32[4,512,62]{1,0,2:T(4,128)S(1)}, u32[]{:S(2)}) copy-start(f32[4,512,62]{1,0,2:T(4,128)S(1)} %reshape.497) | copy-start | bytes 1523716
  48.8 31.2 %copy-start.21 = (f32[4,1,2048]{2,1,0:T(1,128)}, f32[4,1,2048]{2,1,0:T(1,128)S(1)}, u32[]{:S(2)}) copy-start(f32[4,1,2048]{2,1,0:T(1,128)S(1)} %get-tuple-element.186.gain) | copy-start | bytes 98308
  52.1 34.4 %collective-permute-start.3 = (bf16[256,2048]{1,0:T(8,128)(2,1)}, bf16[256,2048]{1,0:T(8,128)(2,1)}, u32[]{:S(2)}, u32[]{:S(2)}) collective-permute-start(bf16[256,2048]{1,0:T(8,128)(2,1)} %refs_0_.1), channel_id=1, source_target_pairs={{0,8},{4,12},{8,0},{12,4},{16,24},{20,28},{24,16},{28,20},{1,9},{5... | collective-permute-start | bytes 3145736 | tf_op jit(solution)/shard_map/ppermute | solution.py:77
  56.1 30.4 %collective-permute-start.4 = (bf16[256,2048]{1,0:T(8,128)(2,1)}, bf16[256,2048]{1,0:T(8,128)(2,1)}, u32[]{:S(2)}, u32[]{:S(2)}) collective-permute-start(bf16[256,2048]{1,0:T(8,128)(2,1)} %refs_0_.1), channel_id=1, source_target_pairs={{0,16},{4,20},{8,24},{12,28},{16,0},{20,4},{24,8},{28,12},{1,17},{... | collective-permute-start | bytes 3145736 | tf_op jit(solution)/shard_map/ppermute | solution.py:77
  56.9 23.1 %collective-permute-start.6 = (bf16[3,256,512]{2,1,0:T(8,128)(2,1)S(1)}, bf16[3,256,512]{2,1,0:T(8,128)(2,1)S(1)}, u32[]{:S(2)}, u32[]{:S(2)}) collective-permute-start(bf16[3,256,512]{2,1,0:T(8,128)(2,1)S(1)} %collective-permute-done.refs_1_), channel_id=1, source_target_pairs={{0,4},{4,0},{8,12},{12,8},{16,20},{20,16},{24,28},{28,24},{1,5},{5... | collective-permute-start | bytes 2359304 | tf_op jit(solution)/shard_map/ppermute | solution.py:77
  56.9 23.1 %collective-permute-start.7 = (bf16[3,256,512]{2,1,0:T(8,128)(2,1)}, bf16[3,256,512]{2,1,0:T(8,128)(2,1)}, u32[]{:S(2)}, u32[]{:S(2)}) collective-permute-start(bf16[3,256,512]{2,1,0:T(8,128)(2,1)} %collective-permute-done.1.refs_2_), channel_id=1, source_target_pairs={{0,4},{4,0},{8,12},{12,8},{16,20},{20,16},{24,28},{28,24},{1,5},{5... | collective-permute-start | bytes 2359304 | tf_op jit(solution)/shard_map/ppermute | solution.py:77
  57.5 22.6 %collective-permute-start.8 = (bf16[3,256,512]{2,1,0:T(8,128)(2,1)}, bf16[3,256,512]{2,1,0:T(8,128)(2,1)}, u32[]{:S(2)}, u32[]{:S(2)}) collective-permute-start(bf16[3,256,512]{2,1,0:T(8,128)(2,1)} %collective-permute-done.2.refs_3_), channel_id=1, source_target_pairs={{0,4},{4,0},{8,12},{12,8},{16,20},{20,16},{24,28},{28,24},{1,5},{5... | collective-permute-start | bytes 2359304 | tf_op jit(solution)/shard_map/ppermute | solution.py:77
  121.0 4.7 collective-permute-start.9
  121.5 39.8 %collective-permute-start.17 = (bf16[512,256]{1,0:T(8,128)(2,1)S(1)}, bf16[512,256]{1,0:T(8,128)(2,1)S(1)}, u32[]{:S(2)}, u32[]{:S(2)}) collective-permute-start(bf16[512,256]{1,0:T(8,128)(2,1)S(1)} %copy-done.34), channel_id=1, source_target_pairs={{0,8},{4,12},{8,0},{12,4},{16,24},{20,28},{24,16},{28,20},{1,9},{5... | collective-permute-start | bytes 786440 | tf_op jit(solution)/shard_map/ppermute | solution.py:77
  122.1 41.1 %collective-permute-start.18 = (bf16[512,256]{1,0:T(8,128)(2,1)S(1)}, bf16[512,256]{1,0:T(8,128)(2,1)}, u32[]{:S(2)}, u32[]{:S(2)}) collective-permute-start(bf16[512,256]{1,0:T(8,128)(2,1)S(1)} %copy-done.34), channel_id=1, source_target_pairs={{0,16},{4,20},{8,24},{12,28},{16,0},{20,4},{24,8},{28,12},{1,17},{... | collective-permute-start | bytes 786440 | tf_op jit(solution)/shard_map/ppermute | solution.py:77
  122.7 40.6 %collective-permute-start.19 = (bf16[512,256]{1,0:T(8,128)(2,1)S(1)}, bf16[512,256]{1,0:T(8,128)(2,1)}, u32[]{:S(2)}, u32[]{:S(2)}) collective-permute-start(bf16[512,256]{1,0:T(8,128)(2,1)S(1)} %copy-done.34), channel_id=1, source_target_pairs={{0,24},{4,28},{8,16},{12,20},{16,8},{20,12},{24,0},{28,4},{1,25},{... | collective-permute-start | bytes 786440 | tf_op jit(solution)/shard_map/ppermute | solution.py:77
  125.1 33.7 %collective-permute-start.25 = (bf16[2048,256]{1,0:T(8,128)(2,1)}, bf16[2048,256]{1,0:T(8,128)(2,1)}, u32[]{:S(2)}, u32[]{:S(2)}) collective-permute-start(bf16[2048,256]{1,0:T(8,128)(2,1)} %refs_0_.3), channel_id=1, source_target_pairs={{0,16},{4,20},{8,24},{12,28},{16,0},{20,4},{24,8},{28,12},{1,17},{... | collective-permute-start | bytes 3145736 | tf_op jit(solution)/shard_map/ppermute | solution.py:77
  125.7 35.7 %collective-permute-start.24 = (bf16[2048,256]{1,0:T(8,128)(2,1)}, bf16[2048,256]{1,0:T(8,128)(2,1)}, u32[]{:S(2)}, u32[]{:S(2)}) collective-permute-start(bf16[2048,256]{1,0:T(8,128)(2,1)} %refs_0_.3), channel_id=1, source_target_pairs={{0,8},{4,12},{8,0},{12,4},{16,24},{20,28},{24,16},{28,20},{1,9},{5... | collective-permute-start | bytes 3145736 | tf_op jit(solution)/shard_map/ppermute | solution.py:77
  159.8 14.9 %collective-permute-start.26 = (bf16[1024,256]{1,0:T(8,128)(2,1)S(1)}, bf16[1024,256]{1,0:T(8,128)(2,1)S(1)}, u32[]{:S(2)}, u32[]{:S(2)}) collective-permute-start(bf16[1024,256]{1,0:T(8,128)(2,1)S(1)} %slice.102), channel_id=1, source_target_pairs={{0,8},{4,12},{8,0},{12,4},{16,24},{20,28},{24,16},{28,20},{1,9},{5... | collective-permute-start | bytes 1572872 | tf_op jit(solution)/shard_map/ppermute | solution.py:77
  161.3 2.3 collective-permute-start.21
  162.5 14.9 %collective-permute-start.27 = (bf16[1024,256]{1,0:T(8,128)(2,1)S(1)}, bf16[1024,256]{1,0:T(8,128)(2,1)S(1)}, u32[]{:S(2)}, u32[]{:S(2)}) collective-permute-start(bf16[1024,256]{1,0:T(8,128)(2,1)S(1)} %slice.103), channel_id=1, source_target_pairs={{0,16},{4,20},{8,24},{12,28},{16,0},{20,4},{24,8},{28,12},{1,17},{... | collective-permute-start | bytes 1572872 | tf_op jit(solution)/shard_map/ppermute | solution.py:77
  163.2 3.5 collective-permute-start.22
  163.3 4.0 collective-permute-start.23
  164.4 4.4 collective-permute-start.20
  166.7 17.7 %collective-permute-start.10 = (bf16[128,2048]{1,0:T(8,128)(2,1)S(1)}, bf16[128,2048]{1,0:T(8,128)(2,1)}, u32[]{:S(2)}, u32[]{:S(2)}) collective-permute-start(bf16[128,2048]{1,0:T(8,128)(2,1)S(1)} %slice.100), channel_id=1, source_target_pairs={{0,8},{4,12},{8,0},{12,4},{16,24},{20,28},{24,16},{28,20},{1,9},{5... | collective-permute-start | bytes 1572872 | tf_op jit(solution)/shard_map/ppermute | solution.py:77
  167.3 24.2 %collective-permute-start.11 = (bf16[128,2048]{1,0:T(8,128)(2,1)S(1)}, bf16[128,2048]{1,0:T(8,128)(2,1)}, u32[]{:S(2)}, u32[]{:S(2)}) collective-permute-start(bf16[128,2048]{1,0:T(8,128)(2,1)S(1)} %slice.101), channel_id=1, source_target_pairs={{0,16},{4,20},{8,24},{12,28},{16,0},{20,4},{24,8},{28,12},{1,17},{... | collective-permute-start | bytes 1572872 | tf_op jit(solution)/shard_map/ppermute | solution.py:77
  168.8 30.2 %collective-permute-start.13 = (bf16[256,2048]{1,0:T(8,128)(2,1)}, bf16[256,2048]{1,0:T(8,128)(2,1)}, u32[]{:S(2)}, u32[]{:S(2)}) collective-permute-start(bf16[256,2048]{1,0:T(8,128)(2,1)} %collective-permute-done.3.refs_1_), channel_id=1, source_target_pairs={{0,4},{4,0},{8,12},{12,8},{16,20},{20,16},{24,28},{28,24},{1,5},{5... | collective-permute-start | bytes 3145736 | tf_op jit(solution)/shard_map/ppermute | solution.py:77
  174.7 24.8 %collective-permute-start.14 = (bf16[256,2048]{1,0:T(8,128)(2,1)}, bf16[256,2048]{1,0:T(8,128)(2,1)}, u32[]{:S(2)}, u32[]{:S(2)}) collective-permute-start(bf16[256,2048]{1,0:T(8,128)(2,1)} %collective-permute-done.4.refs_2_), channel_id=1, source_target_pairs={{0,4},{4,0},{8,12},{12,8},{16,20},{20,16},{24,28},{28,24},{1,5},{5... | collective-permute-start | bytes 3145736 | tf_op jit(solution)/shard_map/ppermute | solution.py:77
  178.2 21.4 %collective-permute-start.12 = (bf16[256,2048]{1,0:T(8,128)(2,1)}, bf16[256,2048]{1,0:T(8,128)(2,1)}, u32[]{:S(2)}, u32[]{:S(2)}) collective-permute-start(bf16[256,2048]{1,0:T(8,128)(2,1)} %refs_0_.1), channel_id=1, source_target_pairs={{0,4},{4,0},{8,12},{12,8},{16,20},{20,16},{24,28},{28,24},{1,5},{5... | collective-permute-start | bytes 3145736 | tf_op jit(solution)/shard_map/ppermute | solution.py:77
  178.2 19.0 %all-to-all-start.1 = ((bf16[8,256,128]{2,1,0:T(8,128)(2,1)}), bf16[8,256,128]{2,1,0:T(8,128)(2,1)S(1)}, u32[]{:S(2)}, u32[]{:S(2)}) async-start(bf16[8,256,128]{2,1,0:T(8,128)(2,1)} %get-tuple-element.81), calls=%async_computation.1 | async-start | bytes 1048576 | tf_op jit(solution)/shard_map/all_to_all | solution.py:972
  181.7 152.4 %all-gather.8.cloned.1.call-start = ((), (), s32[]{:S(2)}) async-start(), calls=%async_computation.11 | async-start | bytes 2621440 | tf_op jit(solution)/shard_map/all_gather | solution.py:991
  184.4 14.1 %collective-permute-start.15 = (bf16[128,2048]{1,0:T(8,128)(2,1)}, bf16[128,2048]{1,0:T(8,128)(2,1)}, u32[]{:S(2)}, u32[]{:S(2)}) collective-permute-start(bf16[128,2048]{1,0:T(8,128)(2,1)} %collective-permute-done.10.refs_3_), channel_id=1, source_target_pairs={{0,4},{4,0},{8,12},{12,8},{16,20},{20,16},{24,28},{28,24},{1,5},{5... | collective-permute-start | bytes 1572872 | tf_op jit(solution)/shard_map/ppermute | solution.py:77
  191.5 7.4 collective-permute-start.16
  198.5 18.1 %collective-permute-start.30 = (bf16[2048,256]{1,0:T(8,128)(2,1)}, bf16[2048,256]{1,0:T(8,128)(2,1)}, u32[]{:S(2)}, u32[]{:S(2)}) collective-permute-start(bf16[2048,256]{1,0:T(8,128)(2,1)} %collective-permute-done.25.refs_2_), channel_id=1, source_target_pairs={{0,4},{4,0},{8,12},{12,8},{16,20},{20,16},{24,28},{28,24},{1,5},{5... | collective-permute-start | bytes 3145736 | tf_op jit(solution)/shard_map/ppermute | solution.py:77
  199.0 17.7 %collective-permute-start.29 = (bf16[2048,256]{1,0:T(8,128)(2,1)}, bf16[2048,256]{1,0:T(8,128)(2,1)}, u32[]{:S(2)}, u32[]{:S(2)}) collective-permute-start(bf16[2048,256]{1,0:T(8,128)(2,1)} %collective-permute-done.24.refs_1_), channel_id=1, source_target_pairs={{0,4},{4,0},{8,12},{12,8},{16,20},{20,16},{24,28},{28,24},{1,5},{5... | collective-permute-start | bytes 3145736 | tf_op jit(solution)/shard_map/ppermute | solution.py:77
  199.0 17.6 %collective-permute-start.28 = (bf16[2048,256]{1,0:T(8,128)(2,1)S(1)}, bf16[2048,256]{1,0:T(8,128)(2,1)}, u32[]{:S(2)}, u32[]{:S(2)}) collective-permute-start(bf16[2048,256]{1,0:T(8,128)(2,1)S(1)} %copy-done.27), channel_id=1, source_target_pairs={{0,4},{4,0},{8,12},{12,8},{16,20},{20,16},{24,28},{28,24},{1,5},{5... | collective-permute-start | bytes 3145736 | tf_op jit(solution)/shard_map/ppermute | solution.py:77
  199.5 17.1 %collective-permute-start.31 = (bf16[1024,256]{1,0:T(8,128)(2,1)S(1)}, bf16[1024,256]{1,0:T(8,128)(2,1)S(1)}, u32[]{:S(2)}, u32[]{:S(2)}) collective-permute-start(bf16[1024,256]{1,0:T(8,128)(2,1)S(1)} %collective-permute-done.26.refs_3_), channel_id=1, source_target_pairs={{0,4},{4,0},{8,12},{12,8},{16,20},{20,16},{24,28},{28,24},{1,5},{5... | collective-permute-start | bytes 1572872 | tf_op jit(solution)/shard_map/ppermute | solution.py:77
  199.6 17.0 %collective-permute-start.32 = (bf16[1024,256]{1,0:T(8,128)(2,1)S(1)}, bf16[1024,256]{1,0:T(8,128)(2,1)}, u32[]{:S(2)}, u32[]{:S(2)}) collective-permute-start(bf16[1024,256]{1,0:T(8,128)(2,1)S(1)} %copy-done.32), channel_id=1, source_target_pairs={{0,4},{4,0},{8,12},{12,8},{16,20},{20,16},{24,28},{28,24},{1,5},{5... | collective-permute-start | bytes 1572872 | tf_op jit(solution)/shard_map/ppermute | solution.py:77
  291.0 175.0 %reduce-scatter.5.cloned.1.call-start = ((), (), s32[]{:S(2)}) async-start(), calls=%async_computation.12 | async-start | bytes 9437184 | tf_op jit(solution)/shard_map/reduce_scatter | solution.py:1017
  374.8 22.5 %all-to-all-start.3 = ((bf16[8,256,128]{2,1,0:T(8,128)(2,1)}), bf16[8,256,128]{2,1,0:T(8,128)(2,1)S(1)}, u32[]{:S(2)}, u32[]{:S(2)}) async-start(bf16[8,256,128]{2,1,0:T(8,128)(2,1)} %bitcast.20), calls=%async_computation.3 | async-start | bytes 1048576 | tf_op jit(solution)/shard_map/all_to_all | solution.py:1028
  378.8 215.4 %reduce-scatter.7.cloned.1.call-start = ((), (), s32[]{:S(2)}) async-start(), calls=%async_computation.13 | async-start | bytes 2359296 | tf_op jit(solution)/shard_map/reduce_scatter | solution.py:1052
  395.3 48.6 %collective-permute-start.34 = (bf16[512,2048]{1,0:T(8,128)(2,1)}, bf16[512,2048]{1,0:T(8,128)(2,1)S(1)}, u32[]{:S(2)}, u32[]{:S(2)}) collective-permute-start(bf16[512,2048]{1,0:T(8,128)(2,1)} %get-tuple-element.103.refs_3_.refs_4_.last), channel_id=1, source_target_pairs={{0,1},{3,2},{4,5},{7,6},{8,9},{11,10},{12,13},{15,14},{16,17},{19,... | collective-permute-start | bytes 6291464 | tf_op jit(solution)/shard_map/ppermute | solution.py:81
  433.9 7.1 collective-permute-start.33
  447.6 251.2 %reduce-scatter.11.cloned.1.call-start = ((), (), s32[]{:S(2)}) async-start(), calls=%async_computation.15 | async-start | bytes 9437184 | tf_op jit(solution)/shard_map/reduce_scatter | solution.py:1054
  457.5 31.1 %all-to-all-start.4 = ((bf16[8,3,256,128]{3,2,1,0:T(8,128)(2,1)}), bf16[8,3,256,128]{3,2,1,0:T(8,128)(2,1)}, u32[]{:S(2)}, u32[]{:S(2)}) async-start(bf16[8,3,256,128]{3,2,1,0:T(8,128)(2,1)} %pad_maximum_fusion), calls=%async_computation.4 | async-start | bytes 3145728 | tf_op jit(solution)/shard_map/all_to_all | solution.py:1038
  462.0 287.1 %reduce-scatter.9.cloned.1.call-start = ((), (), s32[]{:S(2)}) async-start(), calls=%async_computation.14 | async-start | bytes 7077888 | tf_op jit(solution)/shard_map/reduce_scatter | solution.py:1053
  505.8 37.3 %collective-permute-start.35 = (bf16[3,128,2048]{2,1,0:T(8,128)(2,1)}, bf16[3,128,2048]{2,1,0:T(8,128)(2,1)S(1)}, u32[]{:S(2)}, u32[]{:S(2)}) collective-permute-start(bf16[3,128,2048]{2,1,0:T(8,128)(2,1)} %get-tuple-element.114.refs_1_), channel_id=1, source_target_pairs={{0,1},{3,2},{4,5},{7,6},{8,9},{11,10},{12,13},{15,14},{16,17},{19,... | collective-permute-start | bytes 4718600 | tf_op jit(solution)/shard_map/ppermute | solution.py:81
  508.1 64.6 %collective-permute-start.40 = (bf16[3,128,2048]{2,1,0:T(8,128)(2,1)}, bf16[3,128,2048]{2,1,0:T(8,128)(2,1)S(1)}, u32[]{:S(2)}, u32[]{:S(2)}) collective-permute-start(bf16[3,128,2048]{2,1,0:T(8,128)(2,1)} %get-tuple-element.118.refs_1_), channel_id=1, source_target_pairs={{0,1},{3,2},{4,5},{7,6},{8,9},{11,10},{12,13},{15,14},{16,17},{19,... | collective-permute-start | bytes 4718600 | tf_op jit(solution)/shard_map/ppermute | solution.py:81
  509.5 76.6 %collective-permute-start.37 = (bf16[512,2048]{1,0:T(8,128)(2,1)}, bf16[512,2048]{1,0:T(8,128)(2,1)S(1)}, u32[]{:S(2)}, u32[]{:S(2)}) collective-permute-start(bf16[512,2048]{1,0:T(8,128)(2,1)} %add_convert_fusion), channel_id=1, source_target_pairs={{1,2},{2,1},{5,6},{6,5},{9,10},{10,9},{13,14},{14,13},{17,18},{18,... | collective-permute-start | bytes 6291464 | tf_op jit(solution)/shard_map/ppermute | solution.py:81
  546.8 38.4 %copy-start.22 = (f32[4,512,8]{1,0,2:T(4,128)S(1)}, f32[4,512,8]{1,0,2:T(4,128)}, u32[]{:S(2)}) copy-start(f32[4,512,8]{1,0,2:T(4,128)} %get-tuple-element.176) | copy-start | bytes 196612
  546.8 39.2 %collective-permute-start.36 = (bf16[3,128,2048]{2,1,0:T(8,128)(2,1)}, bf16[3,128,2048]{2,1,0:T(8,128)(2,1)}, u32[]{:S(2)}, u32[]{:S(2)}) collective-permute-start(bf16[3,128,2048]{2,1,0:T(8,128)(2,1)} %add_convert_fusion.3), channel_id=1, source_target_pairs={{1,2},{2,1},{5,6},{6,5},{9,10},{10,9},{13,14},{14,13},{17,18},{18,... | collective-permute-start | bytes 4718600 | tf_op jit(solution)/shard_map/ppermute | solution.py:81
  576.4 19.6 %collective-permute-start.41 = (bf16[3,128,2048]{2,1,0:T(8,128)(2,1)}, bf16[3,128,2048]{2,1,0:T(8,128)(2,1)}, u32[]{:S(2)}, u32[]{:S(2)}) collective-permute-start(bf16[3,128,2048]{2,1,0:T(8,128)(2,1)} %add_convert_fusion.2), channel_id=1, source_target_pairs={{1,2},{2,1},{5,6},{6,5},{9,10},{10,9},{13,14},{14,13},{17,18},{18,... | collective-permute-start | bytes 4718600 | tf_op jit(solution)/shard_map/ppermute | solution.py:81
  578.2 53.7 %collective-permute-start.39 = (bf16[3,128,2048]{2,1,0:T(8,128)(2,1)}, bf16[3,128,2048]{2,1,0:T(8,128)(2,1)}, u32[]{:S(2)}, u32[]{:S(2)}) collective-permute-start(bf16[3,128,2048]{2,1,0:T(8,128)(2,1)} %get-tuple-element.117.refs_1_), channel_id=1, source_target_pairs={{0,1},{3,2},{4,5},{7,6},{8,9},{11,10},{12,13},{15,14},{16,17},{19,... | collective-permute-start | bytes 4718600 | tf_op jit(solution)/shard_map/ppermute | solution.py:81
  592.1 44.5 %collective-permute-start.38 = (bf16[2,128,2048]{2,1,0:T(8,128)(2,1)}, bf16[2,128,2048]{2,1,0:T(8,128)(2,1)}, u32[]{:S(2)}, u32[]{:S(2)}) collective-permute-start(bf16[2,128,2048]{2,1,0:T(8,128)(2,1)} %mix_inward.5), channel_id=1, source_target_pairs={{1,0},{2,3},{5,4},{6,7},{9,8},{10,11},{13,12},{14,15},{17,16},{18,... | collective-permute-start | bytes 3145736 | tf_op jit(solution)/shard_map/ppermute | solution.py:81
  600.3 77.0 %collective-permute-start.43 = (bf16[2,128,2048]{2,1,0:T(8,128)(2,1)}, bf16[2,128,2048]{2,1,0:T(8,128)(2,1)}, u32[]{:S(2)}, u32[]{:S(2)}) collective-permute-start(bf16[2,128,2048]{2,1,0:T(8,128)(2,1)} %mix_inward.6), channel_id=1, source_target_pairs={{1,0},{2,3},{5,4},{6,7},{9,8},{10,11},{13,12},{14,15},{17,16},{18,... | collective-permute-start | bytes 3145736 | tf_op jit(solution)/shard_map/ppermute | solution.py:81
  601.6 72.6 %collective-permute-start.46 = (bf16[3,64,2048]{2,1,0:T(8,128)(2,1)S(1)}, bf16[3,64,2048]{2,1,0:T(8,128)(2,1)}, u32[]{:S(2)}, u32[]{:S(2)}) collective-permute-start(bf16[3,64,2048]{2,1,0:T(8,128)(2,1)S(1)} %copy-done.4), channel_id=1, source_target_pairs={{0,1},{3,2},{4,5},{7,6},{8,9},{11,10},{12,13},{15,14},{16,17},{19,... | collective-permute-start | bytes 2359304 | tf_op jit(solution)/shard_map/ppermute | solution.py:81
  635.7 55.4 %collective-permute-start.49 = (bf16[3,128,2048]{2,1,0:T(8,128)(2,1)}, bf16[3,128,2048]{2,1,0:T(8,128)(2,1)S(1)}, u32[]{:S(2)}, u32[]{:S(2)}) collective-permute-start(bf16[3,128,2048]{2,1,0:T(8,128)(2,1)} %add_convert_fusion.1), channel_id=1, source_target_pairs={{1,2},{2,1},{5,6},{6,5},{9,10},{10,9},{13,14},{14,13},{17,18},{18,... | collective-permute-start | bytes 4718600 | tf_op jit(solution)/shard_map/ppermute | solution.py:81
  642.5 40.5 %collective-permute-start.42 = (bf16[3,64,2048]{2,1,0:T(8,128)(2,1)S(1)}, bf16[3,64,2048]{2,1,0:T(8,128)(2,1)}, u32[]{:S(2)}, u32[]{:S(2)}) collective-permute-start(bf16[3,64,2048]{2,1,0:T(8,128)(2,1)S(1)} %copy-done.3), channel_id=1, source_target_pairs={{0,1},{3,2},{4,5},{7,6},{8,9},{11,10},{12,13},{15,14},{16,17},{19,... | collective-permute-start | bytes 2359304 | tf_op jit(solution)/shard_map/ppermute | solution.py:81
  676.5 34.9 %collective-permute-start.47 = (bf16[3,64,2048]{2,1,0:T(8,128)(2,1)}, bf16[3,64,2048]{2,1,0:T(8,128)(2,1)S(1)}, u32[]{:S(2)}, u32[]{:S(2)}) collective-permute-start(bf16[3,64,2048]{2,1,0:T(8,128)(2,1)} %add_convert_fusion.5), channel_id=1, source_target_pairs={{1,2},{2,1},{5,6},{6,5},{9,10},{10,9},{13,14},{14,13},{17,18},{18,... | collective-permute-start | bytes 2359304 | tf_op jit(solution)/shard_map/ppermute | solution.py:81
  685.5 31.0 %collective-permute-start.44 = (bf16[3,64,2048]{2,1,0:T(8,128)(2,1)}, bf16[3,64,2048]{2,1,0:T(8,128)(2,1)S(1)}, u32[]{:S(2)}, u32[]{:S(2)}) collective-permute-start(bf16[3,64,2048]{2,1,0:T(8,128)(2,1)} %add_convert_fusion.6), channel_id=1, source_target_pairs={{1,2},{2,1},{5,6},{6,5},{9,10},{10,9},{13,14},{14,13},{17,18},{18,... | collective-permute-start | bytes 2359304 | tf_op jit(solution)/shard_map/ppermute | solution.py:81
  686.8 24.5 %all-to-all-start.5 = ((f32[4,512,16]{1,2,0:T(8,128)}), f32[4,512,16]{1,2,0:T(8,128)S(1)}, u32[]{:S(2)}, u32[]{:S(2)}) async-start(f32[4,512,16]{1,2,0:T(8,128)} %maximum_maximum_fusion), calls=%async_computation.6 | async-start | bytes 262144 | tf_op jit(solution)/shard_map/all_to_all | solution.py:1078
  696.5 45.7 %collective-permute-start.50 = (bf16[2,128,2048]{2,1,0:T(8,128)(2,1)}, bf16[2,128,2048]{2,1,0:T(8,128)(2,1)S(1)}, u32[]{:S(2)}, u32[]{:S(2)}) collective-permute-start(bf16[2,128,2048]{2,1,0:T(8,128)(2,1)} %mix_inward.9), channel_id=1, source_target_pairs={{1,0},{2,3},{5,4},{6,7},{9,8},{10,11},{13,12},{14,15},{17,16},{18,... | collective-permute-start | bytes 3145736 | tf_op jit(solution)/shard_map/ppermute | solution.py:81
  715.1 36.6 %collective-permute-start.48 = (bf16[2,64,2048]{2,1,0:T(8,128)(2,1)}, bf16[2,64,2048]{2,1,0:T(8,128)(2,1)S(1)}, u32[]{:S(2)}, u32[]{:S(2)}) collective-permute-start(bf16[2,64,2048]{2,1,0:T(8,128)(2,1)} %mix_inward.8), channel_id=1, source_target_pairs={{1,0},{2,3},{5,4},{6,7},{9,8},{10,11},{13,12},{14,15},{17,16},{18,... | collective-permute-start | bytes 1572872 | tf_op jit(solution)/shard_map/ppermute | solution.py:81
  720.2 28.8 %collective-permute-start.45 = (bf16[2,64,2048]{2,1,0:T(8,128)(2,1)}, bf16[2,64,2048]{2,1,0:T(8,128)(2,1)S(1)}, u32[]{:S(2)}, u32[]{:S(2)}) collective-permute-start(bf16[2,64,2048]{2,1,0:T(8,128)(2,1)} %mix_inward.7), channel_id=1, source_target_pairs={{1,0},{2,3},{5,4},{6,7},{9,8},{10,11},{13,12},{14,15},{17,16},{18,... | collective-permute-start | bytes 1572872 | tf_op jit(solution)/shard_map/ppermute | solution.py:81
  (43 other events, 239.6 us)
Sparse Core Ops, SparseCore 0:
  125.2 45.0 all-gather.5
  291.1 42.9 all-gather.7
  347.5 75.7 reduce-scatter.4
  447.7 51.2 reduce-scatter.6
  502.3 71.4 reduce-scatter.10
  577.0 61.6 reduce-scatter.8
where the time goes:
time: 778 us; the launch traced here: 767 us
  Pallas kernels  246 us (32%)
  waiting for transfers between devices  157 us (20%)
  blocking collectives  120 us (15%)
  starting transfers between devices  102 us (13%)
  local copies, waits for them, and re-layouts  53.6 us (7%)
  other arithmetic  40.3 us (5%)
  matrix products  32.3 us (4%)
  between operations  16.2 us (2%)
    ppermute x17, starting transfers between devices, line_hop(): return lax.ppermute(shard, 'stream', pairs)  60.7 us
    ppermute x17, waiting for transfers between devices, line_hop(): return lax.ppermute(shard, 'stream', pairs)  56.7 us
    all_to_all x1, blocking collectives, body(): columns = lax.all_to_all(share, 'stream', 0, 0, tiled=True)  53.2 us
    pallas_call x10, Pallas kernels, mix_block(): pl.pallas_call(kernel, grid=(1,), in_specs=specs, out_specs=out_spec, out...  43.6 us
    all_gather x1, waiting for transfers between devices, body(): block_full = lax.all_gather(block_out, 'stream', axis=1, tiled=True)  42.8 us
    pallas_call x1, Pallas kernels, attend_back(): pl.pallas_call(kernel, grid_spec=pltpu.PrefetchScalarGridSpec(num_scalar_...  35.8 us
    ppermute x34, waiting for transfers between devices, partner(): return lax.ppermute(shard, 'dp', [(i, i ^ bit) for i in range(peers)])  27.7 us
    pallas_call x1, Pallas kernels, attend(): pl.pallas_call(kernel, grid_spec=pltpu.PrefetchScalarGridSpec(num_scalar_...  27.5 us
  transfers between devices with their start and end apart: 61, of which 13 were waited for; matrix products, arithmetic and copies ran while one was open for 13% of the time, Pallas kernels for 28%

commit v1 on v0

--- a/solution.py
+++ b/solution.py
@@ -190,7 +190,8 @@
         if 0 <= step - 2 < count:
             back = step - 2
             load = third(back, ones[back], twos[back])
-            threes.append(line_hop(gated(load, old), INWARD))
+            ahead = ones[back + 2 : back + 3]
+            threes.append(line_hop(gated(load, old + ahead), INWARD))
             if finish is not None:
                 ends.append(finish(back, ones[back], twos[back], threes[back]))
     return ones, twos, threes
@@ -1081,23 +1082,21 @@
         everyone = lax.all_gather(jnp.concatenate(local, axis=1), "dp", axis=0)
         return both[:, :entries], jnp.sum(everyone, axis=0)
 
-    mixes = []
+    mixes = [mixing_back(heads_share, last_share, history, i, 2) for i in range(2)]
+
+    extra["both"], extra["all"] = small_sums()
 
     def second_hop(i, one):
-        return (pieces[i].astype(F32) + one.astype(F32)).astype(BF)
+        load = (pieces[i].astype(F32) + one.astype(F32)).astype(BF)
+        return after(load, *mixes) if i == 0 else load
 
     def third_hop(i, one, two):
-        return mix_block(spans[i][0], there, pieces[i], last_share, [two], [last_two(i)], None, None)
+        load = mix_block(spans[i][0], there, pieces[i], last_share, [two], [last_two(i)], None, None)
+        return after(load, extra["both" if i == 0 else "all"]) if i < 2 else load
 
     def finish(i, one, two, three):
-        if i in (0, 1):
-            mixes.append(mixing_back(heads_share, last_share, after(history, two), i, 2))
-        if i == 1:
-            extra["both"], extra["all"] = small_sums()
         if i == 3:
-            three = after(three, extra["both"], grad_heads)
-        if i == 4:
-            three = after(three, extra["all"])
+            three = after(three, grad_heads)
         extra["history"], token = mix_block(
             spans[i][0],
             here,

time: 778 us -> 778 us (level)
  waiting for transfers between devices: 157 us -> 206 us
  starting transfers between devices: 102 us -> 80.2 us
  Pallas kernels: 246 us -> 227 us
    ppermute x17, waiting for transfers between devices: 56.7 us -> 81 us  [line_hop(): return lax.ppermute(shard, 'stream', pairs)]
    ppermute x17, starting transfers between devices: 60.7 us -> 39.8 us  [line_hop(): return lax.ppermute(shard, 'stream', pairs)]
    all_to_all x1, waiting for transfers between devices: 9.75 us -> 26.9 us  [small_sums(): both = jnp.sum(lax.all_to_all(both, 'stream', 0, 0, tiled=True), axis=0)]
    pallas_call x1, Pallas kernels: 35.8 us -> 25.2 us  [attend_back(): pl.pallas_call(kernel, grid_spec=pltpu.PrefetchScalarGridSpec(num_scalar_...]
    pallas_call x1, Pallas kernels: 27.5 us -> 19.1 us  [attend(): pl.pallas_call(kernel, grid_spec=pltpu.PrefetchScalarGridSpec(num_scalar_...]
    unnamed x104 -> x110, local copies, waits for them, and re-layouts: 21.5 us -> 20.5 us
  transfers between devices with their start and end apart: 61 -> 61, of which waited for: 13 -> 18; matrix products, arithmetic and copies ran while one was open for 13% -> 12% of each run, Pallas kernels for 28% -> 25%
where the time goes in v1:
time: 778 us; the launch traced here: 768 us
  Pallas kernels  227 us (29%)
  waiting for transfers between devices  206 us (26%)
  blocking collectives  119 us (15%)
  starting transfers between devices  80.2 us (10%)
  local copies, waits for them, and re-layouts  48.6 us (6%)
  other arithmetic  38.5 us (5%)
  matrix products  32.3 us (4%)
  between operations  16.2 us (2%)
    ppermute x17, waiting for transfers between devices, line_hop(): return lax.ppermute(shard, 'stream', pairs)  81 us
    all_to_all x1, blocking collectives, body(): columns = lax.all_to_all(share, 'stream', 0, 0, tiled=True)  53.6 us
    pallas_call x10, Pallas kernels, mix_block(): pl.pallas_call(kernel, grid=(1,), in_specs=specs, out_specs=out_spec, out...  42.7 us
    all_gather x1, waiting for transfers between devices, body(): block_full = lax.all_gather(block_out, 'stream', axis=1, tiled=True)  42.7 us
    ppermute x17, starting transfers between devices, line_hop(): return lax.ppermute(shard, 'stream', pairs)  39.8 us
    ppermute x34, waiting for transfers between devices, partner(): return lax.ppermute(shard, 'dp', [(i, i ^ bit) for i in range(peers)])  34.8 us
    all_to_all x1, waiting for transfers between devices, small_sums(): both = jnp.sum(lax.all_to_all(both, 'stream', 0, 0, tiled=True), axis=0)  26.9 us
    pallas_call x1, Pallas kernels, attend_back(): pl.pallas_call(kernel, grid_spec=pltpu.PrefetchScalarGridSpec(num_scalar_...  25.2 us
  transfers between devices with their start and end apart: 61, of which 18 were waited for; matrix products, arithmetic and copies ran while one was open for 12% of the time, Pallas kernels for 25%

profile of v1, /device:TPU:0, one launch (start us, length us, event | category | flops | bytes accessed | tf_op | source)
XLA Modules:
  0.0 767.7 jit_solution(16970239836409601405)
XLA Ops:
  9.9 9.5 %all-reduce.2 = s32[8]{0:T(128)S(1)} all-reduce(s32[8]{0:T(128)S(1)} %dynamic-update-slice), channel_id=3, replica_groups=mesh['dp'=8,'stream'=4] {'dp'}, use_global_device_ids=true, to_apply=%add.2 | all-reduce | flops 8 | bytes 64
  27.2 16.5 %all-gather.1 = f32[2048,62]{0,1:T(8,128)S(1)} all-gather(f32[512,62]{0,1:T(8,128)S(1)} %concatenate.27), channel_id=4, replica_groups=mesh['dp'=8,'stream'=4] {'stream'}, dimensions={0}, use_global_device_ids=true | all-gather | bytes 634880 | tf_op jit(solution)/shard_map/all_gather | solution.py:938
  52.6 4.0 collective-permute-start.3
  57.2 22.6 %make_streams.1 = (bf16[4,512,2048]{2,1,0:T(8,128)(2,1)}, bf16[4,512,2048]{2,1,0:T(8,128)(2,1)}, f32[512,4]{1,0:T(8,128)}, f32[512,2048]{1,0:T(8,128)}) custom-call(bf16[8,512,2048]{2,1,0:T(8,128)(2,1)} %hist.2, f32[512,32]{1,0:T(8,128)} %copy.66.mix, f32[4,2048]{1,0:T(4,128)} %get-tuple-element.205.gain, f32[4,2048]{1,0:T(4,128)} %get-tuple-element.204.bias), custom_call_target="tpu_custom_call" | custom-call | flops 19800000512 | bytes 66000000 | tf_op jit(solution)/shard_map/make_streams/pallas_call | solution.py:266
  80.7 5.5 put_together.4.w
  86.2 8.8 %project.1 = bf16[8,3,256,128]{3,2,1,0:T(8,128)(2,1)} custom-call(bf16[4,512,2048]{2,1,0:T(8,128)(2,1)} %get-tuple-element.82.x, bf16[8,3,256,512]{3,2,1,0:T(8,128)(2,1)} %put_together.4.w, f32[3,512,128]{2,1,0:T(8,128)} %get-tuple-element.184.table), custom_call_target="tpu_custom_call" | custom-call | flops 8099999744 | bytes 27000000 | tf_op jit(solution)/shard_map/project/pallas_call | solution.py:316
  95.0 24.6 %all_to_all.30.mine = bf16[8,3,256,128]{3,2,1,0:T(8,128)(2,1)S(1)} all-to-all(bf16[8,3,256,128]{3,2,1,0:T(8,128)(2,1)} %project.1), channel_id=1, replica_groups=mesh['dp'=8,'stream'=4] {'dp'}, dimensions={0} | all-to-all | bytes 3145728 | tf_op jit(solution)/shard_map/all_to_all | solution.py:967
  126.3 19.1 %attend.1 = (bf16[8,256,128]{2,1,0:T(8,128)(2,1)}, f32[8,256,128]{2,1,0:T(8,128)}, f32[8,256,1]{2,1,0:T(8,128)}) custom-call(s32[8]{0:T(128)} %subtract_maximum_fusion.first, s32[1]{0:T(128)} %bitcast.1.part, bf16[8,3,256,128]{3,2,1,0:T(8,128)(2,1)} %copy-done.6, bf16[8,2,256,128]{3,2,1,0:T(8,128)(2,1)} %collective-permute-done.9.theirs), custom_call_target="tpu_custom_call" | custom-call | flops 14400000000 | bytes 48000000 | tf_op jit(solution)/shard_map/attend/pallas_call | solution.py:375
  145.4 13.0 %collective-permute-done.25.refs_2_ = bf16[2048,256]{1,0:T(8,128)(2,1)} collective-permute-done((bf16[2048,256]{1,0:T(8,128)(2,1)}, bf16[2048,256]{1,0:T(8,128)(2,1)}, u32[]{:S(2)}, u32[]{:S(2)}) %collective-permute-start.25) | collective-permute-done | bytes 1048608 | tf_op jit(solution)/shard_map/ppermute | solution.py:77
  168.5 5.9 collective-permute-done.26.refs_3_
  174.4 2.7 collective-permute-done.27.refs_4_
  177.9 3.5 all-to-all-start.1
  184.1 7.1 collective-permute-done.11.refs_4_
  191.3 3.2 slice_bitcast_fusion.1.x_ref
  199.7 6.5 put_together.5
  206.2 10.1 %hidden_units.1 = (bf16[512,2048]{1,0:T(8,128)(2,1)}, bf16[512,2048]{1,0:T(8,128)(2,1)}) custom-call(bf16[512,2048]{1,0:T(8,128)(2,1)} %slice_bitcast_fusion.1.x_ref, bf16[2048,2048]{1,0:T(8,128)(2,1)} %bitcast.107), custom_call_target="tpu_custom_call" | custom-call | flops 8099999744 | bytes 27000000 | tf_op jit(solution)/shard_map/hidden_units/pallas_call | solution.py:802
  217.1 6.5 put_together.7.wd.refs_1_
  223.6 12.6 %merge_branches.1 = bf16[4,512,512]{2,1,0:T(8,128)(2,1)} custom-call(bf16[512,512]{1,0:T(8,128)(2,1)} %bitcast.98, bf16[512,2048]{1,0:T(8,128)(2,1)} %get-tuple-element.91.h, bf16[8,512,256]{2,1,0:T(8,128)(2,1)} %put_together.6.wm.refs_1_, bf16[8,2048,256]{2,1,0:T(8,128)(2,1)} %put_together.7.wd.refs_1_, f32[512,2048]{1,0:T(8,128)} %get-tuple-element.101.st, ...), custom_call_target="tpu_custom_call" | custom-call | flops 11699999744 | bytes 39000000 | tf_op jit(solution)/shard_map/merge_branches/pallas_call | solution.py:830
  236.2 53.6 %all_to_all.31 = bf16[4,512,512]{2,1,0:T(8,128)(2,1)S(1)} all-to-all(bf16[4,512,512]{2,1,0:T(8,128)(2,1)} %merge_branches.1), channel_id=1, replica_groups=mesh['dp'=8,'stream'=4] {'stream'}, dimensions={0} | all-to-all | bytes 4194304 | tf_op jit(solution)/shard_map/all_to_all | solution.py:990
  291.4 42.7 %all-gather.8.cloned.1.call-done = bf16[512,2048]{1,0:T(8,128)(2,1)} async-done(((bf16[512,512]{1,0:T(8,128)(2,1)}), bf16[512,2048]{1,0:T(8,128)(2,1)}) %all-gather.8.cloned.1.call-update) | async-done | bytes 2097168 | tf_op jit(solution)/shard_map/all_gather | solution.py:992
  340.4 6.8 convolution_convert_fusion.1
  347.8 3.2 slice_bitcast_fusion.u
  351.0 14.3 %back_through.3 = bf16[512,2048]{1,0:T(8,128)(2,1)} custom-call(bf16[512,2048]{1,0:T(8,128)(2,1)} %copy-done.43, bf16[8,2048,256]{2,1,0:T(8,128)(2,1)} %put_together.7.wd.refs_1_, bf16[512,2048]{1,0:T(8,128)(2,1)} %get-tuple-element.102.refs_2_), custom_call_target="tpu_custom_call" | custom-call | flops 11699999744 | bytes 39000000 | tf_op jit(solution)/shard_map/back_through/pallas_call | solution.py:885
  365.3 7.2 back_through.2
  374.6 4.0 all-to-all-start.3
  378.9 9.8 %fusion.37.g = f32[512,2048]{1,0:T(8,128)} fusion(bf16[512,2048]{1,0:T(8,128)(2,1)S(1)} %copy-done.46, bf16[2048,2048]{1,0:T(8,128)(2,1)} %bitcast.108), kind=kOutput, calls=%fused_computation.99 | convolution fusion | flops 4294967296 | bytes 14680064 | tf_op jit(solution)/shard_map/dot_general | solution.py:72
  388.7 6.4 last_back.1
  397.9 25.2 %attend_back.1 = (bf16[8,3,256,128]{3,2,1,0:T(8,128)(2,1)}, bf16[8,2,256,128]{3,2,1,0:T(8,128)(2,1)}) custom-call(s32[8]{0:T(128)} %subtract_maximum_fusion.first, s32[1]{0:T(128)} %bitcast.1.part, bf16[8,3,256,128]{3,2,1,0:T(8,128)(2,1)} %copy-done.6, bf16[8,2,256,128]{3,2,1,0:T(8,128)(2,1)} %collective-permute-done.9.theirs, ...), custom_call_target="tpu_custom_call" | custom-call | flops 19800000512 | bytes 66000000 | tf_op jit(solution)/shard_map/attend_back/pallas_call | solution.py:449
  423.1 4.4 collective-permute-start.33
  432.8 9.8 %collective-permute-done.34.refs_5_ = bf16[512,2048]{1,0:T(8,128)(2,1)S(1)} collective-permute-done((bf16[512,2048]{1,0:T(8,128)(2,1)}, bf16[512,2048]{1,0:T(8,128)(2,1)S(1)}, u32[]{:S(2)}, u32[]{:S(2)}) %collective-permute-start.34) | collective-permute-done | bytes 2097184 | tf_op jit(solution)/shard_map/ppermute | solution.py:81
  446.9 8.4 %convolution_convert_fusion = bf16[2048,2048]{1,0:T(8,128)(2,1)} fusion(bf16[512,2048]{1,0:T(8,128)(2,1)S(1)} %copy-done.47, bf16[4,512,2048]{2,1,0:T(8,128)(2,1)} %get-tuple-element.82.x), kind=kOutput, calls=%fused_computation | convolution fusion | flops 4299161600 | bytes 12582912 | tf_op jit(solution)/shard_map/dot_general | solution.py:68
  455.3 4.5 all-to-all-start.4
  460.1 3.7 add_convert_fusion
  463.8 2.7 convert_element_type.152
  466.5 20.0 %all-to-all-done.4.part = bf16[8,3,256,128]{3,2,1,0:T(8,128)(2,1)} async-done(((bf16[8,3,256,128]{3,2,1,0:T(8,128)(2,1)}), bf16[8,3,256,128]{3,2,1,0:T(8,128)(2,1)}, u32[]{:S(2)}, u32[]{:S(2)}) %all-to-all-start.4) | async-done | bytes 1572896 | tf_op jit(solution)/shard_map/all_to_all | solution.py:1039
  486.4 17.1 %heads_back.1 = (bf16[3,128,2048]{2,1,0:T(8,128)(2,1)}, bf16[3,128,2048]{2,1,0:T(8,128)(2,1)}, bf16[3,128,2048]{2,1,0:T(8,128)(2,1)}, bf16[3,64,2048]{2,1,0:T(8,...) custom-call(bf16[8,3,256,128]{3,2,1,0:T(8,128)(2,1)} %all-to-all-don, ...), custom_call_target="tpu_custom_call" | custom-call | flops 2700000000 | bytes 9000000 | tf_op jit(solution)/shard_map/heads_back/pallas_call | solution.py:521
  503.5 5.5 collective-permute-start.35
  512.2 10.4 %mixing_back.3 = f32[4,256,8]{2,1,0:T(8,128)} custom-call(bf16[3,512,2048]{2,1,0:T(8,128)(2,1)} %get-tuple-element.117.first, bf16[512,2048]{1,0:T(8,128)(2,1)} %get-tuple-element.105.last.refs_3_.refs_4_, bf16[8,512,2048]{2,1,0:T(8,128)(2,1)} %hist.2), custom_call_target="tpu_custom_call" | custom-call | flops 360000000 | bytes 1200000 | tf_op jit(solution)/shard_map/mixing_back/pallas_call | solution.py:615
  522.6 9.7 %mixing_back.2 = f32[4,256,8]{2,1,0:T(8,128)} custom-call(bf16[3,512,2048]{2,1,0:T(8,128)(2,1)} %get-tuple-element.117.first, bf16[512,2048]{1,0:T(8,128)(2,1)} %get-tuple-element.105.last.refs_3_.refs_4_, bf16[8,512,2048]{2,1,0:T(8,128)(2,1)} %hist.2), custom_call_target="tpu_custom_call" | custom-call | flops 360000000 | bytes 1200000 | tf_op jit(solution)/shard_map/mixing_back/pallas_call | solution.py:615
  532.3 10.6 %collective-permute-done.35.refs_2_ = bf16[3,128,2048]{2,1,0:T(8,128)(2,1)} collective-permute-done((bf16[3,128,2048]{2,1,0:T(8,128)(2,1)}, bf16[3,128,2048]{2,1,0:T(8,128)(2,1)}, u32[]{:S(2)}, u32[]{:S(2)}) %collective-permute-start.35) | collective-permute-done | bytes 1572896 | tf_op jit(solution)/shard_map/ppermute | solution.py:81
  542.9 3.7 add_convert_fusion.3
  548.5 7.1 collective-permute-start.38
  558.4 3.3 all-to-all-start.5
  561.7 14.9 %collective-permute-done.40.refs_2_ = bf16[3,128,2048]{2,1,0:T(8,128)(2,1)} collective-permute-done((bf16[3,128,2048]{2,1,0:T(8,128)(2,1)}, bf16[3,128,2048]{2,1,0:T(8,128)(2,1)}, u32[]{:S(2)}, u32[]{:S(2)}) %collective-permute-start.40) | collective-permute-done | bytes 1572896 | tf_op jit(solution)/shard_map/ppermute | solution.py:81
  576.6 3.7 add_convert_fusion.2
  583.9 26.9 %all-to-all-done.5 = f32[4,512,16]{1,2,0:T(8,128)S(1)} async-done(((f32[4,512,16]{1,2,0:T(8,128)}), f32[4,512,16]{1,2,0:T(8,128)S(1)}, u32[]{:S(2)}, u32[]{:S(2)}) %all-to-all-start.5) | async-done | bytes 131104 | tf_op jit(solution)/shard_map/all_to_all | solution.py:1079
  613.1 4.1 mix_inward.5
  622.7 5.6 collective-permute-start.43
  628.3 3.7 add_convert_fusion.1
  634.2 5.5 collective-permute-done.39.refs_7_
  639.8 5.8 mix_final.5
  647.9 15.2 %all-gather.2 = f32[4096,45]{0,1:T(8,128)S(1)} all-gather(f32[512,45]{0,1:T(8,128)S(1)} %pad_maximum_fusion.3), channel_id=5, replica_groups=mesh['dp'=8,'stream'=4] {'dp'}, dimensions={0}, use_global_device_ids=true | all-gather | bytes 829440 | tf_op jit(solution)/shard_map/all_gather | solution.py:1082
  664.4 4.1 mix_inward.6
  673.1 23.0 %collective-permute-done.44.refs_7_ = bf16[2,128,2048]{2,1,0:T(8,128)(2,1)} collective-permute-done((bf16[2,128,2048]{2,1,0:T(8,128)(2,1)}, bf16[2,128,2048]{2,1,0:T(8,128)(2,1)}, u32[]{:S(2)}, u32[]{:S(2)}) %collective-permute-start.44) | collective-permute-done | bytes 1048608 | tf_op jit(solution)/shard_map/ppermute | solution.py:81
  696.1 5.8 mix_final.6
  702.6 4.1 mix_inward.9
  709.0 2.8 mix_inward.8
  714.1 2.8 mix_inward.7
  723.2 2.8 convert_element_type.172
  726.0 8.9 %collective-permute-done.50.refs_7_ = bf16[2,128,2048]{2,1,0:T(8,128)(2,1)S(1)} collective-permute-done((bf16[2,128,2048]{2,1,0:T(8,128)(2,1)}, bf16[2,128,2048]{2,1,0:T(8,128)(2,1)S(1)}, u32[]{:S(2)}, u32[]{:S(2)}) %collective-permute-start.50) | collective-permute-done | bytes 1048608 | tf_op jit(solution)/shard_map/ppermute | solution.py:81
  735.9 5.8 mix_final.7
  746.2 3.6 mix_final.8
  749.9 6.0 collective-permute-done.46.refs_7_
  756.7 3.6 mix_final.9
  (294 shorter events, 117.0 us)
Async XLA Ops:
  7.2 209.1 %all-gather.6.cloned.1.call-start = ((), (), s32[]{:S(2)}) async-start(), calls=%async_computation.10 | async-start | bytes 2621440 | tf_op jit(solution)/shard_map/all_gather | solution.py:959
  19.4 30.8 %collective-permute-start = (bf16[3,256,512]{2,1,0:T(8,128)(2,1)}, bf16[3,256,512]{2,1,0:T(8,128)(2,1)S(1)}, u32[]{:S(2)}, u32[]{:S(2)}) collective-permute-start(bf16[3,256,512]{2,1,0:T(8,128)(2,1)} %refs_0_), channel_id=1, source_target_pairs={{0,8},{4,12},{8,0},{12,4},{16,24},{20,28},{24,16},{28,20},{1,9},{5... | collective-permute-start | bytes 2359304 | tf_op jit(solution)/shard_map/ppermute | solution.py:77
  20.2 32.4 %collective-permute-start.1 = (bf16[3,256,512]{2,1,0:T(8,128)(2,1)}, bf16[3,256,512]{2,1,0:T(8,128)(2,1)S(1)}, u32[]{:S(2)}, u32[]{:S(2)}) collective-permute-start(bf16[3,256,512]{2,1,0:T(8,128)(2,1)} %refs_0_), channel_id=1, source_target_pairs={{0,16},{4,20},{8,24},{12,28},{16,0},{20,4},{24,8},{28,12},{1,17},{... | collective-permute-start | bytes 2359304 | tf_op jit(solution)/shard_map/ppermute | solution.py:77
  20.7 35.9 %collective-permute-start.2 = (bf16[3,256,512]{2,1,0:T(8,128)(2,1)}, bf16[3,256,512]{2,1,0:T(8,128)(2,1)}, u32[]{:S(2)}, u32[]{:S(2)}) collective-permute-start(bf16[3,256,512]{2,1,0:T(8,128)(2,1)} %refs_0_), channel_id=1, source_target_pairs={{0,24},{4,28},{8,16},{12,20},{16,8},{20,12},{24,0},{28,4},{1,25},{... | collective-permute-start | bytes 2359304 | tf_op jit(solution)/shard_map/ppermute | solution.py:77
  22.9 34.3 %collective-permute-start.5 = (bf16[3,256,512]{2,1,0:T(8,128)(2,1)}, bf16[3,256,512]{2,1,0:T(8,128)(2,1)}, u32[]{:S(2)}, u32[]{:S(2)}) collective-permute-start(bf16[3,256,512]{2,1,0:T(8,128)(2,1)} %refs_0_), channel_id=1, source_target_pairs={{0,4},{4,0},{8,12},{12,8},{16,20},{20,16},{24,28},{28,24},{1,5},{5... | collective-permute-start | bytes 2359304 | tf_op jit(solution)/shard_map/ppermute | solution.py:77
  44.0 247.2 %copy-start.13 = (f32[4,512,62]{1,0,2:T(4,128)}, f32[4,512,62]{1,0,2:T(4,128)S(1)}, u32[]{:S(2)}) copy-start(f32[4,512,62]{1,0,2:T(4,128)S(1)} %reshape.497) | copy-start | bytes 1523716
  50.1 29.6 %copy-start.30 = (bf16[3,256,512]{2,1,0:T(8,128)(2,1)}, bf16[3,256,512]{2,1,0:T(8,128)(2,1)S(1)}, u32[]{:S(2)}) copy-start(bf16[3,256,512]{2,1,0:T(8,128)(2,1)S(1)} %collective-permute-done.refs_1_) | copy-start | bytes 2359300
  52.6 27.2 %copy-start.31 = (bf16[3,256,512]{2,1,0:T(8,128)(2,1)}, bf16[3,256,512]{2,1,0:T(8,128)(2,1)S(1)}, u32[]{:S(2)}) copy-start(bf16[3,256,512]{2,1,0:T(8,128)(2,1)S(1)} %collective-permute-done.1.refs_2_) | copy-start | bytes 2359300
  52.6 33.6 %collective-permute-start.3 = (bf16[256,2048]{1,0:T(8,128)(2,1)}, bf16[256,2048]{1,0:T(8,128)(2,1)}, u32[]{:S(2)}, u32[]{:S(2)}) collective-permute-start(bf16[256,2048]{1,0:T(8,128)(2,1)} %refs_0_.1), channel_id=1, source_target_pairs={{0,8},{4,12},{8,0},{12,4},{16,24},{20,28},{24,16},{28,20},{1,9},{5... | collective-permute-start | bytes 3145736 | tf_op jit(solution)/shard_map/ppermute | solution.py:77
  56.6 29.6 %collective-permute-start.4 = (bf16[256,2048]{1,0:T(8,128)(2,1)}, bf16[256,2048]{1,0:T(8,128)(2,1)}, u32[]{:S(2)}, u32[]{:S(2)}) collective-permute-start(bf16[256,2048]{1,0:T(8,128)(2,1)} %refs_0_.1), channel_id=1, source_target_pairs={{0,16},{4,20},{8,24},{12,28},{16,0},{20,4},{24,8},{28,12},{1,17},{... | collective-permute-start | bytes 3145736 | tf_op jit(solution)/shard_map/ppermute | solution.py:77
  56.6 23.2 %collective-permute-start.6 = (bf16[3,256,512]{2,1,0:T(8,128)(2,1)S(1)}, bf16[3,256,512]{2,1,0:T(8,128)(2,1)S(1)}, u32[]{:S(2)}, u32[]{:S(2)}) collective-permute-start(bf16[3,256,512]{2,1,0:T(8,128)(2,1)S(1)} %collective-permute-done.refs_1_), channel_id=1, source_target_pairs={{0,4},{4,0},{8,12},{12,8},{16,20},{20,16},{24,28},{28,24},{1,5},{5... | collective-permute-start | bytes 2359304 | tf_op jit(solution)/shard_map/ppermute | solution.py:77
  56.6 23.2 %collective-permute-start.7 = (bf16[3,256,512]{2,1,0:T(8,128)(2,1)S(1)}, bf16[3,256,512]{2,1,0:T(8,128)(2,1)}, u32[]{:S(2)}, u32[]{:S(2)}) collective-permute-start(bf16[3,256,512]{2,1,0:T(8,128)(2,1)S(1)} %collective-permute-done.1.refs_2_), channel_id=1, source_target_pairs={{0,4},{4,0},{8,12},{12,8},{16,20},{20,16},{24,28},{28,24},{1,5},{5... | collective-permute-start | bytes 2359304 | tf_op jit(solution)/shard_map/ppermute | solution.py:77
  57.1 22.7 %collective-permute-start.8 = (bf16[3,256,512]{2,1,0:T(8,128)(2,1)}, bf16[3,256,512]{2,1,0:T(8,128)(2,1)}, u32[]{:S(2)}, u32[]{:S(2)}) collective-permute-start(bf16[3,256,512]{2,1,0:T(8,128)(2,1)} %collective-permute-done.2.refs_3_), channel_id=1, source_target_pairs={{0,4},{4,0},{8,12},{12,8},{16,20},{20,16},{24,28},{28,24},{1,5},{5... | collective-permute-start | bytes 2359304 | tf_op jit(solution)/shard_map/ppermute | solution.py:77
  120.7 4.7 collective-permute-start.9
  121.2 39.8 %collective-permute-start.17 = (bf16[512,256]{1,0:T(8,128)(2,1)S(1)}, bf16[512,256]{1,0:T(8,128)(2,1)S(1)}, u32[]{:S(2)}, u32[]{:S(2)}) collective-permute-start(bf16[512,256]{1,0:T(8,128)(2,1)S(1)} %copy-done.37), channel_id=1, source_target_pairs={{0,8},{4,12},{8,0},{12,4},{16,24},{20,28},{24,16},{28,20},{1,9},{5... | collective-permute-start | bytes 786440 | tf_op jit(solution)/shard_map/ppermute | solution.py:77
  121.8 41.1 %collective-permute-start.18 = (bf16[512,256]{1,0:T(8,128)(2,1)S(1)}, bf16[512,256]{1,0:T(8,128)(2,1)}, u32[]{:S(2)}, u32[]{:S(2)}) collective-permute-start(bf16[512,256]{1,0:T(8,128)(2,1)S(1)} %copy-done.37), channel_id=1, source_target_pairs={{0,16},{4,20},{8,24},{12,28},{16,0},{20,4},{24,8},{28,12},{1,17},{... | collective-permute-start | bytes 786440 | tf_op jit(solution)/shard_map/ppermute | solution.py:77
  122.7 40.2 %collective-permute-start.19 = (bf16[512,256]{1,0:T(8,128)(2,1)S(1)}, bf16[512,256]{1,0:T(8,128)(2,1)}, u32[]{:S(2)}, u32[]{:S(2)}) collective-permute-start(bf16[512,256]{1,0:T(8,128)(2,1)S(1)} %copy-done.37), channel_id=1, source_target_pairs={{0,24},{4,28},{8,16},{12,20},{16,8},{20,12},{24,0},{28,4},{1,25},{... | collective-permute-start | bytes 786440 | tf_op jit(solution)/shard_map/ppermute | solution.py:77
  124.8 33.7 %collective-permute-start.25 = (bf16[2048,256]{1,0:T(8,128)(2,1)}, bf16[2048,256]{1,0:T(8,128)(2,1)}, u32[]{:S(2)}, u32[]{:S(2)}) collective-permute-start(bf16[2048,256]{1,0:T(8,128)(2,1)} %refs_0_.3), channel_id=1, source_target_pairs={{0,16},{4,20},{8,24},{12,28},{16,0},{20,4},{24,8},{28,12},{1,17},{... | collective-permute-start | bytes 3145736 | tf_op jit(solution)/shard_map/ppermute | solution.py:77
  125.4 35.7 %collective-permute-start.24 = (bf16[2048,256]{1,0:T(8,128)(2,1)}, bf16[2048,256]{1,0:T(8,128)(2,1)}, u32[]{:S(2)}, u32[]{:S(2)}) collective-permute-start(bf16[2048,256]{1,0:T(8,128)(2,1)} %refs_0_.3), channel_id=1, source_target_pairs={{0,8},{4,12},{8,0},{12,4},{16,24},{20,28},{24,16},{28,20},{1,9},{5... | collective-permute-start | bytes 3145736 | tf_op jit(solution)/shard_map/ppermute | solution.py:77
  159.5 14.9 %collective-permute-start.26 = (bf16[1024,256]{1,0:T(8,128)(2,1)S(1)}, bf16[1024,256]{1,0:T(8,128)(2,1)S(1)}, u32[]{:S(2)}, u32[]{:S(2)}) collective-permute-start(bf16[1024,256]{1,0:T(8,128)(2,1)S(1)} %slice.102), channel_id=1, source_target_pairs={{0,8},{4,12},{8,0},{12,4},{16,24},{20,28},{24,16},{28,20},{1,9},{5... | collective-permute-start | bytes 1572872 | tf_op jit(solution)/shard_map/ppermute | solution.py:77
  161.0 2.3 collective-permute-start.21
  162.2 14.9 %collective-permute-start.27 = (bf16[1024,256]{1,0:T(8,128)(2,1)S(1)}, bf16[1024,256]{1,0:T(8,128)(2,1)S(1)}, u32[]{:S(2)}, u32[]{:S(2)}) collective-permute-start(bf16[1024,256]{1,0:T(8,128)(2,1)S(1)} %slice.103), channel_id=1, source_target_pairs={{0,16},{4,20},{8,24},{12,28},{16,0},{20,4},{24,8},{28,12},{1,17},{... | collective-permute-start | bytes 1572872 | tf_op jit(solution)/shard_map/ppermute | solution.py:77
  162.9 3.5 collective-permute-start.22
  163.0 4.4 collective-permute-start.23
  164.1 4.4 collective-permute-start.20
  166.4 17.7 %collective-permute-start.10 = (bf16[128,2048]{1,0:T(8,128)(2,1)S(1)}, bf16[128,2048]{1,0:T(8,128)(2,1)}, u32[]{:S(2)}, u32[]{:S(2)}) collective-permute-start(bf16[128,2048]{1,0:T(8,128)(2,1)S(1)} %slice.100), channel_id=1, source_target_pairs={{0,8},{4,12},{8,0},{12,4},{16,24},{20,28},{24,16},{28,20},{1,9},{5... | collective-permute-start | bytes 1572872 | tf_op jit(solution)/shard_map/ppermute | solution.py:77
  167.4 23.8 %collective-permute-start.11 = (bf16[128,2048]{1,0:T(8,128)(2,1)S(1)}, bf16[128,2048]{1,0:T(8,128)(2,1)}, u32[]{:S(2)}, u32[]{:S(2)}) collective-permute-start(bf16[128,2048]{1,0:T(8,128)(2,1)S(1)} %slice.101), channel_id=1, source_target_pairs={{0,16},{4,20},{8,24},{12,28},{16,0},{20,4},{24,8},{28,12},{1,17},{... | collective-permute-start | bytes 1572872 | tf_op jit(solution)/shard_map/ppermute | solution.py:77
  168.5 30.2 %collective-permute-start.13 = (bf16[256,2048]{1,0:T(8,128)(2,1)}, bf16[256,2048]{1,0:T(8,128)(2,1)}, u32[]{:S(2)}, u32[]{:S(2)}) collective-permute-start(bf16[256,2048]{1,0:T(8,128)(2,1)} %collective-permute-done.3.refs_1_), channel_id=1, source_target_pairs={{0,4},{4,0},{8,12},{12,8},{16,20},{20,16},{24,28},{28,24},{1,5},{5... | collective-permute-start | bytes 3145736 | tf_op jit(solution)/shard_map/ppermute | solution.py:77
  174.4 24.8 %collective-permute-start.14 = (bf16[256,2048]{1,0:T(8,128)(2,1)}, bf16[256,2048]{1,0:T(8,128)(2,1)}, u32[]{:S(2)}, u32[]{:S(2)}) collective-permute-start(bf16[256,2048]{1,0:T(8,128)(2,1)} %collective-permute-done.4.refs_2_), channel_id=1, source_target_pairs={{0,4},{4,0},{8,12},{12,8},{16,20},{20,16},{24,28},{28,24},{1,5},{5... | collective-permute-start | bytes 3145736 | tf_op jit(solution)/shard_map/ppermute | solution.py:77
  177.9 21.4 %collective-permute-start.12 = (bf16[256,2048]{1,0:T(8,128)(2,1)}, bf16[256,2048]{1,0:T(8,128)(2,1)}, u32[]{:S(2)}, u32[]{:S(2)}) collective-permute-start(bf16[256,2048]{1,0:T(8,128)(2,1)} %refs_0_.1), channel_id=1, source_target_pairs={{0,4},{4,0},{8,12},{12,8},{16,20},{20,16},{24,28},{28,24},{1,5},{5... | collective-permute-start | bytes 3145736 | tf_op jit(solution)/shard_map/ppermute | solution.py:77
  177.9 19.0 %all-to-all-start.1 = ((bf16[8,256,128]{2,1,0:T(8,128)(2,1)}), bf16[8,256,128]{2,1,0:T(8,128)(2,1)S(1)}, u32[]{:S(2)}, u32[]{:S(2)}) async-start(bf16[8,256,128]{2,1,0:T(8,128)(2,1)} %get-tuple-element.83), calls=%async_computation.1 | async-start | bytes 1048576 | tf_op jit(solution)/shard_map/all_to_all | solution.py:973
  181.4 152.7 %all-gather.8.cloned.1.call-start = ((), (), s32[]{:S(2)}) async-start(), calls=%async_computation.11 | async-start | bytes 2621440 | tf_op jit(solution)/shard_map/all_gather | solution.py:992
  184.1 14.1 %collective-permute-start.15 = (bf16[128,2048]{1,0:T(8,128)(2,1)}, bf16[128,2048]{1,0:T(8,128)(2,1)}, u32[]{:S(2)}, u32[]{:S(2)}) collective-permute-start(bf16[128,2048]{1,0:T(8,128)(2,1)} %collective-permute-done.10.refs_3_), channel_id=1, source_target_pairs={{0,4},{4,0},{8,12},{12,8},{16,20},{20,16},{24,28},{28,24},{1,5},{5... | collective-permute-start | bytes 1572872 | tf_op jit(solution)/shard_map/ppermute | solution.py:77
  191.2 7.4 collective-permute-start.16
  198.2 18.1 %collective-permute-start.30 = (bf16[2048,256]{1,0:T(8,128)(2,1)}, bf16[2048,256]{1,0:T(8,128)(2,1)}, u32[]{:S(2)}, u32[]{:S(2)}) collective-permute-start(bf16[2048,256]{1,0:T(8,128)(2,1)} %collective-permute-done.25.refs_2_), channel_id=1, source_target_pairs={{0,4},{4,0},{8,12},{12,8},{16,20},{20,16},{24,28},{28,24},{1,5},{5... | collective-permute-start | bytes 3145736 | tf_op jit(solution)/shard_map/ppermute | solution.py:77
  198.7 17.7 %collective-permute-start.29 = (bf16[2048,256]{1,0:T(8,128)(2,1)}, bf16[2048,256]{1,0:T(8,128)(2,1)}, u32[]{:S(2)}, u32[]{:S(2)}) collective-permute-start(bf16[2048,256]{1,0:T(8,128)(2,1)} %collective-permute-done.24.refs_1_), channel_id=1, source_target_pairs={{0,4},{4,0},{8,12},{12,8},{16,20},{20,16},{24,28},{28,24},{1,5},{5... | collective-permute-start | bytes 3145736 | tf_op jit(solution)/shard_map/ppermute | solution.py:77
  198.7 17.6 %collective-permute-start.28 = (bf16[2048,256]{1,0:T(8,128)(2,1)S(1)}, bf16[2048,256]{1,0:T(8,128)(2,1)}, u32[]{:S(2)}, u32[]{:S(2)}) collective-permute-start(bf16[2048,256]{1,0:T(8,128)(2,1)S(1)} %copy-done.29), channel_id=1, source_target_pairs={{0,4},{4,0},{8,12},{12,8},{16,20},{20,16},{24,28},{28,24},{1,5},{5... | collective-permute-start | bytes 3145736 | tf_op jit(solution)/shard_map/ppermute | solution.py:77
  199.2 17.1 %collective-permute-start.31 = (bf16[1024,256]{1,0:T(8,128)(2,1)S(1)}, bf16[1024,256]{1,0:T(8,128)(2,1)S(1)}, u32[]{:S(2)}, u32[]{:S(2)}) collective-permute-start(bf16[1024,256]{1,0:T(8,128)(2,1)S(1)} %collective-permute-done.26.refs_3_), channel_id=1, source_target_pairs={{0,4},{4,0},{8,12},{12,8},{16,20},{20,16},{24,28},{28,24},{1,5},{5... | collective-permute-start | bytes 1572872 | tf_op jit(solution)/shard_map/ppermute | solution.py:77
  199.3 17.0 %collective-permute-start.32 = (bf16[1024,256]{1,0:T(8,128)(2,1)S(1)}, bf16[1024,256]{1,0:T(8,128)(2,1)}, u32[]{:S(2)}, u32[]{:S(2)}) collective-permute-start(bf16[1024,256]{1,0:T(8,128)(2,1)S(1)} %copy-done.35), channel_id=1, source_target_pairs={{0,4},{4,0},{8,12},{12,8},{16,20},{20,16},{24,28},{28,24},{1,5},{5... | collective-permute-start | bytes 1572872 | tf_op jit(solution)/shard_map/ppermute | solution.py:77
  291.0 172.8 %reduce-scatter.5.cloned.1.call-start = ((), (), s32[]{:S(2)}) async-start(), calls=%async_computation.12 | async-start | bytes 9437184 | tf_op jit(solution)/shard_map/reduce_scatter | solution.py:1018
  374.6 22.5 %all-to-all-start.3 = ((bf16[8,256,128]{2,1,0:T(8,128)(2,1)}), bf16[8,256,128]{2,1,0:T(8,128)(2,1)S(1)}, u32[]{:S(2)}, u32[]{:S(2)}) async-start(bf16[8,256,128]{2,1,0:T(8,128)(2,1)} %bitcast.20), calls=%async_computation.3 | async-start | bytes 1048576 | tf_op jit(solution)/shard_map/all_to_all | solution.py:1029
  378.6 242.2 %reduce-scatter.7.cloned.1.call-start = ((), (), s32[]{:S(2)}) async-start(), calls=%async_computation.13 | async-start | bytes 2359296 | tf_op jit(solution)/shard_map/reduce_scatter | solution.py:1053
  395.1 47.6 %collective-permute-start.34 = (bf16[512,2048]{1,0:T(8,128)(2,1)}, bf16[512,2048]{1,0:T(8,128)(2,1)S(1)}, u32[]{:S(2)}, u32[]{:S(2)}) collective-permute-start(bf16[512,2048]{1,0:T(8,128)(2,1)} %get-tuple-element.105.last.refs_3_.refs_4_), channel_id=1, source_target_pairs={{0,1},{3,2},{4,5},{7,6},{8,9},{11,10},{12,13},{15,14},{16,17},{19,... | collective-permute-start | bytes 6291464 | tf_op jit(solution)/shard_map/ppermute | solution.py:81
  423.1 6.9 collective-permute-start.33
  445.3 277.9 %reduce-scatter.11.cloned.1.call-start = ((), (), s32[]{:S(2)}) async-start(), calls=%async_computation.15 | async-start | bytes 9437184 | tf_op jit(solution)/shard_map/reduce_scatter | solution.py:1055
  455.3 31.1 %all-to-all-start.4 = ((bf16[8,3,256,128]{3,2,1,0:T(8,128)(2,1)}), bf16[8,3,256,128]{3,2,1,0:T(8,128)(2,1)}, u32[]{:S(2)}, u32[]{:S(2)}) async-start(bf16[8,3,256,128]{3,2,1,0:T(8,128)(2,1)} %pad_maximum_fusion), calls=%async_computation.4 | async-start | bytes 3145728 | tf_op jit(solution)/shard_map/all_to_all | solution.py:1039
  459.8 281.9 %reduce-scatter.9.cloned.1.call-start = ((), (), s32[]{:S(2)}) async-start(), calls=%async_computation.14 | async-start | bytes 7077888 | tf_op jit(solution)/shard_map/reduce_scatter | solution.py:1054
  503.5 39.4 %collective-permute-start.35 = (bf16[3,128,2048]{2,1,0:T(8,128)(2,1)}, bf16[3,128,2048]{2,1,0:T(8,128)(2,1)}, u32[]{:S(2)}, u32[]{:S(2)}) collective-permute-start(bf16[3,128,2048]{2,1,0:T(8,128)(2,1)} %get-tuple-element.116.refs_1_), channel_id=1, source_target_pairs={{0,1},{3,2},{4,5},{7,6},{8,9},{11,10},{12,13},{15,14},{16,17},{19,... | collective-permute-start | bytes 4718600 | tf_op jit(solution)/shard_map/ppermute | solution.py:81
  509.0 67.6 %collective-permute-start.40 = (bf16[3,128,2048]{2,1,0:T(8,128)(2,1)}, bf16[3,128,2048]{2,1,0:T(8,128)(2,1)}, u32[]{:S(2)}, u32[]{:S(2)}) collective-permute-start(bf16[3,128,2048]{2,1,0:T(8,128)(2,1)} %get-tuple-element.126.refs_1_), channel_id=1, source_target_pairs={{0,1},{3,2},{4,5},{7,6},{8,9},{11,10},{12,13},{15,14},{16,17},{19,... | collective-permute-start | bytes 4718600 | tf_op jit(solution)/shard_map/ppermute | solution.py:81
  511.4 100.3 %collective-permute-start.37 = (bf16[512,2048]{1,0:T(8,128)(2,1)}, bf16[512,2048]{1,0:T(8,128)(2,1)S(1)}, u32[]{:S(2)}, u32[]{:S(2)}) collective-permute-start(bf16[512,2048]{1,0:T(8,128)(2,1)} %add_convert_fusion), channel_id=1, source_target_pairs={{1,2},{2,1},{5,6},{6,5},{9,10},{10,9},{13,14},{14,13},{17,18},{18,... | collective-permute-start | bytes 6291464 | tf_op jit(solution)/shard_map/ppermute | solution.py:81
  546.7 65.0 %collective-permute-start.36 = (bf16[3,128,2048]{2,1,0:T(8,128)(2,1)}, bf16[3,128,2048]{2,1,0:T(8,128)(2,1)}, u32[]{:S(2)}, u32[]{:S(2)}) collective-permute-start(bf16[3,128,2048]{2,1,0:T(8,128)(2,1)} %add_convert_fusion.3), channel_id=1, source_target_pairs={{1,2},{2,1},{5,6},{6,5},{9,10},{10,9},{13,14},{14,13},{17,18},{18,... | collective-permute-start | bytes 4718600 | tf_op jit(solution)/shard_map/ppermute | solution.py:81
  548.5 68.8 %collective-permute-start.38 = (bf16[3,128,2048]{2,1,0:T(8,128)(2,1)}, bf16[3,128,2048]{2,1,0:T(8,128)(2,1)}, u32[]{:S(2)}, u32[]{:S(2)}) collective-permute-start(bf16[3,128,2048]{2,1,0:T(8,128)(2,1)} %get-tuple-element.123.refs_1_), channel_id=1, source_target_pairs={{0,1},{3,2},{4,5},{7,6},{8,9},{11,10},{12,13},{15,14},{16,17},{19,... | collective-permute-start | bytes 4718600 | tf_op jit(solution)/shard_map/ppermute | solution.py:81
  558.4 52.4 %all-to-all-start.5 = ((f32[4,512,16]{1,2,0:T(8,128)}), f32[4,512,16]{1,2,0:T(8,128)S(1)}, u32[]{:S(2)}, u32[]{:S(2)}) async-start(f32[4,512,16]{1,2,0:T(8,128)} %maximum_maximum_fusion), calls=%async_computation.6 | async-start | bytes 262144 | tf_op jit(solution)/shard_map/all_to_all | solution.py:1079
  580.3 65.2 %collective-permute-start.41 = (bf16[3,128,2048]{2,1,0:T(8,128)(2,1)}, bf16[3,128,2048]{2,1,0:T(8,128)(2,1)}, u32[]{:S(2)}, u32[]{:S(2)}) collective-permute-start(bf16[3,128,2048]{2,1,0:T(8,128)(2,1)} %add_convert_fusion.2), channel_id=1, source_target_pairs={{1,2},{2,1},{5,6},{6,5},{9,10},{10,9},{13,14},{14,13},{17,18},{18,... | collective-permute-start | bytes 4718600 | tf_op jit(solution)/shard_map/ppermute | solution.py:81
  617.2 22.5 %collective-permute-start.39 = (bf16[2,128,2048]{2,1,0:T(8,128)(2,1)}, bf16[2,128,2048]{2,1,0:T(8,128)(2,1)}, u32[]{:S(2)}, u32[]{:S(2)}) collective-permute-start(bf16[2,128,2048]{2,1,0:T(8,128)(2,1)} %mix_inward.5), channel_id=1, source_target_pairs={{1,0},{2,3},{5,4},{6,7},{9,8},{10,11},{13,12},{14,15},{17,16},{18,... | collective-permute-start | bytes 3145736 | tf_op jit(solution)/shard_map/ppermute | solution.py:81
  622.7 45.8 %collective-permute-start.43 = (bf16[3,64,2048]{2,1,0:T(8,128)(2,1)S(1)}, bf16[3,64,2048]{2,1,0:T(8,128)(2,1)S(1)}, u32[]{:S(2)}, u32[]{:S(2)}) collective-permute-start(bf16[3,64,2048]{2,1,0:T(8,128)(2,1)S(1)} %copy-done.4), channel_id=1, source_target_pairs={{0,1},{3,2},{4,5},{7,6},{8,9},{11,10},{12,13},{15,14},{16,17},{19,... | collective-permute-start | bytes 2359304 | tf_op jit(solution)/shard_map/ppermute | solution.py:81
  632.0 70.7 %collective-permute-start.49 = (bf16[3,128,2048]{2,1,0:T(8,128)(2,1)}, bf16[3,128,2048]{2,1,0:T(8,128)(2,1)}, u32[]{:S(2)}, u32[]{:S(2)}) collective-permute-start(bf16[3,128,2048]{2,1,0:T(8,128)(2,1)} %add_convert_fusion.1), channel_id=1, source_target_pairs={{1,2},{2,1},{5,6},{6,5},{9,10},{10,9},{13,14},{14,13},{17,18},{18,... | collective-permute-start | bytes 4718600 | tf_op jit(solution)/shard_map/ppermute | solution.py:81
  645.6 26.1 %collective-permute-start.42 = (bf16[3,64,2048]{2,1,0:T(8,128)(2,1)S(1)}, bf16[3,64,2048]{2,1,0:T(8,128)(2,1)}, u32[]{:S(2)}, u32[]{:S(2)}) collective-permute-start(bf16[3,64,2048]{2,1,0:T(8,128)(2,1)S(1)} %copy-done.3), channel_id=1, source_target_pairs={{0,1},{3,2},{4,5},{7,6},{8,9},{11,10},{12,13},{15,14},{16,17},{19,... | collective-permute-start | bytes 2359304 | tf_op jit(solution)/shard_map/ppermute | solution.py:81
  668.5 27.6 %collective-permute-start.44 = (bf16[2,128,2048]{2,1,0:T(8,128)(2,1)}, bf16[2,128,2048]{2,1,0:T(8,128)(2,1)}, u32[]{:S(2)}, u32[]{:S(2)}) collective-permute-start(bf16[2,128,2048]{2,1,0:T(8,128)(2,1)} %mix_inward.6), channel_id=1, source_target_pairs={{1,0},{2,3},{5,4},{6,7},{9,8},{10,11},{13,12},{14,15},{17,16},{18,... | collective-permute-start | bytes 3145736 | tf_op jit(solution)/shard_map/ppermute | solution.py:81
  671.0 37.1 %collective-permute-start.47 = (bf16[3,64,2048]{2,1,0:T(8,128)(2,1)}, bf16[3,64,2048]{2,1,0:T(8,128)(2,1)S(1)}, u32[]{:S(2)}, u32[]{:S(2)}) collective-permute-start(bf16[3,64,2048]{2,1,0:T(8,128)(2,1)} %add_convert_fusion.5), channel_id=1, source_target_pairs={{1,2},{2,1},{5,6},{6,5},{9,10},{10,9},{13,14},{14,13},{17,18},{18,... | collective-permute-start | bytes 2359304 | tf_op jit(solution)/shard_map/ppermute | solution.py:81
  701.9 11.3 %collective-permute-start.45 = (bf16[3,64,2048]{2,1,0:T(8,128)(2,1)S(1)}, bf16[3,64,2048]{2,1,0:T(8,128)(2,1)S(1)}, u32[]{:S(2)}, u32[]{:S(2)}) collective-permute-start(bf16[3,64,2048]{2,1,0:T(8,128)(2,1)S(1)} %add_convert_fusion.6), channel_id=1, source_target_pairs={{1,2},{2,1},{5,6},{6,5},{9,10},{10,9},{13,14},{14,13},{17,18},{18,... | collective-permute-start | bytes 2359304 | tf_op jit(solution)/shard_map/ppermute | solution.py:81
  706.8 28.1 %collective-permute-start.50 = (bf16[2,128,2048]{2,1,0:T(8,128)(2,1)}, bf16[2,128,2048]{2,1,0:T(8,128)(2,1)S(1)}, u32[]{:S(2)}, u32[]{:S(2)}) collective-permute-start(bf16[2,128,2048]{2,1,0:T(8,128)(2,1)} %mix_inward.9), channel_id=1, source_target_pairs={{1,0},{2,3},{5,4},{6,7},{9,8},{10,11},{13,12},{14,15},{17,16},{18,... | collective-permute-start | bytes 3145736 | tf_op jit(solution)/shard_map/ppermute | solution.py:81
  711.8 34.5 %collective-permute-start.48 = (bf16[2,64,2048]{2,1,0:T(8,128)(2,1)}, bf16[2,64,2048]{2,1,0:T(8,128)(2,1)}, u32[]{:S(2)}, u32[]{:S(2)}) collective-permute-start(bf16[2,64,2048]{2,1,0:T(8,128)(2,1)} %mix_inward.8), channel_id=1, source_target_pairs={{1,0},{2,3},{5,4},{6,7},{9,8},{10,11},{13,12},{14,15},{17,16},{18,... | collective-permute-start | bytes 1572872 | tf_op jit(solution)/shard_map/ppermute | solution.py:81
  716.9 39.0 %collective-permute-start.46 = (bf16[2,64,2048]{2,1,0:T(8,128)(2,1)}, bf16[2,64,2048]{2,1,0:T(8,128)(2,1)S(1)}, u32[]{:S(2)}, u32[]{:S(2)}) collective-permute-start(bf16[2,64,2048]{2,1,0:T(8,128)(2,1)} %mix_inward.7), channel_id=1, source_target_pairs={{1,0},{2,3},{5,4},{6,7},{9,8},{10,11},{13,12},{14,15},{17,16},{18,... | collective-permute-start | bytes 1572872 | tf_op jit(solution)/shard_map/ppermute | solution.py:81
  (46 other events, 314.4 us)
Sparse Core Ops, SparseCore 0:
  124.9 45.2 all-gather.5
  291.1 42.9 all-gather.7
  347.4 75.7 reduce-scatter.4
  445.5 51.3 reduce-scatter.6
  500.2 71.4 reduce-scatter.10
  575.0 61.6 reduce-scatter.8

commit v2 on v1

--- a/solution.py
+++ b/solution.py
@@ -948,9 +948,8 @@
     if near:
         early = (got_heads.by_x, got_heads.by_y, got_heads.across)
         history = after(history, *early)
-        w_up, w_merge = after(w_up, *early[:2]), after(w_merge, *early[:2])
+        w_up = after(w_up, *early[:2])
     got_up = Gathered(w_up)
-    got_merge = Gathered(w_merge, direct=near)
     gains, biases = norms[:, 0], norms[:, 1]
     mix_rows = jnp.transpose(mix_all, (1, 0, 2)).reshape(tokens, members * entries)
 
@@ -965,22 +964,23 @@
         place = jnp.arange(shards, dtype=jnp.int32)
         first_key = jnp.maximum(place - offsets // tokens, 0).astype(jnp.int32)
         own = lax.all_to_all(projected, "dp", 0, 0, tiled=True)
-        got_down = Gathered(after(w_down, own))
         other = partner(own[:, 1:], 1)
+        full_up = got_up.whole(own)
         result, exact, level = attend(own, other, first_key, side)
-        full_up = got_up.whole(result)
-        full_merge = got_merge.whole(result)
+        got_down = Gathered(after(w_down, result))
+        got_merge = Gathered(after(w_merge, result), direct=True)
+        full_merge = got_merge.whole()
         back = lax.all_to_all(result, "dp", 0, 0, tiled=True)
         attended = jnp.transpose(back.reshape(heads_here, tokens, HD), (1, 0, 2)).reshape(tokens, -1)
     else:
         got_down = Gathered(w_down)
         full_up = got_up.whole()
-        full_merge = got_merge.whole()
+        full_merge = Gathered(w_merge).whole()
         split = projected.reshape(heads_here, 2, 3, half, HD)
         split = jnp.transpose(split, (2, 1, 3, 0, 4)).reshape(3, tokens, heads_here, HD)
         result, kept = far_attend(split[0], split[1], split[2], shard_offset)
         attended = result.reshape(tokens, -1).astype(BF)
-    full_down = got_down.whole(result)
+    full_down = got_down.whole()
     flat_up = full_up.reshape(width, -1)
     hidden, slope = hidden_units(normed[members - 1], flat_up)
     attended = after(attended, hidden)
@@ -1092,11 +1092,11 @@
 
     def third_hop(i, one, two):
         load = mix_block(spans[i][0], there, pieces[i], last_share, [two], [last_two(i)], None, None)
-        return after(load, extra["both" if i == 0 else "all"]) if i < 2 else load
+        return after(load, extra["both"]) if i == 2 else load
 
     def finish(i, one, two, three):
         if i == 3:
-            three = after(three, grad_heads)
+            three = after(three, grad_heads, extra["all"])
         extra["history"], token = mix_block(
             spans[i][0],
             here,

time: 778 us -> 767 us (0.986)
  waiting for transfers between devices: 206 us -> 174 us
  starting transfers between devices: 80.2 us -> 96.8 us
    all_to_all x1, waiting for transfers between devices: 26.9 us -> 0.01 us  [small_sums(): both = jnp.sum(lax.all_to_all(both, 'stream', 0, 0, tiled=True), axis=0)]
    ppermute x34, starting transfers between devices: 23.9 us -> 39 us  [partner(): return lax.ppermute(shard, 'dp', [(i, i ^ bit) for i in range(peers)])]
    unnamed x110 -> x96, local copies, waits for them, and re-layouts: 20.5 us -> 18.9 us
  transfers between devices with their start and end apart: 61 -> 61, of which waited for: 18 -> 16; matrix products, arithmetic and copies ran while one was open for 12% -> 12% of each run, Pallas kernels for 25% -> 26%
where the time goes in v2:
time: 767 us; the launch traced here: 753 us
  Pallas kernels  228 us (30%)
  waiting for transfers between devices  174 us (23%)
  blocking collectives  123 us (16%)
  starting transfers between devices  96.8 us (13%)
  local copies, waits for them, and re-layouts  43.6 us (6%)
  other arithmetic  40.2 us (5%)
  matrix products  31.9 us (4%)
  between operations  16.2 us (2%)
    ppermute x17, waiting for transfers between devices, line_hop(): return lax.ppermute(shard, 'stream', pairs)  76.5 us
    all_to_all x1, blocking collectives, body(): columns = lax.all_to_all(share, 'stream', 0, 0, tiled=True)  54.8 us
    all_gather x1, waiting for transfers between devices, body(): block_full = lax.all_gather(block_out, 'stream', axis=1, tiled=True)  43.5 us
    pallas_call x10, Pallas kernels, mix_block(): pl.pallas_call(kernel, grid=(1,), in_specs=specs, out_specs=out_spec, out...  43.5 us
    ppermute x34, starting transfers between devices, partner(): return lax.ppermute(shard, 'dp', [(i, i ^ bit) for i in range(peers)])  39 us
    ppermute x17, starting transfers between devices, line_hop(): return lax.ppermute(shard, 'stream', pairs)  39 us
    ppermute x34, waiting for transfers between devices, partner(): return lax.ppermute(shard, 'dp', [(i, i ^ bit) for i in range(peers)])  33.6 us
    pallas_call x1, Pallas kernels, attend_back(): pl.pallas_call(kernel, grid_spec=pltpu.PrefetchScalarGridSpec(num_scalar_...  25.2 us
  transfers between devices with their start and end apart: 61, of which 16 were waited for; matrix products, arithmetic and copies ran while one was open for 12% of the time, Pallas kernels for 26%

profile of v2, /device:TPU:0, one launch (start us, length us, event | category | flops | bytes accessed | tf_op | source)
XLA Modules:
  0.0 753.4 jit_solution(13783657280077046866)
XLA Ops:
  9.9 9.5 %all-reduce.2 = s32[8]{0:T(128)S(1)} all-reduce(s32[8]{0:T(128)S(1)} %dynamic-update-slice), channel_id=3, replica_groups=mesh['dp'=8,'stream'=4] {'dp'}, use_global_device_ids=true, to_apply=%add.2 | all-reduce | flops 8 | bytes 64
  27.2 16.5 %all-gather.1 = f32[2048,62]{0,1:T(8,128)S(1)} all-gather(f32[512,62]{0,1:T(8,128)S(1)} %concatenate.27), channel_id=4, replica_groups=mesh['dp'=8,'stream'=4] {'stream'}, dimensions={0}, use_global_device_ids=true | all-gather | bytes 634880 | tf_op jit(solution)/shard_map/all_gather | solution.py:938
  49.5 3.4 collective-permute-done.1.refs_2_
  52.9 3.8 collective-permute-start.3
  57.3 22.6 %make_streams.1 = (bf16[4,512,2048]{2,1,0:T(8,128)(2,1)}, bf16[4,512,2048]{2,1,0:T(8,128)(2,1)}, f32[512,4]{1,0:T(8,128)}, f32[512,2048]{1,0:T(8,128)}) custom-call(bf16[8,512,2048]{2,1,0:T(8,128)(2,1)} %hist.2, f32[512,32]{1,0:T(8,128)} %copy.66.mix, f32[4,2048]{1,0:T(4,128)} %get-tuple-element.189.gain, f32[4,2048]{1,0:T(4,128)} %get-tuple-element.188.bias), custom_call_target="tpu_custom_call" | custom-call | flops 19800000512 | bytes 66000000 | tf_op jit(solution)/shard_map/make_streams/pallas_call | solution.py:266
  79.9 5.5 put_together.4.w
  86.8 8.8 %project.1 = bf16[8,3,256,128]{3,2,1,0:T(8,128)(2,1)} custom-call(bf16[4,512,2048]{2,1,0:T(8,128)(2,1)} %get-tuple-element.74.x, bf16[8,3,256,512]{3,2,1,0:T(8,128)(2,1)} %put_together.4.w, f32[3,512,128]{2,1,0:T(8,128)} %get-tuple-element.168.table), custom_call_target="tpu_custom_call" | custom-call | flops 8099999744 | bytes 27000000 | tf_op jit(solution)/shard_map/project/pallas_call | solution.py:316
  95.6 24.6 %all_to_all.30.mine = bf16[8,3,256,128]{3,2,1,0:T(8,128)(2,1)S(1)} all-to-all(bf16[8,3,256,128]{3,2,1,0:T(8,128)(2,1)} %project.1), channel_id=1, replica_groups=mesh['dp'=8,'stream'=4] {'dp'}, dimensions={0} | all-to-all | bytes 3145728 | tf_op jit(solution)/shard_map/all_to_all | solution.py:966
  124.1 11.7 %collective-permute-done.10.refs_3_ = bf16[128,2048]{1,0:T(8,128)(2,1)} collective-permute-done((bf16[128,2048]{1,0:T(8,128)(2,1)S(1)}, bf16[128,2048]{1,0:T(8,128)(2,1)}, u32[]{:S(2)}, u32[]{:S(2)}) %collective-permute-start.10) | collective-permute-done | bytes 524320 | tf_op jit(solution)/shard_map/ppermute | solution.py:77
  136.3 19.0 %attend.1 = (bf16[8,256,128]{2,1,0:T(8,128)(2,1)}, f32[8,256,128]{2,1,0:T(8,128)}, f32[8,256,1]{2,1,0:T(8,128)}) custom-call(s32[8]{0:T(128)} %subtract_maximum_fusion.first, s32[1]{0:T(128)} %bitcast.1.part, bf16[8,3,256,128]{3,2,1,0:T(8,128)(2,1)} %copy-done.7, bf16[8,2,256,128]{3,2,1,0:T(8,128)(2,1)} %collective-permute-done.9.theirs), custom_call_target="tpu_custom_call" | custom-call | flops 14400000000 | bytes 48000000 | tf_op jit(solution)/shard_map/attend/pallas_call | solution.py:375
  157.3 3.6 collective-permute-start.12
  162.9 15.6 %collective-permute-done.25.refs_2_ = bf16[2048,256]{1,0:T(8,128)(2,1)S(1)} collective-permute-done((bf16[2048,256]{1,0:T(8,128)(2,1)}, bf16[2048,256]{1,0:T(8,128)(2,1)S(1)}, u32[]{:S(2)}, u32[]{:S(2)}) %collective-permute-start.25) | collective-permute-done | bytes 1048608 | tf_op jit(solution)/shard_map/ppermute | solution.py:77
  179.8 6.0 collective-permute-start.20
  186.9 4.2 collective-permute-start.21
  196.2 3.2 slice_bitcast_fusion.1.x_ref
  199.3 3.5 all-to-all-start.1
  204.4 6.5 put_together.5
  211.6 10.1 %hidden_units.1 = (bf16[512,2048]{1,0:T(8,128)(2,1)}, bf16[512,2048]{1,0:T(8,128)(2,1)}) custom-call(bf16[512,2048]{1,0:T(8,128)(2,1)} %slice_bitcast_fusion.1.x_ref, bf16[2048,2048]{1,0:T(8,128)(2,1)} %bitcast.107), custom_call_target="tpu_custom_call" | custom-call | flops 8099999744 | bytes 27000000 | tf_op jit(solution)/shard_map/hidden_units/pallas_call | solution.py:802
  226.4 6.5 put_together.7.wd.refs_1_
  232.9 12.6 %merge_branches.1 = bf16[4,512,512]{2,1,0:T(8,128)(2,1)} custom-call(bf16[512,512]{1,0:T(8,128)(2,1)} %bitcast.98, bf16[512,2048]{1,0:T(8,128)(2,1)} %get-tuple-element.83.h, bf16[8,512,256]{2,1,0:T(8,128)(2,1)} %put_together.6.wm.refs_1_, bf16[8,2048,256]{2,1,0:T(8,128)(2,1)} %put_together.7.wd.refs_1_, f32[512,2048]{1,0:T(8,128)} %get-tuple-element.86.st, ...), custom_call_target="tpu_custom_call" | custom-call | flops 11699999744 | bytes 39000000 | tf_op jit(solution)/shard_map/merge_branches/pallas_call | solution.py:830
  245.5 54.8 %all_to_all.31 = bf16[4,512,512]{2,1,0:T(8,128)(2,1)S(1)} all-to-all(bf16[4,512,512]{2,1,0:T(8,128)(2,1)} %merge_branches.1), channel_id=1, replica_groups=mesh['dp'=8,'stream'=4] {'stream'}, dimensions={0} | all-to-all | bytes 4194304 | tf_op jit(solution)/shard_map/all_to_all | solution.py:990
  301.9 43.5 %all-gather.8.cloned.1.call-done = bf16[512,2048]{1,0:T(8,128)(2,1)} async-done(((bf16[512,512]{1,0:T(8,128)(2,1)}), bf16[512,2048]{1,0:T(8,128)(2,1)}) %all-gather.8.cloned.1.call-update) | async-done | bytes 2097168 | tf_op jit(solution)/shard_map/all_gather | solution.py:992
  351.7 6.9 convolution_convert_fusion.1
  359.3 3.2 slice_bitcast_fusion.u
  362.4 14.3 %back_through.3 = bf16[512,2048]{1,0:T(8,128)(2,1)} custom-call(bf16[512,2048]{1,0:T(8,128)(2,1)} %copy-done.36, bf16[8,2048,256]{2,1,0:T(8,128)(2,1)} %put_together.7.wd.refs_1_, bf16[512,2048]{1,0:T(8,128)(2,1)} %get-tuple-element.87.refs_2_), custom_call_target="tpu_custom_call" | custom-call | flops 11699999744 | bytes 39000000 | tf_op jit(solution)/shard_map/back_through/pallas_call | solution.py:885
  376.7 7.3 back_through.2
  386.1 4.0 all-to-all-start.3
  390.3 9.8 %fusion.37.g = f32[512,2048]{1,0:T(8,128)} fusion(bf16[512,2048]{1,0:T(8,128)(2,1)S(1)} %copy-done.39, bf16[2048,2048]{1,0:T(8,128)(2,1)} %bitcast.108), kind=kOutput, calls=%fused_computation.99 | convolution fusion | flops 4294967296 | bytes 14680064 | tf_op jit(solution)/shard_map/dot_general | solution.py:72
  400.1 6.4 last_back.1
  409.4 25.2 %attend_back.1 = (bf16[8,3,256,128]{3,2,1,0:T(8,128)(2,1)}, bf16[8,2,256,128]{3,2,1,0:T(8,128)(2,1)}) custom-call(s32[8]{0:T(128)} %subtract_maximum_fusion.first, s32[1]{0:T(128)} %bitcast.1.part, bf16[8,3,256,128]{3,2,1,0:T(8,128)(2,1)} %copy-done.7, bf16[8,2,256,128]{3,2,1,0:T(8,128)(2,1)} %collective-permute-done.9.theirs, ...), custom_call_target="tpu_custom_call" | custom-call | flops 19800000512 | bytes 66000000 | tf_op jit(solution)/shard_map/attend_back/pallas_call | solution.py:449
  434.6 4.4 collective-permute-start.33
  444.3 9.8 %collective-permute-done.34.refs_5_ = bf16[512,2048]{1,0:T(8,128)(2,1)S(1)} collective-permute-done((bf16[512,2048]{1,0:T(8,128)(2,1)}, bf16[512,2048]{1,0:T(8,128)(2,1)S(1)}, u32[]{:S(2)}, u32[]{:S(2)}) %collective-permute-start.34) | collective-permute-done | bytes 2097184 | tf_op jit(solution)/shard_map/ppermute | solution.py:81
  458.3 8.4 %convolution_convert_fusion = bf16[2048,2048]{1,0:T(8,128)(2,1)} fusion(bf16[512,2048]{1,0:T(8,128)(2,1)S(1)} %copy-done.40, bf16[4,512,2048]{2,1,0:T(8,128)(2,1)} %get-tuple-element.74.x), kind=kOutput, calls=%fused_computation | convolution fusion | flops 4299161600 | bytes 12582912 | tf_op jit(solution)/shard_map/dot_general | solution.py:68
  466.7 4.5 all-to-all-start.4
  471.5 3.7 add_convert_fusion
  475.2 2.7 convert_element_type.152
  477.9 20.0 %all-to-all-done.4.part = bf16[8,3,256,128]{3,2,1,0:T(8,128)(2,1)} async-done(((bf16[8,3,256,128]{3,2,1,0:T(8,128)(2,1)}), bf16[8,3,256,128]{3,2,1,0:T(8,128)(2,1)}, u32[]{:S(2)}, u32[]{:S(2)}) %all-to-all-start.4) | async-done | bytes 1572896 | tf_op jit(solution)/shard_map/all_to_all | solution.py:1039
  497.8 17.1 %heads_back.1 = (bf16[3,128,2048]{2,1,0:T(8,128)(2,1)}, bf16[3,128,2048]{2,1,0:T(8,128)(2,1)}, bf16[3,128,2048]{2,1,0:T(8,128)(2,1)}, bf16[3,64,2048]{2,1,0:T(8,...) custom-call(bf16[8,3,256,128]{3,2,1,0:T(8,128)(2,1)} %all-to-all-don, ...), custom_call_target="tpu_custom_call" | custom-call | flops 2700000000 | bytes 9000000 | tf_op jit(solution)/shard_map/heads_back/pallas_call | solution.py:521
  514.9 5.4 collective-permute-start.35
  523.6 10.4 %mixing_back.3 = f32[4,256,8]{2,1,0:T(8,128)} custom-call(bf16[3,512,2048]{2,1,0:T(8,128)(2,1)} %get-tuple-element.102.first, bf16[512,2048]{1,0:T(8,128)(2,1)} %get-tuple-element.90.last.refs_3_.refs_4_, bf16[8,512,2048]{2,1,0:T(8,128)(2,1)} %hist.2), custom_call_target="tpu_custom_call" | custom-call | flops 360000000 | bytes 1200000 | tf_op jit(solution)/shard_map/mixing_back/pallas_call | solution.py:615
  534.0 9.7 %mixing_back.2 = f32[4,256,8]{2,1,0:T(8,128)} custom-call(bf16[3,512,2048]{2,1,0:T(8,128)(2,1)} %get-tuple-element.102.first, bf16[512,2048]{1,0:T(8,128)(2,1)} %get-tuple-element.90.last.refs_3_.refs_4_, bf16[8,512,2048]{2,1,0:T(8,128)(2,1)} %hist.2), custom_call_target="tpu_custom_call" | custom-call | flops 360000000 | bytes 1200000 | tf_op jit(solution)/shard_map/mixing_back/pallas_call | solution.py:615
  543.7 10.6 %collective-permute-done.35.refs_2_ = bf16[3,128,2048]{2,1,0:T(8,128)(2,1)} collective-permute-done((bf16[3,128,2048]{2,1,0:T(8,128)(2,1)}, bf16[3,128,2048]{2,1,0:T(8,128)(2,1)}, u32[]{:S(2)}, u32[]{:S(2)}) %collective-permute-start.35) | collective-permute-done | bytes 1572896 | tf_op jit(solution)/shard_map/ppermute | solution.py:81
  554.3 3.7 add_convert_fusion.3
  559.8 7.2 collective-permute-start.38
  567.1 20.9 %collective-permute-done.40.refs_2_ = bf16[3,128,2048]{2,1,0:T(8,128)(2,1)} collective-permute-done((bf16[3,128,2048]{2,1,0:T(8,128)(2,1)}, bf16[3,128,2048]{2,1,0:T(8,128)(2,1)}, u32[]{:S(2)}, u32[]{:S(2)}) %collective-permute-start.40) | collective-permute-done | bytes 1572896 | tf_op jit(solution)/shard_map/ppermute | solution.py:81
  588.0 3.7 add_convert_fusion.2
  595.9 4.7 mix_inward.5
  600.6 17.4 %collective-permute-done.38.refs_2_ = bf16[3,128,2048]{2,1,0:T(8,128)(2,1)} collective-permute-done((bf16[3,128,2048]{2,1,0:T(8,128)(2,1)}, bf16[3,128,2048]{2,1,0:T(8,128)(2,1)}, u32[]{:S(2)}, u32[]{:S(2)}) %collective-permute-start.38) | collective-permute-done | bytes 1572896 | tf_op jit(solution)/shard_map/ppermute | solution.py:81
  624.0 5.8 all-to-all-start.5
  629.7 4.9 collective-permute-start.43
  634.6 3.9 add_convert_fusion.1
  639.7 3.8 collective-permute-done.39.refs_7_
  643.5 5.9 mix_final.5
  652.6 4.1 mix_inward.6
  666.6 12.5 %collective-permute-done.44.refs_7_ = bf16[2,128,2048]{2,1,0:T(8,128)(2,1)} collective-permute-done((bf16[2,128,2048]{2,1,0:T(8,128)(2,1)}, bf16[2,128,2048]{2,1,0:T(8,128)(2,1)}, u32[]{:S(2)}, u32[]{:S(2)}) %collective-permute-start.44) | collective-permute-done | bytes 1048608 | tf_op jit(solution)/shard_map/ppermute | solution.py:81
  679.1 5.8 mix_final.6
  686.9 4.2 mix_inward.9
  692.6 17.8 %all-gather.2 = f32[4096,45]{0,1:T(8,128)S(1)} all-gather(f32[512,45]{0,1:T(8,128)S(1)} %pad_maximum_fusion.3), channel_id=5, replica_groups=mesh['dp'=8,'stream'=4] {'dp'}, dimensions={0}, use_global_device_ids=true | all-gather | bytes 829440 | tf_op jit(solution)/shard_map/all_gather | solution.py:1082
  711.0 2.8 mix_inward.8
  716.0 2.8 mix_inward.7
  724.4 2.8 convert_element_type.172
  728.3 5.8 mix_final.7
  736.6 3.6 mix_final.8
  742.4 3.6 mix_final.9
  (280 shorter events, 110.1 us)
Async XLA Ops:
  7.2 214.5 %all-gather.6.cloned.1.call-start = ((), (), s32[]{:S(2)}) async-start(), calls=%async_computation.10 | async-start | bytes 2621440 | tf_op jit(solution)/shard_map/all_gather | solution.py:958
  19.4 30.1 %collective-permute-start = (bf16[3,256,512]{2,1,0:T(8,128)(2,1)}, bf16[3,256,512]{2,1,0:T(8,128)(2,1)S(1)}, u32[]{:S(2)}, u32[]{:S(2)}) collective-permute-start(bf16[3,256,512]{2,1,0:T(8,128)(2,1)} %refs_0_), channel_id=1, source_target_pairs={{0,8},{4,12},{8,0},{12,4},{16,24},{20,28},{24,16},{28,20},{1,9},{5... | collective-permute-start | bytes 2359304 | tf_op jit(solution)/shard_map/ppermute | solution.py:77
  20.2 32.7 %collective-permute-start.1 = (bf16[3,256,512]{2,1,0:T(8,128)(2,1)}, bf16[3,256,512]{2,1,0:T(8,128)(2,1)}, u32[]{:S(2)}, u32[]{:S(2)}) collective-permute-start(bf16[3,256,512]{2,1,0:T(8,128)(2,1)} %refs_0_), channel_id=1, source_target_pairs={{0,16},{4,20},{8,24},{12,28},{16,0},{20,4},{24,8},{28,12},{1,17},{... | collective-permute-start | bytes 2359304 | tf_op jit(solution)/shard_map/ppermute | solution.py:77
  20.7 36.0 %collective-permute-start.2 = (bf16[3,256,512]{2,1,0:T(8,128)(2,1)}, bf16[3,256,512]{2,1,0:T(8,128)(2,1)}, u32[]{:S(2)}, u32[]{:S(2)}) collective-permute-start(bf16[3,256,512]{2,1,0:T(8,128)(2,1)} %refs_0_), channel_id=1, source_target_pairs={{0,24},{4,28},{8,16},{12,20},{16,8},{20,12},{24,0},{28,4},{1,25},{... | collective-permute-start | bytes 2359304 | tf_op jit(solution)/shard_map/ppermute | solution.py:77
  22.9 34.4 %collective-permute-start.5 = (bf16[3,256,512]{2,1,0:T(8,128)(2,1)}, bf16[3,256,512]{2,1,0:T(8,128)(2,1)}, u32[]{:S(2)}, u32[]{:S(2)}) collective-permute-start(bf16[3,256,512]{2,1,0:T(8,128)(2,1)} %refs_0_), channel_id=1, source_target_pairs={{0,4},{4,0},{8,12},{12,8},{16,20},{20,16},{24,28},{28,24},{1,5},{5... | collective-permute-start | bytes 2359304 | tf_op jit(solution)/shard_map/ppermute | solution.py:77
  44.0 257.8 %copy-start.12 = (f32[4,512,62]{1,0,2:T(4,128)}, f32[4,512,62]{1,0,2:T(4,128)S(1)}, u32[]{:S(2)}) copy-start(f32[4,512,62]{1,0,2:T(4,128)S(1)} %reshape.497) | copy-start | bytes 1523716
  52.9 32.6 %collective-permute-start.3 = (bf16[256,2048]{1,0:T(8,128)(2,1)}, bf16[256,2048]{1,0:T(8,128)(2,1)S(1)}, u32[]{:S(2)}, u32[]{:S(2)}) collective-permute-start(bf16[256,2048]{1,0:T(8,128)(2,1)} %refs_0_.1), channel_id=1, source_target_pairs={{0,8},{4,12},{8,0},{12,4},{16,24},{20,28},{24,16},{28,20},{1,9},{5... | collective-permute-start | bytes 3145736 | tf_op jit(solution)/shard_map/ppermute | solution.py:77
  56.7 28.8 %collective-permute-start.4 = (bf16[256,2048]{1,0:T(8,128)(2,1)}, bf16[256,2048]{1,0:T(8,128)(2,1)S(1)}, u32[]{:S(2)}, u32[]{:S(2)}) collective-permute-start(bf16[256,2048]{1,0:T(8,128)(2,1)} %refs_0_.1), channel_id=1, source_target_pairs={{0,16},{4,20},{8,24},{12,28},{16,0},{20,4},{24,8},{28,12},{1,17},{... | collective-permute-start | bytes 3145736 | tf_op jit(solution)/shard_map/ppermute | solution.py:77
  56.7 23.2 %collective-permute-start.6 = (bf16[3,256,512]{2,1,0:T(8,128)(2,1)}, bf16[3,256,512]{2,1,0:T(8,128)(2,1)}, u32[]{:S(2)}, u32[]{:S(2)}) collective-permute-start(bf16[3,256,512]{2,1,0:T(8,128)(2,1)} %copy-done.31), channel_id=1, source_target_pairs={{0,4},{4,0},{8,12},{12,8},{16,20},{20,16},{24,28},{28,24},{1,5},{5... | collective-permute-start | bytes 2359304 | tf_op jit(solution)/shard_map/ppermute | solution.py:77
  56.7 23.2 %collective-permute-start.7 = (bf16[3,256,512]{2,1,0:T(8,128)(2,1)}, bf16[3,256,512]{2,1,0:T(8,128)(2,1)}, u32[]{:S(2)}, u32[]{:S(2)}) collective-permute-start(bf16[3,256,512]{2,1,0:T(8,128)(2,1)} %collective-permute-done.1.refs_2_), channel_id=1, source_target_pairs={{0,4},{4,0},{8,12},{12,8},{16,20},{20,16},{24,28},{28,24},{1,5},{5... | collective-permute-start | bytes 2359304 | tf_op jit(solution)/shard_map/ppermute | solution.py:77
  57.2 22.7 %collective-permute-start.8 = (bf16[3,256,512]{2,1,0:T(8,128)(2,1)}, bf16[3,256,512]{2,1,0:T(8,128)(2,1)}, u32[]{:S(2)}, u32[]{:S(2)}) collective-permute-start(bf16[3,256,512]{2,1,0:T(8,128)(2,1)} %collective-permute-done.2.refs_3_), channel_id=1, source_target_pairs={{0,4},{4,0},{8,12},{12,8},{16,20},{20,16},{24,28},{28,24},{1,5},{5... | collective-permute-start | bytes 2359304 | tf_op jit(solution)/shard_map/ppermute | solution.py:77
  121.3 15.1 %collective-permute-start.9 = (bf16[8,2,256,128]{3,2,1,0:T(8,128)(2,1)}, bf16[8,2,256,128]{3,2,1,0:T(8,128)(2,1)}, u32[]{:S(2)}, u32[]{:S(2)}) collective-permute-start(bf16[8,2,256,128]{3,2,1,0:T(8,128)(2,1)} %slice.125), channel_id=1, source_target_pairs={{0,4},{4,0},{8,12},{12,8},{16,20},{20,16},{24,28},{28,24},{1,5},{5... | collective-permute-start | bytes 3145736 | tf_op jit(solution)/shard_map/ppermute | solution.py:77
  121.3 14.5 %collective-permute-start.10 = (bf16[128,2048]{1,0:T(8,128)(2,1)S(1)}, bf16[128,2048]{1,0:T(8,128)(2,1)}, u32[]{:S(2)}, u32[]{:S(2)}) collective-permute-start(bf16[128,2048]{1,0:T(8,128)(2,1)S(1)} %slice.100), channel_id=1, source_target_pairs={{0,8},{4,12},{8,0},{12,4},{16,24},{20,28},{24,16},{28,20},{1,9},{5... | collective-permute-start | bytes 1572872 | tf_op jit(solution)/shard_map/ppermute | solution.py:77
  122.3 14.0 %collective-permute-start.11 = (bf16[128,2048]{1,0:T(8,128)(2,1)S(1)}, bf16[128,2048]{1,0:T(8,128)(2,1)}, u32[]{:S(2)}, u32[]{:S(2)}) collective-permute-start(bf16[128,2048]{1,0:T(8,128)(2,1)S(1)} %slice.101), channel_id=1, source_target_pairs={{0,16},{4,20},{8,24},{12,28},{16,0},{20,4},{24,8},{28,12},{1,17},{... | collective-permute-start | bytes 1572872 | tf_op jit(solution)/shard_map/ppermute | solution.py:77
  123.5 37.4 %collective-permute-start.13 = (bf16[256,2048]{1,0:T(8,128)(2,1)}, bf16[256,2048]{1,0:T(8,128)(2,1)}, u32[]{:S(2)}, u32[]{:S(2)}) collective-permute-start(bf16[256,2048]{1,0:T(8,128)(2,1)} %copy-done.18), channel_id=1, source_target_pairs={{0,4},{4,0},{8,12},{12,8},{16,20},{20,16},{24,28},{28,24},{1,5},{5... | collective-permute-start | bytes 3145736 | tf_op jit(solution)/shard_map/ppermute | solution.py:77
  123.6 38.2 %collective-permute-start.14 = (bf16[256,2048]{1,0:T(8,128)(2,1)}, bf16[256,2048]{1,0:T(8,128)(2,1)}, u32[]{:S(2)}, u32[]{:S(2)}) collective-permute-start(bf16[256,2048]{1,0:T(8,128)(2,1)} %copy-done.20), channel_id=1, source_target_pairs={{0,4},{4,0},{8,12},{12,8},{16,20},{20,16},{24,28},{28,24},{1,5},{5... | collective-permute-start | bytes 3145736 | tf_op jit(solution)/shard_map/ppermute | solution.py:77
  135.8 20.4 %collective-permute-start.15 = (bf16[128,2048]{1,0:T(8,128)(2,1)}, bf16[128,2048]{1,0:T(8,128)(2,1)S(1)}, u32[]{:S(2)}, u32[]{:S(2)}) collective-permute-start(bf16[128,2048]{1,0:T(8,128)(2,1)} %collective-permute-done.10.refs_3_), channel_id=1, source_target_pairs={{0,4},{4,0},{8,12},{12,8},{16,20},{20,16},{24,28},{28,24},{1,5},{5... | collective-permute-start | bytes 1572872 | tf_op jit(solution)/shard_map/ppermute | solution.py:77
  136.2 21.1 %collective-permute-start.16 = (bf16[128,2048]{1,0:T(8,128)(2,1)}, bf16[128,2048]{1,0:T(8,128)(2,1)}, u32[]{:S(2)}, u32[]{:S(2)}) collective-permute-start(bf16[128,2048]{1,0:T(8,128)(2,1)} %collective-permute-done.11.refs_4_), channel_id=1, source_target_pairs={{0,4},{4,0},{8,12},{12,8},{16,20},{20,16},{24,28},{28,24},{1,5},{5... | collective-permute-start | bytes 1572872 | tf_op jit(solution)/shard_map/ppermute | solution.py:77
  155.4 23.2 %collective-permute-start.25 = (bf16[2048,256]{1,0:T(8,128)(2,1)}, bf16[2048,256]{1,0:T(8,128)(2,1)S(1)}, u32[]{:S(2)}, u32[]{:S(2)}) collective-permute-start(bf16[2048,256]{1,0:T(8,128)(2,1)} %refs_0_.3), channel_id=1, source_target_pairs={{0,16},{4,20},{8,24},{12,28},{16,0},{20,4},{24,8},{28,12},{1,17},{... | collective-permute-start | bytes 3145736 | tf_op jit(solution)/shard_map/ppermute | solution.py:77
  156.2 48.2 %copy-start.32 = (bf16[128,2048]{1,0:T(8,128)(2,1)}, bf16[128,2048]{1,0:T(8,128)(2,1)S(1)}, u32[]{:S(2)}) copy-start(bf16[128,2048]{1,0:T(8,128)(2,1)S(1)} %collective-permute-done.15.refs_8_) | copy-start | bytes 1572868
  156.2 23.6 %collective-permute-start.24 = (bf16[2048,256]{1,0:T(8,128)(2,1)}, bf16[2048,256]{1,0:T(8,128)(2,1)S(1)}, u32[]{:S(2)}, u32[]{:S(2)}) collective-permute-start(bf16[2048,256]{1,0:T(8,128)(2,1)} %refs_0_.3), channel_id=1, source_target_pairs={{0,8},{4,12},{8,0},{12,4},{16,24},{20,28},{24,16},{28,20},{1,9},{5... | collective-permute-start | bytes 3145736 | tf_op jit(solution)/shard_map/ppermute | solution.py:77
  157.3 37.0 %collective-permute-start.12 = (bf16[256,2048]{1,0:T(8,128)(2,1)}, bf16[256,2048]{1,0:T(8,128)(2,1)}, u32[]{:S(2)}, u32[]{:S(2)}) collective-permute-start(bf16[256,2048]{1,0:T(8,128)(2,1)} %refs_0_.1), channel_id=1, source_target_pairs={{0,4},{4,0},{8,12},{12,8},{16,20},{20,16},{24,28},{28,24},{1,5},{5... | collective-permute-start | bytes 3145736 | tf_op jit(solution)/shard_map/ppermute | solution.py:77
  160.9 25.9 %collective-permute-start.17 = (bf16[512,256]{1,0:T(8,128)(2,1)}, bf16[512,256]{1,0:T(8,128)(2,1)}, u32[]{:S(2)}, u32[]{:S(2)}) collective-permute-start(bf16[512,256]{1,0:T(8,128)(2,1)} %refs_0_.2), channel_id=1, source_target_pairs={{0,8},{4,12},{8,0},{12,4},{16,24},{20,28},{24,16},{28,20},{1,9},{5... | collective-permute-start | bytes 786440 | tf_op jit(solution)/shard_map/ppermute | solution.py:77
  161.8 29.3 %collective-permute-start.18 = (bf16[512,256]{1,0:T(8,128)(2,1)}, bf16[512,256]{1,0:T(8,128)(2,1)}, u32[]{:S(2)}, u32[]{:S(2)}) collective-permute-start(bf16[512,256]{1,0:T(8,128)(2,1)} %refs_0_.2), channel_id=1, source_target_pairs={{0,16},{4,20},{8,24},{12,28},{16,0},{20,4},{24,8},{28,12},{1,17},{... | collective-permute-start | bytes 786440 | tf_op jit(solution)/shard_map/ppermute | solution.py:77
  178.5 13.1 %collective-permute-start.19 = (bf16[512,256]{1,0:T(8,128)(2,1)}, bf16[512,256]{1,0:T(8,128)(2,1)}, u32[]{:S(2)}, u32[]{:S(2)}) collective-permute-start(bf16[512,256]{1,0:T(8,128)(2,1)} %refs_0_.2), channel_id=1, source_target_pairs={{0,24},{4,28},{8,16},{12,20},{16,8},{20,12},{24,0},{28,4},{1,25},{... | collective-permute-start | bytes 786440 | tf_op jit(solution)/shard_map/ppermute | solution.py:77
  179.8 15.9 %collective-permute-start.20 = (bf16[512,256]{1,0:T(8,128)(2,1)}, bf16[512,256]{1,0:T(8,128)(2,1)}, u32[]{:S(2)}, u32[]{:S(2)}) collective-permute-start(bf16[512,256]{1,0:T(8,128)(2,1)} %refs_0_.2), channel_id=1, source_target_pairs={{0,4},{4,0},{8,12},{12,8},{16,20},{20,16},{24,28},{28,24},{1,5},{5... | collective-permute-start | bytes 786440 | tf_op jit(solution)/shard_map/ppermute | solution.py:77
  186.9 16.5 %collective-permute-start.21 = (bf16[512,256]{1,0:T(8,128)(2,1)}, bf16[512,256]{1,0:T(8,128)(2,1)}, u32[]{:S(2)}, u32[]{:S(2)}) collective-permute-start(bf16[512,256]{1,0:T(8,128)(2,1)} %collective-permute-done.17.refs_1_), channel_id=1, source_target_pairs={{0,4},{4,0},{8,12},{12,8},{16,20},{20,16},{24,28},{28,24},{1,5},{5... | collective-permute-start | bytes 786440 | tf_op jit(solution)/shard_map/ppermute | solution.py:77
  191.1 12.7 %collective-permute-start.22 = (bf16[512,256]{1,0:T(8,128)(2,1)}, bf16[512,256]{1,0:T(8,128)(2,1)}, u32[]{:S(2)}, u32[]{:S(2)}) collective-permute-start(bf16[512,256]{1,0:T(8,128)(2,1)} %collective-permute-done.18.refs_2_), channel_id=1, source_target_pairs={{0,4},{4,0},{8,12},{12,8},{16,20},{20,16},{24,28},{28,24},{1,5},{5... | collective-permute-start | bytes 786440 | tf_op jit(solution)/shard_map/ppermute | solution.py:77
  191.6 12.4 %collective-permute-start.23 = (bf16[512,256]{1,0:T(8,128)(2,1)}, bf16[512,256]{1,0:T(8,128)(2,1)}, u32[]{:S(2)}, u32[]{:S(2)}) collective-permute-start(bf16[512,256]{1,0:T(8,128)(2,1)} %collective-permute-done.19.refs_3_), channel_id=1, source_target_pairs={{0,4},{4,0},{8,12},{12,8},{16,20},{20,16},{24,28},{28,24},{1,5},{5... | collective-permute-start | bytes 786440 | tf_op jit(solution)/shard_map/ppermute | solution.py:77
  194.2 16.6 %collective-permute-start.26 = (bf16[1024,256]{1,0:T(8,128)(2,1)S(1)}, bf16[1024,256]{1,0:T(8,128)(2,1)S(1)}, u32[]{:S(2)}, u32[]{:S(2)}) collective-permute-start(bf16[1024,256]{1,0:T(8,128)(2,1)S(1)} %slice.126), channel_id=1, source_target_pairs={{0,8},{4,12},{8,0},{12,4},{16,24},{20,28},{24,16},{28,20},{1,9},{5... | collective-permute-start | bytes 1572872 | tf_op jit(solution)/shard_map/ppermute | solution.py:77
  195.6 16.0 %collective-permute-start.27 = (bf16[1024,256]{1,0:T(8,128)(2,1)S(1)}, bf16[1024,256]{1,0:T(8,128)(2,1)}, u32[]{:S(2)}, u32[]{:S(2)}) collective-permute-start(bf16[1024,256]{1,0:T(8,128)(2,1)S(1)} %slice.127), channel_id=1, source_target_pairs={{0,16},{4,20},{8,24},{12,28},{16,0},{20,4},{24,8},{28,12},{1,17},{... | collective-permute-start | bytes 1572872 | tf_op jit(solution)/shard_map/ppermute | solution.py:77
  199.3 22.4 %all-to-all-start.1 = ((bf16[8,256,128]{2,1,0:T(8,128)(2,1)}), bf16[8,256,128]{2,1,0:T(8,128)(2,1)S(1)}, u32[]{:S(2)}, u32[]{:S(2)}) async-start(bf16[8,256,128]{2,1,0:T(8,128)(2,1)} %get-tuple-element.75), calls=%async_computation.1 | async-start | bytes 1048576 | tf_op jit(solution)/shard_map/all_to_all | solution.py:973
  202.8 142.6 %all-gather.8.cloned.1.call-start = ((), (), s32[]{:S(2)}) async-start(), calls=%async_computation.11 | async-start | bytes 2621440 | tf_op jit(solution)/shard_map/all_gather | solution.py:992
  203.4 22.0 %collective-permute-start.28 = (bf16[2048,256]{1,0:T(8,128)(2,1)}, bf16[2048,256]{1,0:T(8,128)(2,1)}, u32[]{:S(2)}, u32[]{:S(2)}) collective-permute-start(bf16[2048,256]{1,0:T(8,128)(2,1)} %refs_0_.3), channel_id=1, source_target_pairs={{0,4},{4,0},{8,12},{12,8},{16,20},{20,16},{24,28},{28,24},{1,5},{5... | collective-permute-start | bytes 3145736 | tf_op jit(solution)/shard_map/ppermute | solution.py:77
  203.8 21.6 %collective-permute-start.29 = (bf16[2048,256]{1,0:T(8,128)(2,1)}, bf16[2048,256]{1,0:T(8,128)(2,1)}, u32[]{:S(2)}, u32[]{:S(2)}) collective-permute-start(bf16[2048,256]{1,0:T(8,128)(2,1)} %copy-done.23), channel_id=1, source_target_pairs={{0,4},{4,0},{8,12},{12,8},{16,20},{20,16},{24,28},{28,24},{1,5},{5... | collective-permute-start | bytes 3145736 | tf_op jit(solution)/shard_map/ppermute | solution.py:77
  204.0 21.5 %collective-permute-start.30 = (bf16[2048,256]{1,0:T(8,128)(2,1)}, bf16[2048,256]{1,0:T(8,128)(2,1)}, u32[]{:S(2)}, u32[]{:S(2)}) collective-permute-start(bf16[2048,256]{1,0:T(8,128)(2,1)} %copy-done.22), channel_id=1, source_target_pairs={{0,4},{4,0},{8,12},{12,8},{16,20},{20,16},{24,28},{28,24},{1,5},{5... | collective-permute-start | bytes 3145736 | tf_op jit(solution)/shard_map/ppermute | solution.py:77
  210.9 14.5 %collective-permute-start.31 = (bf16[1024,256]{1,0:T(8,128)(2,1)S(1)}, bf16[1024,256]{1,0:T(8,128)(2,1)S(1)}, u32[]{:S(2)}, u32[]{:S(2)}) collective-permute-start(bf16[1024,256]{1,0:T(8,128)(2,1)S(1)} %collective-permute-done.26.refs_3_), channel_id=1, source_target_pairs={{0,4},{4,0},{8,12},{12,8},{16,20},{20,16},{24,28},{28,24},{1,5},{5... | collective-permute-start | bytes 1572872 | tf_op jit(solution)/shard_map/ppermute | solution.py:77
  211.6 13.8 %collective-permute-start.32 = (bf16[1024,256]{1,0:T(8,128)(2,1)}, bf16[1024,256]{1,0:T(8,128)(2,1)S(1)}, u32[]{:S(2)}, u32[]{:S(2)}) collective-permute-start(bf16[1024,256]{1,0:T(8,128)(2,1)} %collective-permute-done.27.refs_4_), channel_id=1, source_target_pairs={{0,4},{4,0},{8,12},{12,8},{16,20},{20,16},{24,28},{28,24},{1,5},{5... | collective-permute-start | bytes 1572872 | tf_op jit(solution)/shard_map/ppermute | solution.py:77
  301.6 173.6 %reduce-scatter.5.cloned.1.call-start = ((), (), s32[]{:S(2)}) async-start(), calls=%async_computation.12 | async-start | bytes 9437184 | tf_op jit(solution)/shard_map/reduce_scatter | solution.py:1018
  347.7 304.1 %copy-start.26 = (f32[512]{0:T(512)}, f32[512]{0:T(512)S(1)}, u32[]{:S(2)}) copy-start(f32[512]{0:T(512)S(1)} %add_rsqrt_fusion) | copy-start | bytes 6148
  386.1 22.5 %all-to-all-start.3 = ((bf16[8,256,128]{2,1,0:T(8,128)(2,1)}), bf16[8,256,128]{2,1,0:T(8,128)(2,1)S(1)}, u32[]{:S(2)}, u32[]{:S(2)}) async-start(bf16[8,256,128]{2,1,0:T(8,128)(2,1)} %bitcast.20), calls=%async_computation.3 | async-start | bytes 1048576 | tf_op jit(solution)/shard_map/all_to_all | solution.py:1029
  390.1 230.3 %reduce-scatter.7.cloned.1.call-start = ((), (), s32[]{:S(2)}) async-start(), calls=%async_computation.13 | async-start | bytes 2359296 | tf_op jit(solution)/shard_map/reduce_scatter | solution.py:1053
  406.5 47.6 %collective-permute-start.34 = (bf16[512,2048]{1,0:T(8,128)(2,1)}, bf16[512,2048]{1,0:T(8,128)(2,1)S(1)}, u32[]{:S(2)}, u32[]{:S(2)}) collective-permute-start(bf16[512,2048]{1,0:T(8,128)(2,1)} %get-tuple-element.90.last.refs_3_.refs_4_), channel_id=1, source_target_pairs={{0,1},{3,2},{4,5},{7,6},{8,9},{11,10},{12,13},{15,14},{16,17},{19,... | collective-permute-start | bytes 6291464 | tf_op jit(solution)/shard_map/ppermute | solution.py:81
  434.6 6.9 collective-permute-start.33
  456.8 267.7 %reduce-scatter.11.cloned.1.call-start = ((), (), s32[]{:S(2)}) async-start(), calls=%async_computation.15 | async-start | bytes 9437184 | tf_op jit(solution)/shard_map/reduce_scatter | solution.py:1055
  466.7 31.1 %all-to-all-start.4 = ((bf16[8,3,256,128]{3,2,1,0:T(8,128)(2,1)}), bf16[8,3,256,128]{3,2,1,0:T(8,128)(2,1)}, u32[]{:S(2)}, u32[]{:S(2)}) async-start(bf16[8,3,256,128]{3,2,1,0:T(8,128)(2,1)} %pad_maximum_fusion), calls=%async_computation.4 | async-start | bytes 3145728 | tf_op jit(solution)/shard_map/all_to_all | solution.py:1039
  471.2 262.9 %reduce-scatter.9.cloned.1.call-start = ((), (), s32[]{:S(2)}) async-start(), calls=%async_computation.14 | async-start | bytes 7077888 | tf_op jit(solution)/shard_map/reduce_scatter | solution.py:1054
  514.9 39.3 %collective-permute-start.35 = (bf16[3,128,2048]{2,1,0:T(8,128)(2,1)}, bf16[3,128,2048]{2,1,0:T(8,128)(2,1)}, u32[]{:S(2)}, u32[]{:S(2)}) collective-permute-start(bf16[3,128,2048]{2,1,0:T(8,128)(2,1)} %get-tuple-element.101.refs_1_), channel_id=1, source_target_pairs={{0,1},{3,2},{4,5},{7,6},{8,9},{11,10},{12,13},{15,14},{16,17},{19,... | collective-permute-start | bytes 4718600 | tf_op jit(solution)/shard_map/ppermute | solution.py:81
  520.4 67.6 %collective-permute-start.40 = (bf16[3,128,2048]{2,1,0:T(8,128)(2,1)}, bf16[3,128,2048]{2,1,0:T(8,128)(2,1)}, u32[]{:S(2)}, u32[]{:S(2)}) collective-permute-start(bf16[3,128,2048]{2,1,0:T(8,128)(2,1)} %get-tuple-element.108.refs_1_), channel_id=1, source_target_pairs={{0,1},{3,2},{4,5},{7,6},{8,9},{11,10},{12,13},{15,14},{16,17},{19,... | collective-permute-start | bytes 4718600 | tf_op jit(solution)/shard_map/ppermute | solution.py:81
  522.8 71.7 %collective-permute-start.37 = (bf16[512,2048]{1,0:T(8,128)(2,1)}, bf16[512,2048]{1,0:T(8,128)(2,1)S(1)}, u32[]{:S(2)}, u32[]{:S(2)}) collective-permute-start(bf16[512,2048]{1,0:T(8,128)(2,1)} %add_convert_fusion), channel_id=1, source_target_pairs={{1,2},{2,1},{5,6},{6,5},{9,10},{10,9},{13,14},{14,13},{17,18},{18,... | collective-permute-start | bytes 6291464 | tf_op jit(solution)/shard_map/ppermute | solution.py:81
  558.0 36.4 %collective-permute-start.36 = (bf16[3,128,2048]{2,1,0:T(8,128)(2,1)}, bf16[3,128,2048]{2,1,0:T(8,128)(2,1)}, u32[]{:S(2)}, u32[]{:S(2)}) collective-permute-start(bf16[3,128,2048]{2,1,0:T(8,128)(2,1)} %add_convert_fusion.3), channel_id=1, source_target_pairs={{1,2},{2,1},{5,6},{6,5},{9,10},{10,9},{13,14},{14,13},{17,18},{18,... | collective-permute-start | bytes 4718600 | tf_op jit(solution)/shard_map/ppermute | solution.py:81
  559.8 58.1 %collective-permute-start.38 = (bf16[3,128,2048]{2,1,0:T(8,128)(2,1)}, bf16[3,128,2048]{2,1,0:T(8,128)(2,1)}, u32[]{:S(2)}, u32[]{:S(2)}) collective-permute-start(bf16[3,128,2048]{2,1,0:T(8,128)(2,1)} %get-tuple-element.105.refs_1_), channel_id=1, source_target_pairs={{0,1},{3,2},{4,5},{7,6},{8,9},{11,10},{12,13},{15,14},{16,17},{19,... | collective-permute-start | bytes 4718600 | tf_op jit(solution)/shard_map/ppermute | solution.py:81
  591.7 57.7 %collective-permute-start.41 = (bf16[3,128,2048]{2,1,0:T(8,128)(2,1)}, bf16[3,128,2048]{2,1,0:T(8,128)(2,1)}, u32[]{:S(2)}, u32[]{:S(2)}) collective-permute-start(bf16[3,128,2048]{2,1,0:T(8,128)(2,1)} %add_convert_fusion.2), channel_id=1, source_target_pairs={{1,2},{2,1},{5,6},{6,5},{9,10},{10,9},{13,14},{14,13},{17,18},{18,... | collective-permute-start | bytes 4718600 | tf_op jit(solution)/shard_map/ppermute | solution.py:81
  618.0 25.5 %collective-permute-start.39 = (bf16[2,128,2048]{2,1,0:T(8,128)(2,1)}, bf16[2,128,2048]{2,1,0:T(8,128)(2,1)}, u32[]{:S(2)}, u32[]{:S(2)}) collective-permute-start(bf16[2,128,2048]{2,1,0:T(8,128)(2,1)} %mix_inward.5), channel_id=1, source_target_pairs={{1,0},{2,3},{5,4},{6,7},{9,8},{10,11},{13,12},{14,15},{17,16},{18,... | collective-permute-start | bytes 3145736 | tf_op jit(solution)/shard_map/ppermute | solution.py:81
  624.0 36.4 %all-to-all-start.5 = ((f32[4,512,16]{1,2,0:T(8,128)}), f32[4,512,16]{1,2,0:T(8,128)S(1)}, u32[]{:S(2)}, u32[]{:S(2)}) async-start(f32[4,512,16]{1,2,0:T(8,128)} %maximum_maximum_fusion), calls=%async_computation.8 | async-start | bytes 262144 | tf_op jit(solution)/shard_map/all_to_all | solution.py:1079
  629.7 27.0 %collective-permute-start.43 = (bf16[3,64,2048]{2,1,0:T(8,128)(2,1)S(1)}, bf16[3,64,2048]{2,1,0:T(8,128)(2,1)}, u32[]{:S(2)}, u32[]{:S(2)}) collective-permute-start(bf16[3,64,2048]{2,1,0:T(8,128)(2,1)S(1)} %copy-done.4), channel_id=1, source_target_pairs={{0,1},{3,2},{4,5},{7,6},{8,9},{11,10},{12,13},{15,14},{16,17},{19,... | collective-permute-start | bytes 2359304 | tf_op jit(solution)/shard_map/ppermute | solution.py:81
  638.6 47.2 %collective-permute-start.49 = (bf16[3,128,2048]{2,1,0:T(8,128)(2,1)}, bf16[3,128,2048]{2,1,0:T(8,128)(2,1)S(1)}, u32[]{:S(2)}, u32[]{:S(2)}) collective-permute-start(bf16[3,128,2048]{2,1,0:T(8,128)(2,1)} %add_convert_fusion.1), channel_id=1, source_target_pairs={{1,2},{2,1},{5,6},{6,5},{9,10},{10,9},{13,14},{14,13},{17,18},{18,... | collective-permute-start | bytes 4718600 | tf_op jit(solution)/shard_map/ppermute | solution.py:81
  649.4 14.9 %collective-permute-start.42 = (bf16[3,64,2048]{2,1,0:T(8,128)(2,1)S(1)}, bf16[3,64,2048]{2,1,0:T(8,128)(2,1)}, u32[]{:S(2)}, u32[]{:S(2)}) collective-permute-start(bf16[3,64,2048]{2,1,0:T(8,128)(2,1)S(1)} %copy-done.3), channel_id=1, source_target_pairs={{0,1},{3,2},{4,5},{7,6},{8,9},{11,10},{12,13},{15,14},{16,17},{19,... | collective-permute-start | bytes 2359304 | tf_op jit(solution)/shard_map/ppermute | solution.py:81
  656.7 22.4 %collective-permute-start.44 = (bf16[2,128,2048]{2,1,0:T(8,128)(2,1)}, bf16[2,128,2048]{2,1,0:T(8,128)(2,1)}, u32[]{:S(2)}, u32[]{:S(2)}) collective-permute-start(bf16[2,128,2048]{2,1,0:T(8,128)(2,1)} %mix_inward.6), channel_id=1, source_target_pairs={{1,0},{2,3},{5,4},{6,7},{9,8},{10,11},{13,12},{14,15},{17,16},{18,... | collective-permute-start | bytes 3145736 | tf_op jit(solution)/shard_map/ppermute | solution.py:81
  662.7 48.3 %collective-permute-start.47 = (bf16[3,64,2048]{2,1,0:T(8,128)(2,1)}, bf16[3,64,2048]{2,1,0:T(8,128)(2,1)}, u32[]{:S(2)}, u32[]{:S(2)}) collective-permute-start(bf16[3,64,2048]{2,1,0:T(8,128)(2,1)} %add_convert_fusion.5), channel_id=1, source_target_pairs={{1,2},{2,1},{5,6},{6,5},{9,10},{10,9},{13,14},{14,13},{17,18},{18,... | collective-permute-start | bytes 2359304 | tf_op jit(solution)/shard_map/ppermute | solution.py:81
  684.9 30.2 %collective-permute-start.45 = (bf16[3,64,2048]{2,1,0:T(8,128)(2,1)}, bf16[3,64,2048]{2,1,0:T(8,128)(2,1)S(1)}, u32[]{:S(2)}, u32[]{:S(2)}) collective-permute-start(bf16[3,64,2048]{2,1,0:T(8,128)(2,1)} %add_convert_fusion.6), channel_id=1, source_target_pairs={{1,2},{2,1},{5,6},{6,5},{9,10},{10,9},{13,14},{14,13},{17,18},{18,... | collective-permute-start | bytes 2359304 | tf_op jit(solution)/shard_map/ppermute | solution.py:81
  691.1 36.1 %collective-permute-start.50 = (bf16[2,128,2048]{2,1,0:T(8,128)(2,1)}, bf16[2,128,2048]{2,1,0:T(8,128)(2,1)S(1)}, u32[]{:S(2)}, u32[]{:S(2)}) collective-permute-start(bf16[2,128,2048]{2,1,0:T(8,128)(2,1)} %mix_inward.9), channel_id=1, source_target_pairs={{1,0},{2,3},{5,4},{6,7},{9,8},{10,11},{13,12},{14,15},{17,16},{18,... | collective-permute-start | bytes 3145736 | tf_op jit(solution)/shard_map/ppermute | solution.py:81
  713.8 22.8 %collective-permute-start.48 = (bf16[2,64,2048]{2,1,0:T(8,128)(2,1)}, bf16[2,64,2048]{2,1,0:T(8,128)(2,1)}, u32[]{:S(2)}, u32[]{:S(2)}) collective-permute-start(bf16[2,64,2048]{2,1,0:T(8,128)(2,1)} %mix_inward.8), channel_id=1, source_target_pairs={{1,0},{2,3},{5,4},{6,7},{9,8},{10,11},{13,12},{14,15},{17,16},{18,... | collective-permute-start | bytes 1572872 | tf_op jit(solution)/shard_map/ppermute | solution.py:81
  718.8 22.8 %collective-permute-start.46 = (bf16[2,64,2048]{2,1,0:T(8,128)(2,1)}, bf16[2,64,2048]{2,1,0:T(8,128)(2,1)S(1)}, u32[]{:S(2)}, u32[]{:S(2)}) collective-permute-start(bf16[2,64,2048]{2,1,0:T(8,128)(2,1)} %mix_inward.7), channel_id=1, source_target_pairs={{1,0},{2,3},{5,4},{6,7},{9,8},{10,11},{13,12},{14,15},{17,16},{18,... | collective-permute-start | bytes 1572872 | tf_op jit(solution)/shard_map/ppermute | solution.py:81
  (39 other events, 321.9 us)
Sparse Core Ops, SparseCore 0:
  123.6 46.6 all-gather.5
  301.7 43.6 all-gather.7
  358.8 75.7 reduce-scatter.4
  456.9 51.3 reduce-scatter.6
  511.6 71.4 reduce-scatter.10
  586.4 61.6 reduce-scatter.8

commit v3 on v1

--- a/solution.py
+++ b/solution.py
@@ -1092,11 +1092,11 @@
 
     def third_hop(i, one, two):
         load = mix_block(spans[i][0], there, pieces[i], last_share, [two], [last_two(i)], None, None)
-        return after(load, extra["both" if i == 0 else "all"]) if i < 2 else load
+        return after(load, extra["both"]) if i == 2 else load
 
     def finish(i, one, two, three):
         if i == 3:
-            three = after(three, grad_heads)
+            three = after(three, grad_heads, extra["all"])
         extra["history"], token = mix_block(
             spans[i][0],
             here,

time: 778 us -> 755 us (0.970)
  waiting for transfers between devices: 206 us -> 180 us
    all_to_all x1, waiting for transfers between devices: 26.9 us -> 0.01 us  [small_sums(): both = jnp.sum(lax.all_to_all(both, 'stream', 0, 0, tiled=True), axis=0)]
    unnamed x110 -> x98, local copies, waits for them, and re-layouts: 20.5 us -> 19.5 us
  transfers between devices with their start and end apart: 61 -> 61, of which waited for: 18 -> 17; matrix products, arithmetic and copies ran while one was open for 12% -> 12% of each run, Pallas kernels for 25% -> 26%
where the time goes in v3:
time: 755 us; the launch traced here: 742 us
  Pallas kernels  223 us (30%)
  waiting for transfers between devices  180 us (24%)
  blocking collectives  121 us (16%)
  starting transfers between devices  81.4 us (11%)
  local copies, waits for them, and re-layouts  47.5 us (6%)
  other arithmetic  40.3 us (5%)
  matrix products  31.8 us (4%)
  between operations  16.1 us (2%)
    ppermute x17, waiting for transfers between devices, line_hop(): return lax.ppermute(shard, 'stream', pairs)  79.2 us
    all_to_all x1, blocking collectives, body(): columns = lax.all_to_all(share, 'stream', 0, 0, tiled=True)  53.3 us
    pallas_call x10, Pallas kernels, mix_block(): pl.pallas_call(kernel, grid=(1,), in_specs=specs, out_specs=out_spec, out...  43.5 us
    all_gather x1, waiting for transfers between devices, body(): block_full = lax.all_gather(block_out, 'stream', axis=1, tiled=True)  42.7 us
    ppermute x17, starting transfers between devices, line_hop(): return lax.ppermute(shard, 'stream', pairs)  38.9 us
    ppermute x34, waiting for transfers between devices, partner(): return lax.ppermute(shard, 'dp', [(i, i ^ bit) for i in range(peers)])  38.5 us
    all_to_all x1, blocking collectives, body(): own = lax.all_to_all(projected, 'dp', 0, 0, tiled=True)  24.4 us
    ppermute x34, starting transfers between devices, partner(): return lax.ppermute(shard, 'dp', [(i, i ^ bit) for i in range(peers)])  23.5 us
  transfers between devices with their start and end apart: 61, of which 17 were waited for; matrix products, arithmetic and copies ran while one was open for 12% of the time, Pallas kernels for 26%

profile of v3, /device:TPU:0, one launch (start us, length us, event | category | flops | bytes accessed | tf_op | source)
XLA Modules:
  0.0 742.1 jit_solution(3775103309573178454)
XLA Ops:
  9.9 9.5 %all-reduce.2 = s32[8]{0:T(128)S(1)} all-reduce(s32[8]{0:T(128)S(1)} %dynamic-update-slice), channel_id=3, replica_groups=mesh['dp'=8,'stream'=4] {'dp'}, use_global_device_ids=true, to_apply=%add.2 | all-reduce | flops 8 | bytes 64
  27.2 16.5 %all-gather.1 = f32[2048,62]{0,1:T(8,128)S(1)} all-gather(f32[512,62]{0,1:T(8,128)S(1)} %concatenate.27), channel_id=4, replica_groups=mesh['dp'=8,'stream'=4] {'stream'}, dimensions={0}, use_global_device_ids=true | all-gather | bytes 634880 | tf_op jit(solution)/shard_map/all_gather | solution.py:938
  49.5 2.6 collective-permute-done.1.refs_2_
  52.1 4.0 collective-permute-start.3
  57.5 22.6 %make_streams.1 = (bf16[4,512,2048]{2,1,0:T(8,128)(2,1)}, bf16[4,512,2048]{2,1,0:T(8,128)(2,1)}, f32[512,4]{1,0:T(8,128)}, f32[512,2048]{1,0:T(8,128)}) custom-call(bf16[8,512,2048]{2,1,0:T(8,128)(2,1)} %hist.2, f32[512,32]{1,0:T(8,128)} %copy.66.mix, f32[4,2048]{1,0:T(4,128)} %get-tuple-element.203.gain, f32[4,2048]{1,0:T(4,128)} %get-tuple-element.202.bias), custom_call_target="tpu_custom_call" | custom-call | flops 19800000512 | bytes 66000000 | tf_op jit(solution)/shard_map/make_streams/pallas_call | solution.py:266
  81.0 5.5 put_together.4.w
  86.5 8.8 %project.1 = bf16[8,3,256,128]{3,2,1,0:T(8,128)(2,1)} custom-call(bf16[4,512,2048]{2,1,0:T(8,128)(2,1)} %get-tuple-element.81.x, bf16[8,3,256,512]{3,2,1,0:T(8,128)(2,1)} %put_together.4.w, f32[3,512,128]{2,1,0:T(8,128)} %get-tuple-element.182.table), custom_call_target="tpu_custom_call" | custom-call | flops 8099999744 | bytes 27000000 | tf_op jit(solution)/shard_map/project/pallas_call | solution.py:316
  95.3 24.4 %all_to_all.30.mine = bf16[8,3,256,128]{3,2,1,0:T(8,128)(2,1)S(1)} all-to-all(bf16[8,3,256,128]{3,2,1,0:T(8,128)(2,1)} %project.1), channel_id=1, replica_groups=mesh['dp'=8,'stream'=4] {'dp'}, dimensions={0} | all-to-all | bytes 3145728 | tf_op jit(solution)/shard_map/all_to_all | solution.py:967
  126.1 16.9 %attend.1 = (bf16[8,256,128]{2,1,0:T(8,128)(2,1)}, f32[8,256,128]{2,1,0:T(8,128)}, f32[8,256,1]{2,1,0:T(8,128)}) custom-call(s32[8]{0:T(128)} %subtract_maximum_fusion.first, s32[1]{0:T(128)} %bitcast.1.part, bf16[8,3,256,128]{3,2,1,0:T(8,128)(2,1)} %copy-done.7, bf16[8,2,256,128]{3,2,1,0:T(8,128)(2,1)} %collective-permute-done.9.theirs), custom_call_target="tpu_custom_call" | custom-call | flops 14400000000 | bytes 48000000 | tf_op jit(solution)/shard_map/attend/pallas_call | solution.py:375
  143.0 15.8 %collective-permute-done.25.refs_2_ = bf16[2048,256]{1,0:T(8,128)(2,1)} collective-permute-done((bf16[2048,256]{1,0:T(8,128)(2,1)}, bf16[2048,256]{1,0:T(8,128)(2,1)}, u32[]{:S(2)}, u32[]{:S(2)}) %collective-permute-start.25) | collective-permute-done | bytes 1048608 | tf_op jit(solution)/shard_map/ppermute | solution.py:77
  168.9 5.9 collective-permute-done.26.refs_3_
  174.7 2.7 collective-permute-done.27.refs_4_
  178.3 3.5 all-to-all-start.1
  184.5 7.1 collective-permute-done.11.refs_4_
  191.6 3.2 slice_bitcast_fusion.1.x_ref
  200.1 6.5 put_together.5
  206.6 10.1 %hidden_units.1 = (bf16[512,2048]{1,0:T(8,128)(2,1)}, bf16[512,2048]{1,0:T(8,128)(2,1)}) custom-call(bf16[512,2048]{1,0:T(8,128)(2,1)} %slice_bitcast_fusion.1.x_ref, bf16[2048,2048]{1,0:T(8,128)(2,1)} %bitcast.107), custom_call_target="tpu_custom_call" | custom-call | flops 8099999744 | bytes 27000000 | tf_op jit(solution)/shard_map/hidden_units/pallas_call | solution.py:802
  217.4 6.5 put_together.7.wd.refs_1_
  223.9 12.6 %merge_branches.1 = bf16[4,512,512]{2,1,0:T(8,128)(2,1)} custom-call(bf16[512,512]{1,0:T(8,128)(2,1)} %bitcast.98, bf16[512,2048]{1,0:T(8,128)(2,1)} %get-tuple-element.90.h, bf16[8,512,256]{2,1,0:T(8,128)(2,1)} %put_together.6.wm.refs_1_, bf16[8,2048,256]{2,1,0:T(8,128)(2,1)} %put_together.7.wd.refs_1_, f32[512,2048]{1,0:T(8,128)} %get-tuple-element.100.st, ...), custom_call_target="tpu_custom_call" | custom-call | flops 11699999744 | bytes 39000000 | tf_op jit(solution)/shard_map/merge_branches/pallas_call | solution.py:830
  236.5 53.3 %all_to_all.31 = bf16[4,512,512]{2,1,0:T(8,128)(2,1)S(1)} all-to-all(bf16[4,512,512]{2,1,0:T(8,128)(2,1)} %merge_branches.1), channel_id=1, replica_groups=mesh['dp'=8,'stream'=4] {'stream'}, dimensions={0} | all-to-all | bytes 4194304 | tf_op jit(solution)/shard_map/all_to_all | solution.py:990
  291.4 42.7 %all-gather.8.cloned.1.call-done = bf16[512,2048]{1,0:T(8,128)(2,1)} async-done(((bf16[512,512]{1,0:T(8,128)(2,1)}), bf16[512,2048]{1,0:T(8,128)(2,1)}) %all-gather.8.cloned.1.call-update) | async-done | bytes 2097168 | tf_op jit(solution)/shard_map/all_gather | solution.py:992
  340.5 6.8 convolution_convert_fusion.1
  347.9 3.2 slice_bitcast_fusion.u
  351.1 14.3 %back_through.3 = bf16[512,2048]{1,0:T(8,128)(2,1)} custom-call(bf16[512,2048]{1,0:T(8,128)(2,1)} %copy-done.37, bf16[8,2048,256]{2,1,0:T(8,128)(2,1)} %put_together.7.wd.refs_1_, bf16[512,2048]{1,0:T(8,128)(2,1)} %get-tuple-element.101.refs_2_), custom_call_target="tpu_custom_call" | custom-call | flops 11699999744 | bytes 39000000 | tf_op jit(solution)/shard_map/back_through/pallas_call | solution.py:885
  365.4 7.2 back_through.2
  374.7 4.0 all-to-all-start.3
  378.9 9.8 %fusion.37.g = f32[512,2048]{1,0:T(8,128)} fusion(bf16[512,2048]{1,0:T(8,128)(2,1)S(1)} %copy-done.40, bf16[2048,2048]{1,0:T(8,128)(2,1)} %bitcast.108), kind=kOutput, calls=%fused_computation.99 | convolution fusion | flops 4294967296 | bytes 14680064 | tf_op jit(solution)/shard_map/dot_general | solution.py:72
  388.7 6.4 last_back.1
  398.0 22.5 %attend_back.1 = (bf16[8,3,256,128]{3,2,1,0:T(8,128)(2,1)}, bf16[8,2,256,128]{3,2,1,0:T(8,128)(2,1)}) custom-call(s32[8]{0:T(128)} %subtract_maximum_fusion.first, s32[1]{0:T(128)} %bitcast.1.part, bf16[8,3,256,128]{3,2,1,0:T(8,128)(2,1)} %copy-done.7, bf16[8,2,256,128]{3,2,1,0:T(8,128)(2,1)} %collective-permute-done.9.theirs, ...), custom_call_target="tpu_custom_call" | custom-call | flops 19800000512 | bytes 66000000 | tf_op jit(solution)/shard_map/attend_back/pallas_call | solution.py:449
  420.5 4.4 collective-permute-start.33
  430.2 12.5 %collective-permute-done.34.refs_5_ = bf16[512,2048]{1,0:T(8,128)(2,1)S(1)} collective-permute-done((bf16[512,2048]{1,0:T(8,128)(2,1)}, bf16[512,2048]{1,0:T(8,128)(2,1)S(1)}, u32[]{:S(2)}, u32[]{:S(2)}) %collective-permute-start.34) | collective-permute-done | bytes 2097184 | tf_op jit(solution)/shard_map/ppermute | solution.py:81
  442.7 2.6 convolution_convert_fusion.2
  446.9 8.4 %convolution_convert_fusion = bf16[2048,2048]{1,0:T(8,128)(2,1)} fusion(bf16[512,2048]{1,0:T(8,128)(2,1)S(1)} %copy-done.41, bf16[4,512,2048]{2,1,0:T(8,128)(2,1)} %get-tuple-element.81.x), kind=kOutput, calls=%fused_computation | convolution fusion | flops 4299161600 | bytes 12582912 | tf_op jit(solution)/shard_map/dot_general | solution.py:68
  455.4 4.5 all-to-all-start.4
  460.1 3.7 add_convert_fusion
  463.8 2.7 convert_element_type.152
  466.5 20.0 %all-to-all-done.4.part = bf16[8,3,256,128]{3,2,1,0:T(8,128)(2,1)} async-done(((bf16[8,3,256,128]{3,2,1,0:T(8,128)(2,1)}), bf16[8,3,256,128]{3,2,1,0:T(8,128)(2,1)}, u32[]{:S(2)}, u32[]{:S(2)}) %all-to-all-start.4) | async-done | bytes 1572896 | tf_op jit(solution)/shard_map/all_to_all | solution.py:1039
  486.5 17.1 %heads_back.1 = (bf16[3,128,2048]{2,1,0:T(8,128)(2,1)}, bf16[3,128,2048]{2,1,0:T(8,128)(2,1)}, bf16[3,128,2048]{2,1,0:T(8,128)(2,1)}, bf16[3,64,2048]{2,1,0:T(8,...) custom-call(bf16[8,3,256,128]{3,2,1,0:T(8,128)(2,1)} %all-to-all-don, ...), custom_call_target="tpu_custom_call" | custom-call | flops 2700000000 | bytes 9000000 | tf_op jit(solution)/shard_map/heads_back/pallas_call | solution.py:521
  503.6 5.5 collective-permute-start.35
  512.3 10.4 %mixing_back.3 = f32[4,256,8]{2,1,0:T(8,128)} custom-call(bf16[3,512,2048]{2,1,0:T(8,128)(2,1)} %get-tuple-element.116.first, bf16[512,2048]{1,0:T(8,128)(2,1)} %get-tuple-element.104.last.refs_3_.refs_4_, bf16[8,512,2048]{2,1,0:T(8,128)(2,1)} %hist.2), custom_call_target="tpu_custom_call" | custom-call | flops 360000000 | bytes 1200000 | tf_op jit(solution)/shard_map/mixing_back/pallas_call | solution.py:615
  522.6 9.7 %mixing_back.2 = f32[4,256,8]{2,1,0:T(8,128)} custom-call(bf16[3,512,2048]{2,1,0:T(8,128)(2,1)} %get-tuple-element.116.first, bf16[512,2048]{1,0:T(8,128)(2,1)} %get-tuple-element.104.last.refs_3_.refs_4_, bf16[8,512,2048]{2,1,0:T(8,128)(2,1)} %hist.2), custom_call_target="tpu_custom_call" | custom-call | flops 360000000 | bytes 1200000 | tf_op jit(solution)/shard_map/mixing_back/pallas_call | solution.py:615
  532.3 10.6 %collective-permute-done.35.refs_2_ = bf16[3,128,2048]{2,1,0:T(8,128)(2,1)} collective-permute-done((bf16[3,128,2048]{2,1,0:T(8,128)(2,1)}, bf16[3,128,2048]{2,1,0:T(8,128)(2,1)}, u32[]{:S(2)}, u32[]{:S(2)}) %collective-permute-start.35) | collective-permute-done | bytes 1572896 | tf_op jit(solution)/shard_map/ppermute | solution.py:81
  542.9 3.7 add_convert_fusion.3
  548.5 7.2 collective-permute-start.38
  555.7 20.9 %collective-permute-done.40.refs_2_ = bf16[3,128,2048]{2,1,0:T(8,128)(2,1)} collective-permute-done((bf16[3,128,2048]{2,1,0:T(8,128)(2,1)}, bf16[3,128,2048]{2,1,0:T(8,128)(2,1)}, u32[]{:S(2)}, u32[]{:S(2)}) %collective-permute-start.40) | collective-permute-done | bytes 1572896 | tf_op jit(solution)/shard_map/ppermute | solution.py:81
  576.7 3.7 add_convert_fusion.2
  584.5 4.7 mix_inward.5
  589.3 17.4 %collective-permute-done.38.refs_2_ = bf16[3,128,2048]{2,1,0:T(8,128)(2,1)} collective-permute-done((bf16[3,128,2048]{2,1,0:T(8,128)(2,1)}, bf16[3,128,2048]{2,1,0:T(8,128)(2,1)}, u32[]{:S(2)}, u32[]{:S(2)}) %collective-permute-start.38) | collective-permute-done | bytes 1572896 | tf_op jit(solution)/shard_map/ppermute | solution.py:81
  612.7 5.8 all-to-all-start.5
  618.5 4.9 collective-permute-start.43
  623.3 4.0 add_convert_fusion.1
  628.5 3.7 collective-permute-done.39.refs_7_
  632.2 5.9 mix_final.5
  641.3 4.1 mix_inward.6
  655.3 12.6 %collective-permute-done.44.refs_7_ = bf16[2,128,2048]{2,1,0:T(8,128)(2,1)} collective-permute-done((bf16[2,128,2048]{2,1,0:T(8,128)(2,1)}, bf16[2,128,2048]{2,1,0:T(8,128)(2,1)}, u32[]{:S(2)}, u32[]{:S(2)}) %collective-permute-start.44) | collective-permute-done | bytes 1048608 | tf_op jit(solution)/shard_map/ppermute | solution.py:81
  667.9 5.8 mix_final.6
  675.7 4.2 mix_inward.9
  681.4 17.8 %all-gather.2 = f32[4096,45]{0,1:T(8,128)S(1)} all-gather(f32[512,45]{0,1:T(8,128)S(1)} %pad_maximum_fusion.3), channel_id=5, replica_groups=mesh['dp'=8,'stream'=4] {'dp'}, dimensions={0}, use_global_device_ids=true | all-gather | bytes 829440 | tf_op jit(solution)/shard_map/all_gather | solution.py:1082
  699.6 2.8 mix_inward.8
  704.7 2.8 mix_inward.7
  713.1 2.8 convert_element_type.172
  716.9 5.8 mix_final.7
  725.2 3.6 mix_final.8
  731.1 3.6 mix_final.9
  (282 shorter events, 111.1 us)
Async XLA Ops:
  7.2 209.4 %all-gather.6.cloned.1.call-start = ((), (), s32[]{:S(2)}) async-start(), calls=%async_computation.10 | async-start | bytes 2621440 | tf_op jit(solution)/shard_map/all_gather | solution.py:959
  19.4 30.1 %collective-permute-start = (bf16[3,256,512]{2,1,0:T(8,128)(2,1)}, bf16[3,256,512]{2,1,0:T(8,128)(2,1)S(1)}, u32[]{:S(2)}, u32[]{:S(2)}) collective-permute-start(bf16[3,256,512]{2,1,0:T(8,128)(2,1)} %refs_0_), channel_id=1, source_target_pairs={{0,8},{4,12},{8,0},{12,4},{16,24},{20,28},{24,16},{28,20},{1,9},{5... | collective-permute-start | bytes 2359304 | tf_op jit(solution)/shard_map/ppermute | solution.py:77
  20.2 31.9 %collective-permute-start.1 = (bf16[3,256,512]{2,1,0:T(8,128)(2,1)}, bf16[3,256,512]{2,1,0:T(8,128)(2,1)}, u32[]{:S(2)}, u32[]{:S(2)}) collective-permute-start(bf16[3,256,512]{2,1,0:T(8,128)(2,1)} %refs_0_), channel_id=1, source_target_pairs={{0,16},{4,20},{8,24},{12,28},{16,0},{20,4},{24,8},{28,12},{1,17},{... | collective-permute-start | bytes 2359304 | tf_op jit(solution)/shard_map/ppermute | solution.py:77
  20.7 36.2 %collective-permute-start.2 = (bf16[3,256,512]{2,1,0:T(8,128)(2,1)}, bf16[3,256,512]{2,1,0:T(8,128)(2,1)}, u32[]{:S(2)}, u32[]{:S(2)}) collective-permute-start(bf16[3,256,512]{2,1,0:T(8,128)(2,1)} %refs_0_), channel_id=1, source_target_pairs={{0,24},{4,28},{8,16},{12,20},{16,8},{20,12},{24,0},{28,4},{1,25},{... | collective-permute-start | bytes 2359304 | tf_op jit(solution)/shard_map/ppermute | solution.py:77
  22.9 34.6 %collective-permute-start.5 = (bf16[3,256,512]{2,1,0:T(8,128)(2,1)}, bf16[3,256,512]{2,1,0:T(8,128)(2,1)}, u32[]{:S(2)}, u32[]{:S(2)}) collective-permute-start(bf16[3,256,512]{2,1,0:T(8,128)(2,1)} %refs_0_), channel_id=1, source_target_pairs={{0,4},{4,0},{8,12},{12,8},{16,20},{20,16},{24,28},{28,24},{1,5},{5... | collective-permute-start | bytes 2359304 | tf_op jit(solution)/shard_map/ppermute | solution.py:77
  44.0 247.3 %copy-start.12 = (f32[4,512,62]{1,0,2:T(4,128)}, f32[4,512,62]{1,0,2:T(4,128)S(1)}, u32[]{:S(2)}) copy-start(f32[4,512,62]{1,0,2:T(4,128)S(1)} %reshape.497) | copy-start | bytes 1523716
  52.1 34.4 %collective-permute-start.3 = (bf16[256,2048]{1,0:T(8,128)(2,1)}, bf16[256,2048]{1,0:T(8,128)(2,1)}, u32[]{:S(2)}, u32[]{:S(2)}) collective-permute-start(bf16[256,2048]{1,0:T(8,128)(2,1)} %refs_0_.1), channel_id=1, source_target_pairs={{0,8},{4,12},{8,0},{12,4},{16,24},{20,28},{24,16},{28,20},{1,9},{5... | collective-permute-start | bytes 3145736 | tf_op jit(solution)/shard_map/ppermute | solution.py:77
  56.1 30.4 %collective-permute-start.4 = (bf16[256,2048]{1,0:T(8,128)(2,1)}, bf16[256,2048]{1,0:T(8,128)(2,1)}, u32[]{:S(2)}, u32[]{:S(2)}) collective-permute-start(bf16[256,2048]{1,0:T(8,128)(2,1)} %refs_0_.1), channel_id=1, source_target_pairs={{0,16},{4,20},{8,24},{12,28},{16,0},{20,4},{24,8},{28,12},{1,17},{... | collective-permute-start | bytes 3145736 | tf_op jit(solution)/shard_map/ppermute | solution.py:77
  56.9 23.1 %collective-permute-start.6 = (bf16[3,256,512]{2,1,0:T(8,128)(2,1)S(1)}, bf16[3,256,512]{2,1,0:T(8,128)(2,1)S(1)}, u32[]{:S(2)}, u32[]{:S(2)}) collective-permute-start(bf16[3,256,512]{2,1,0:T(8,128)(2,1)S(1)} %collective-permute-done.refs_1_), channel_id=1, source_target_pairs={{0,4},{4,0},{8,12},{12,8},{16,20},{20,16},{24,28},{28,24},{1,5},{5... | collective-permute-start | bytes 2359304 | tf_op jit(solution)/shard_map/ppermute | solution.py:77
  56.9 23.1 %collective-permute-start.7 = (bf16[3,256,512]{2,1,0:T(8,128)(2,1)}, bf16[3,256,512]{2,1,0:T(8,128)(2,1)}, u32[]{:S(2)}, u32[]{:S(2)}) collective-permute-start(bf16[3,256,512]{2,1,0:T(8,128)(2,1)} %collective-permute-done.1.refs_2_), channel_id=1, source_target_pairs={{0,4},{4,0},{8,12},{12,8},{16,20},{20,16},{24,28},{28,24},{1,5},{5... | collective-permute-start | bytes 2359304 | tf_op jit(solution)/shard_map/ppermute | solution.py:77
  57.5 22.6 %collective-permute-start.8 = (bf16[3,256,512]{2,1,0:T(8,128)(2,1)}, bf16[3,256,512]{2,1,0:T(8,128)(2,1)}, u32[]{:S(2)}, u32[]{:S(2)}) collective-permute-start(bf16[3,256,512]{2,1,0:T(8,128)(2,1)} %collective-permute-done.2.refs_3_), channel_id=1, source_target_pairs={{0,4},{4,0},{8,12},{12,8},{16,20},{20,16},{24,28},{28,24},{1,5},{5... | collective-permute-start | bytes 2359304 | tf_op jit(solution)/shard_map/ppermute | solution.py:77
  120.9 4.7 collective-permute-start.9
  121.4 40.0 %collective-permute-start.17 = (bf16[512,256]{1,0:T(8,128)(2,1)}, bf16[512,256]{1,0:T(8,128)(2,1)S(1)}, u32[]{:S(2)}, u32[]{:S(2)}) collective-permute-start(bf16[512,256]{1,0:T(8,128)(2,1)} %refs_0_.2), channel_id=1, source_target_pairs={{0,8},{4,12},{8,0},{12,4},{16,24},{20,28},{24,16},{28,20},{1,9},{5... | collective-permute-start | bytes 786440 | tf_op jit(solution)/shard_map/ppermute | solution.py:77
  122.0 41.3 %collective-permute-start.18 = (bf16[512,256]{1,0:T(8,128)(2,1)}, bf16[512,256]{1,0:T(8,128)(2,1)}, u32[]{:S(2)}, u32[]{:S(2)}) collective-permute-start(bf16[512,256]{1,0:T(8,128)(2,1)} %refs_0_.2), channel_id=1, source_target_pairs={{0,16},{4,20},{8,24},{12,28},{16,0},{20,4},{24,8},{28,12},{1,17},{... | collective-permute-start | bytes 786440 | tf_op jit(solution)/shard_map/ppermute | solution.py:77
  122.5 40.8 %collective-permute-start.19 = (bf16[512,256]{1,0:T(8,128)(2,1)}, bf16[512,256]{1,0:T(8,128)(2,1)}, u32[]{:S(2)}, u32[]{:S(2)}) collective-permute-start(bf16[512,256]{1,0:T(8,128)(2,1)} %refs_0_.2), channel_id=1, source_target_pairs={{0,24},{4,28},{8,16},{12,20},{16,8},{20,12},{24,0},{28,4},{1,25},{... | collective-permute-start | bytes 786440 | tf_op jit(solution)/shard_map/ppermute | solution.py:77
  124.9 33.9 %collective-permute-start.25 = (bf16[2048,256]{1,0:T(8,128)(2,1)}, bf16[2048,256]{1,0:T(8,128)(2,1)}, u32[]{:S(2)}, u32[]{:S(2)}) collective-permute-start(bf16[2048,256]{1,0:T(8,128)(2,1)} %refs_0_.3), channel_id=1, source_target_pairs={{0,16},{4,20},{8,24},{12,28},{16,0},{20,4},{24,8},{28,12},{1,17},{... | collective-permute-start | bytes 3145736 | tf_op jit(solution)/shard_map/ppermute | solution.py:77
  125.5 35.9 %collective-permute-start.24 = (bf16[2048,256]{1,0:T(8,128)(2,1)}, bf16[2048,256]{1,0:T(8,128)(2,1)}, u32[]{:S(2)}, u32[]{:S(2)}) collective-permute-start(bf16[2048,256]{1,0:T(8,128)(2,1)} %refs_0_.3), channel_id=1, source_target_pairs={{0,8},{4,12},{8,0},{12,4},{16,24},{20,28},{24,16},{28,20},{1,9},{5... | collective-permute-start | bytes 3145736 | tf_op jit(solution)/shard_map/ppermute | solution.py:77
  159.9 14.9 %collective-permute-start.26 = (bf16[1024,256]{1,0:T(8,128)(2,1)S(1)}, bf16[1024,256]{1,0:T(8,128)(2,1)S(1)}, u32[]{:S(2)}, u32[]{:S(2)}) collective-permute-start(bf16[1024,256]{1,0:T(8,128)(2,1)S(1)} %slice.102), channel_id=1, source_target_pairs={{0,8},{4,12},{8,0},{12,4},{16,24},{20,28},{24,16},{28,20},{1,9},{5... | collective-permute-start | bytes 1572872 | tf_op jit(solution)/shard_map/ppermute | solution.py:77
  161.4 2.3 collective-permute-start.21
  162.6 14.9 %collective-permute-start.27 = (bf16[1024,256]{1,0:T(8,128)(2,1)S(1)}, bf16[1024,256]{1,0:T(8,128)(2,1)S(1)}, u32[]{:S(2)}, u32[]{:S(2)}) collective-permute-start(bf16[1024,256]{1,0:T(8,128)(2,1)S(1)} %slice.103), channel_id=1, source_target_pairs={{0,16},{4,20},{8,24},{12,28},{16,0},{20,4},{24,8},{28,12},{1,17},{... | collective-permute-start | bytes 1572872 | tf_op jit(solution)/shard_map/ppermute | solution.py:77
  163.2 3.5 collective-permute-start.22
  163.4 4.1 collective-permute-start.23
  164.5 4.4 collective-permute-start.20
  166.8 17.7 %collective-permute-start.10 = (bf16[128,2048]{1,0:T(8,128)(2,1)S(1)}, bf16[128,2048]{1,0:T(8,128)(2,1)}, u32[]{:S(2)}, u32[]{:S(2)}) collective-permute-start(bf16[128,2048]{1,0:T(8,128)(2,1)S(1)} %slice.100), channel_id=1, source_target_pairs={{0,8},{4,12},{8,0},{12,4},{16,24},{20,28},{24,16},{28,20},{1,9},{5... | collective-permute-start | bytes 1572872 | tf_op jit(solution)/shard_map/ppermute | solution.py:77
  167.4 24.2 %collective-permute-start.11 = (bf16[128,2048]{1,0:T(8,128)(2,1)S(1)}, bf16[128,2048]{1,0:T(8,128)(2,1)}, u32[]{:S(2)}, u32[]{:S(2)}) collective-permute-start(bf16[128,2048]{1,0:T(8,128)(2,1)S(1)} %slice.101), channel_id=1, source_target_pairs={{0,16},{4,20},{8,24},{12,28},{16,0},{20,4},{24,8},{28,12},{1,17},{... | collective-permute-start | bytes 1572872 | tf_op jit(solution)/shard_map/ppermute | solution.py:77
  168.9 30.2 %collective-permute-start.13 = (bf16[256,2048]{1,0:T(8,128)(2,1)}, bf16[256,2048]{1,0:T(8,128)(2,1)}, u32[]{:S(2)}, u32[]{:S(2)}) collective-permute-start(bf16[256,2048]{1,0:T(8,128)(2,1)} %collective-permute-done.3.refs_1_), channel_id=1, source_target_pairs={{0,4},{4,0},{8,12},{12,8},{16,20},{20,16},{24,28},{28,24},{1,5},{5... | collective-permute-start | bytes 3145736 | tf_op jit(solution)/shard_map/ppermute | solution.py:77
  174.7 24.8 %collective-permute-start.14 = (bf16[256,2048]{1,0:T(8,128)(2,1)}, bf16[256,2048]{1,0:T(8,128)(2,1)}, u32[]{:S(2)}, u32[]{:S(2)}) collective-permute-start(bf16[256,2048]{1,0:T(8,128)(2,1)} %collective-permute-done.4.refs_2_), channel_id=1, source_target_pairs={{0,4},{4,0},{8,12},{12,8},{16,20},{20,16},{24,28},{28,24},{1,5},{5... | collective-permute-start | bytes 3145736 | tf_op jit(solution)/shard_map/ppermute | solution.py:77
  178.3 21.4 %collective-permute-start.12 = (bf16[256,2048]{1,0:T(8,128)(2,1)}, bf16[256,2048]{1,0:T(8,128)(2,1)}, u32[]{:S(2)}, u32[]{:S(2)}) collective-permute-start(bf16[256,2048]{1,0:T(8,128)(2,1)} %refs_0_.1), channel_id=1, source_target_pairs={{0,4},{4,0},{8,12},{12,8},{16,20},{20,16},{24,28},{28,24},{1,5},{5... | collective-permute-start | bytes 3145736 | tf_op jit(solution)/shard_map/ppermute | solution.py:77
  178.3 19.0 %all-to-all-start.1 = ((bf16[8,256,128]{2,1,0:T(8,128)(2,1)}), bf16[8,256,128]{2,1,0:T(8,128)(2,1)S(1)}, u32[]{:S(2)}, u32[]{:S(2)}) async-start(bf16[8,256,128]{2,1,0:T(8,128)(2,1)} %get-tuple-element.82), calls=%async_computation.1 | async-start | bytes 1048576 | tf_op jit(solution)/shard_map/all_to_all | solution.py:973
  181.8 152.3 %all-gather.8.cloned.1.call-start = ((), (), s32[]{:S(2)}) async-start(), calls=%async_computation.11 | async-start | bytes 2621440 | tf_op jit(solution)/shard_map/all_gather | solution.py:992
  184.5 14.1 %collective-permute-start.15 = (bf16[128,2048]{1,0:T(8,128)(2,1)}, bf16[128,2048]{1,0:T(8,128)(2,1)}, u32[]{:S(2)}, u32[]{:S(2)}) collective-permute-start(bf16[128,2048]{1,0:T(8,128)(2,1)} %collective-permute-done.10.refs_3_), channel_id=1, source_target_pairs={{0,4},{4,0},{8,12},{12,8},{16,20},{20,16},{24,28},{28,24},{1,5},{5... | collective-permute-start | bytes 1572872 | tf_op jit(solution)/shard_map/ppermute | solution.py:77
  191.6 7.4 collective-permute-start.16
  198.5 18.1 %collective-permute-start.30 = (bf16[2048,256]{1,0:T(8,128)(2,1)}, bf16[2048,256]{1,0:T(8,128)(2,1)}, u32[]{:S(2)}, u32[]{:S(2)}) collective-permute-start(bf16[2048,256]{1,0:T(8,128)(2,1)} %collective-permute-done.25.refs_2_), channel_id=1, source_target_pairs={{0,4},{4,0},{8,12},{12,8},{16,20},{20,16},{24,28},{28,24},{1,5},{5... | collective-permute-start | bytes 3145736 | tf_op jit(solution)/shard_map/ppermute | solution.py:77
  199.0 17.6 %collective-permute-start.29 = (bf16[2048,256]{1,0:T(8,128)(2,1)}, bf16[2048,256]{1,0:T(8,128)(2,1)}, u32[]{:S(2)}, u32[]{:S(2)}) collective-permute-start(bf16[2048,256]{1,0:T(8,128)(2,1)} %collective-permute-done.24.refs_1_), channel_id=1, source_target_pairs={{0,4},{4,0},{8,12},{12,8},{16,20},{20,16},{24,28},{28,24},{1,5},{5... | collective-permute-start | bytes 3145736 | tf_op jit(solution)/shard_map/ppermute | solution.py:77
  199.1 17.6 %collective-permute-start.28 = (bf16[2048,256]{1,0:T(8,128)(2,1)S(1)}, bf16[2048,256]{1,0:T(8,128)(2,1)}, u32[]{:S(2)}, u32[]{:S(2)}) collective-permute-start(bf16[2048,256]{1,0:T(8,128)(2,1)S(1)} %copy-done.25), channel_id=1, source_target_pairs={{0,4},{4,0},{8,12},{12,8},{16,20},{20,16},{24,28},{28,24},{1,5},{5... | collective-permute-start | bytes 3145736 | tf_op jit(solution)/shard_map/ppermute | solution.py:77
  199.5 17.1 %collective-permute-start.31 = (bf16[1024,256]{1,0:T(8,128)(2,1)S(1)}, bf16[1024,256]{1,0:T(8,128)(2,1)S(1)}, u32[]{:S(2)}, u32[]{:S(2)}) collective-permute-start(bf16[1024,256]{1,0:T(8,128)(2,1)S(1)} %collective-permute-done.26.refs_3_), channel_id=1, source_target_pairs={{0,4},{4,0},{8,12},{12,8},{16,20},{20,16},{24,28},{28,24},{1,5},{5... | collective-permute-start | bytes 1572872 | tf_op jit(solution)/shard_map/ppermute | solution.py:77
  199.6 17.0 %collective-permute-start.32 = (bf16[1024,256]{1,0:T(8,128)(2,1)S(1)}, bf16[1024,256]{1,0:T(8,128)(2,1)}, u32[]{:S(2)}, u32[]{:S(2)}) collective-permute-start(bf16[1024,256]{1,0:T(8,128)(2,1)S(1)} %copy-done.30), channel_id=1, source_target_pairs={{0,4},{4,0},{8,12},{12,8},{16,20},{20,16},{24,28},{28,24},{1,5},{5... | collective-permute-start | bytes 1572872 | tf_op jit(solution)/shard_map/ppermute | solution.py:77
  291.1 172.7 %reduce-scatter.5.cloned.1.call-start = ((), (), s32[]{:S(2)}) async-start(), calls=%async_computation.12 | async-start | bytes 9437184 | tf_op jit(solution)/shard_map/reduce_scatter | solution.py:1018
  336.4 304.1 %copy-start.20 = (f32[512]{0:T(512)}, f32[512]{0:T(512)S(1)}, u32[]{:S(2)}) copy-start(f32[512]{0:T(512)S(1)} %add_rsqrt_fusion) | copy-start | bytes 6148
  374.7 22.5 %all-to-all-start.3 = ((bf16[8,256,128]{2,1,0:T(8,128)(2,1)}), bf16[8,256,128]{2,1,0:T(8,128)(2,1)S(1)}, u32[]{:S(2)}, u32[]{:S(2)}) async-start(bf16[8,256,128]{2,1,0:T(8,128)(2,1)} %bitcast.20), calls=%async_computation.3 | async-start | bytes 1048576 | tf_op jit(solution)/shard_map/all_to_all | solution.py:1029
  378.7 230.4 %reduce-scatter.7.cloned.1.call-start = ((), (), s32[]{:S(2)}) async-start(), calls=%async_computation.13 | async-start | bytes 2359296 | tf_op jit(solution)/shard_map/reduce_scatter | solution.py:1053
  395.2 47.6 %collective-permute-start.34 = (bf16[512,2048]{1,0:T(8,128)(2,1)}, bf16[512,2048]{1,0:T(8,128)(2,1)S(1)}, u32[]{:S(2)}, u32[]{:S(2)}) collective-permute-start(bf16[512,2048]{1,0:T(8,128)(2,1)} %get-tuple-element.104.last.refs_3_.refs_4_), channel_id=1, source_target_pairs={{0,1},{3,2},{4,5},{7,6},{8,9},{11,10},{12,13},{15,14},{16,17},{19,... | collective-permute-start | bytes 6291464 | tf_op jit(solution)/shard_map/ppermute | solution.py:81
  420.5 6.9 collective-permute-start.33
  445.4 267.8 %reduce-scatter.11.cloned.1.call-start = ((), (), s32[]{:S(2)}) async-start(), calls=%async_computation.15 | async-start | bytes 9437184 | tf_op jit(solution)/shard_map/reduce_scatter | solution.py:1055
  455.4 31.1 %all-to-all-start.4 = ((bf16[8,3,256,128]{3,2,1,0:T(8,128)(2,1)}), bf16[8,3,256,128]{3,2,1,0:T(8,128)(2,1)}, u32[]{:S(2)}, u32[]{:S(2)}) async-start(bf16[8,3,256,128]{3,2,1,0:T(8,128)(2,1)} %pad_maximum_fusion), calls=%async_computation.4 | async-start | bytes 3145728 | tf_op jit(solution)/shard_map/all_to_all | solution.py:1039
  459.8 262.9 %reduce-scatter.9.cloned.1.call-start = ((), (), s32[]{:S(2)}) async-start(), calls=%async_computation.14 | async-start | bytes 7077888 | tf_op jit(solution)/shard_map/reduce_scatter | solution.py:1054
  503.6 39.4 %collective-permute-start.35 = (bf16[3,128,2048]{2,1,0:T(8,128)(2,1)}, bf16[3,128,2048]{2,1,0:T(8,128)(2,1)}, u32[]{:S(2)}, u32[]{:S(2)}) collective-permute-start(bf16[3,128,2048]{2,1,0:T(8,128)(2,1)} %get-tuple-element.115.refs_1_), channel_id=1, source_target_pairs={{0,1},{3,2},{4,5},{7,6},{8,9},{11,10},{12,13},{15,14},{16,17},{19,... | collective-permute-start | bytes 4718600 | tf_op jit(solution)/shard_map/ppermute | solution.py:81
  509.0 67.6 %collective-permute-start.40 = (bf16[3,128,2048]{2,1,0:T(8,128)(2,1)}, bf16[3,128,2048]{2,1,0:T(8,128)(2,1)}, u32[]{:S(2)}, u32[]{:S(2)}) collective-permute-start(bf16[3,128,2048]{2,1,0:T(8,128)(2,1)} %get-tuple-element.122.refs_1_), channel_id=1, source_target_pairs={{0,1},{3,2},{4,5},{7,6},{8,9},{11,10},{12,13},{15,14},{16,17},{19,... | collective-permute-start | bytes 4718600 | tf_op jit(solution)/shard_map/ppermute | solution.py:81
  511.5 71.7 %collective-permute-start.37 = (bf16[512,2048]{1,0:T(8,128)(2,1)}, bf16[512,2048]{1,0:T(8,128)(2,1)S(1)}, u32[]{:S(2)}, u32[]{:S(2)}) collective-permute-start(bf16[512,2048]{1,0:T(8,128)(2,1)} %add_convert_fusion), channel_id=1, source_target_pairs={{1,2},{2,1},{5,6},{6,5},{9,10},{10,9},{13,14},{14,13},{17,18},{18,... | collective-permute-start | bytes 6291464 | tf_op jit(solution)/shard_map/ppermute | solution.py:81
  546.7 36.4 %collective-permute-start.36 = (bf16[3,128,2048]{2,1,0:T(8,128)(2,1)}, bf16[3,128,2048]{2,1,0:T(8,128)(2,1)}, u32[]{:S(2)}, u32[]{:S(2)}) collective-permute-start(bf16[3,128,2048]{2,1,0:T(8,128)(2,1)} %add_convert_fusion.3), channel_id=1, source_target_pairs={{1,2},{2,1},{5,6},{6,5},{9,10},{10,9},{13,14},{14,13},{17,18},{18,... | collective-permute-start | bytes 4718600 | tf_op jit(solution)/shard_map/ppermute | solution.py:81
  548.5 33.8 %copy-start.18 = (f32[4,512,8]{1,0,2:T(4,128)S(1)}, f32[4,512,8]{1,0,2:T(4,128)}, u32[]{:S(2)}) copy-start(f32[4,512,8]{1,0,2:T(4,128)} %get-tuple-element.178) | copy-start | bytes 196612
  548.5 58.2 %collective-permute-start.38 = (bf16[3,128,2048]{2,1,0:T(8,128)(2,1)}, bf16[3,128,2048]{2,1,0:T(8,128)(2,1)}, u32[]{:S(2)}, u32[]{:S(2)}) collective-permute-start(bf16[3,128,2048]{2,1,0:T(8,128)(2,1)} %get-tuple-element.119.refs_1_), channel_id=1, source_target_pairs={{0,1},{3,2},{4,5},{7,6},{8,9},{11,10},{12,13},{15,14},{16,17},{19,... | collective-permute-start | bytes 4718600 | tf_op jit(solution)/shard_map/ppermute | solution.py:81
  580.4 57.8 %collective-permute-start.41 = (bf16[3,128,2048]{2,1,0:T(8,128)(2,1)}, bf16[3,128,2048]{2,1,0:T(8,128)(2,1)}, u32[]{:S(2)}, u32[]{:S(2)}) collective-permute-start(bf16[3,128,2048]{2,1,0:T(8,128)(2,1)} %add_convert_fusion.2), channel_id=1, source_target_pairs={{1,2},{2,1},{5,6},{6,5},{9,10},{10,9},{13,14},{14,13},{17,18},{18,... | collective-permute-start | bytes 4718600 | tf_op jit(solution)/shard_map/ppermute | solution.py:81
  606.7 25.6 %collective-permute-start.39 = (bf16[2,128,2048]{2,1,0:T(8,128)(2,1)}, bf16[2,128,2048]{2,1,0:T(8,128)(2,1)}, u32[]{:S(2)}, u32[]{:S(2)}) collective-permute-start(bf16[2,128,2048]{2,1,0:T(8,128)(2,1)} %mix_inward.5), channel_id=1, source_target_pairs={{1,0},{2,3},{5,4},{6,7},{9,8},{10,11},{13,12},{14,15},{17,16},{18,... | collective-permute-start | bytes 3145736 | tf_op jit(solution)/shard_map/ppermute | solution.py:81
  612.7 36.4 %all-to-all-start.5 = ((f32[4,512,16]{1,2,0:T(8,128)}), f32[4,512,16]{1,2,0:T(8,128)S(1)}, u32[]{:S(2)}, u32[]{:S(2)}) async-start(f32[4,512,16]{1,2,0:T(8,128)} %maximum_maximum_fusion), calls=%async_computation.8 | async-start | bytes 262144 | tf_op jit(solution)/shard_map/all_to_all | solution.py:1079
  618.5 27.0 %collective-permute-start.43 = (bf16[3,64,2048]{2,1,0:T(8,128)(2,1)S(1)}, bf16[3,64,2048]{2,1,0:T(8,128)(2,1)}, u32[]{:S(2)}, u32[]{:S(2)}) collective-permute-start(bf16[3,64,2048]{2,1,0:T(8,128)(2,1)S(1)} %copy-done.4), channel_id=1, source_target_pairs={{0,1},{3,2},{4,5},{7,6},{8,9},{11,10},{12,13},{15,14},{16,17},{19,... | collective-permute-start | bytes 2359304 | tf_op jit(solution)/shard_map/ppermute | solution.py:81
  627.4 47.2 %collective-permute-start.49 = (bf16[3,128,2048]{2,1,0:T(8,128)(2,1)}, bf16[3,128,2048]{2,1,0:T(8,128)(2,1)S(1)}, u32[]{:S(2)}, u32[]{:S(2)}) collective-permute-start(bf16[3,128,2048]{2,1,0:T(8,128)(2,1)} %add_convert_fusion.1), channel_id=1, source_target_pairs={{1,2},{2,1},{5,6},{6,5},{9,10},{10,9},{13,14},{14,13},{17,18},{18,... | collective-permute-start | bytes 4718600 | tf_op jit(solution)/shard_map/ppermute | solution.py:81
  638.1 14.8 %collective-permute-start.42 = (bf16[3,64,2048]{2,1,0:T(8,128)(2,1)S(1)}, bf16[3,64,2048]{2,1,0:T(8,128)(2,1)}, u32[]{:S(2)}, u32[]{:S(2)}) collective-permute-start(bf16[3,64,2048]{2,1,0:T(8,128)(2,1)S(1)} %copy-done.3), channel_id=1, source_target_pairs={{0,1},{3,2},{4,5},{7,6},{8,9},{11,10},{12,13},{15,14},{16,17},{19,... | collective-permute-start | bytes 2359304 | tf_op jit(solution)/shard_map/ppermute | solution.py:81
  645.4 22.4 %collective-permute-start.44 = (bf16[2,128,2048]{2,1,0:T(8,128)(2,1)}, bf16[2,128,2048]{2,1,0:T(8,128)(2,1)}, u32[]{:S(2)}, u32[]{:S(2)}) collective-permute-start(bf16[2,128,2048]{2,1,0:T(8,128)(2,1)} %mix_inward.6), channel_id=1, source_target_pairs={{1,0},{2,3},{5,4},{6,7},{9,8},{10,11},{13,12},{14,15},{17,16},{18,... | collective-permute-start | bytes 3145736 | tf_op jit(solution)/shard_map/ppermute | solution.py:81
  651.4 48.2 %collective-permute-start.47 = (bf16[3,64,2048]{2,1,0:T(8,128)(2,1)}, bf16[3,64,2048]{2,1,0:T(8,128)(2,1)}, u32[]{:S(2)}, u32[]{:S(2)}) collective-permute-start(bf16[3,64,2048]{2,1,0:T(8,128)(2,1)} %add_convert_fusion.5), channel_id=1, source_target_pairs={{1,2},{2,1},{5,6},{6,5},{9,10},{10,9},{13,14},{14,13},{17,18},{18,... | collective-permute-start | bytes 2359304 | tf_op jit(solution)/shard_map/ppermute | solution.py:81
  673.7 30.1 %collective-permute-start.45 = (bf16[3,64,2048]{2,1,0:T(8,128)(2,1)}, bf16[3,64,2048]{2,1,0:T(8,128)(2,1)S(1)}, u32[]{:S(2)}, u32[]{:S(2)}) collective-permute-start(bf16[3,64,2048]{2,1,0:T(8,128)(2,1)} %add_convert_fusion.6), channel_id=1, source_target_pairs={{1,2},{2,1},{5,6},{6,5},{9,10},{10,9},{13,14},{14,13},{17,18},{18,... | collective-permute-start | bytes 2359304 | tf_op jit(solution)/shard_map/ppermute | solution.py:81
  679.9 36.0 %collective-permute-start.50 = (bf16[2,128,2048]{2,1,0:T(8,128)(2,1)}, bf16[2,128,2048]{2,1,0:T(8,128)(2,1)S(1)}, u32[]{:S(2)}, u32[]{:S(2)}) collective-permute-start(bf16[2,128,2048]{2,1,0:T(8,128)(2,1)} %mix_inward.9), channel_id=1, source_target_pairs={{1,0},{2,3},{5,4},{6,7},{9,8},{10,11},{13,12},{14,15},{17,16},{18,... | collective-permute-start | bytes 3145736 | tf_op jit(solution)/shard_map/ppermute | solution.py:81
  702.5 22.8 %collective-permute-start.48 = (bf16[2,64,2048]{2,1,0:T(8,128)(2,1)}, bf16[2,64,2048]{2,1,0:T(8,128)(2,1)}, u32[]{:S(2)}, u32[]{:S(2)}) collective-permute-start(bf16[2,64,2048]{2,1,0:T(8,128)(2,1)} %mix_inward.8), channel_id=1, source_target_pairs={{1,0},{2,3},{5,4},{6,7},{9,8},{10,11},{13,12},{14,15},{17,16},{18,... | collective-permute-start | bytes 1572872 | tf_op jit(solution)/shard_map/ppermute | solution.py:81
  707.5 22.8 %collective-permute-start.46 = (bf16[2,64,2048]{2,1,0:T(8,128)(2,1)}, bf16[2,64,2048]{2,1,0:T(8,128)(2,1)S(1)}, u32[]{:S(2)}, u32[]{:S(2)}) collective-permute-start(bf16[2,64,2048]{2,1,0:T(8,128)(2,1)} %mix_inward.7), channel_id=1, source_target_pairs={{1,0},{2,3},{5,4},{6,7},{9,8},{10,11},{13,12},{14,15},{17,16},{18,... | collective-permute-start | bytes 1572872 | tf_op jit(solution)/shard_map/ppermute | solution.py:81
  (40 other events, 333.7 us)
Sparse Core Ops, SparseCore 0:
  125.0 45.0 all-gather.5
  291.2 42.8 all-gather.7
  347.4 75.6 reduce-scatter.4
  445.5 51.3 reduce-scatter.6
  500.2 71.5 reduce-scatter.10
  575.0 61.6 reduce-scatter.8

commit v4 on v3

--- a/solution.py
+++ b/solution.py
@@ -167,7 +167,7 @@
 
 
 def block_spans(tokens):
-    sizes = [tokens // 4] * 3 + [tokens // 8] * 2
+    sizes = [tokens // 4] * 4
     return [(sum(sizes[:i]), size) for i, size in enumerate(sizes)]
 
 

time: 755 us -> 820 us (1.086)
  the two profiles are of different devices: /device:TPU:0 before, /device:TPU:2 now
where the time goes in v4:
time: 820 us; the launch traced here: 810 us
  Pallas kernels  245 us (30%)
  waiting for transfers between devices  228 us (28%)
  blocking collectives  112 us (14%)
  starting transfers between devices  86.5 us (11%)
  local copies, waits for them, and re-layouts  53.8 us (7%)
  other arithmetic  38.8 us (5%)
  matrix products  30.6 us (4%)
  between operations  16.1 us (2%)
    ppermute x14, waiting for transfers between devices, line_hop(): return lax.ppermute(shard, 'stream', pairs)  74 us
    all_to_all x1, waiting for transfers between devices, small_sums(): both = jnp.sum(lax.all_to_all(both, 'stream', 0, 0, tiled=True), axis=0)  63.5 us
    all_to_all x1, blocking collectives, body(): columns = lax.all_to_all(share, 'stream', 0, 0, tiled=True)  53.5 us
    ppermute x14, starting transfers between devices, line_hop(): return lax.ppermute(shard, 'stream', pairs)  44.7 us
    all_gather x1, waiting for transfers between devices, body(): block_full = lax.all_gather(block_out, 'stream', axis=1, tiled=True)  43.6 us
    pallas_call x8, Pallas kernels, mix_block(): pl.pallas_call(kernel, grid=(1,), in_specs=specs, out_specs=out_spec, out...  39.9 us
    pallas_call x1, Pallas kernels, attend_back(): pl.pallas_call(kernel, grid_spec=pltpu.PrefetchScalarGridSpec(num_scalar_...  35.8 us
    ppermute x34, waiting for transfers between devices, partner(): return lax.ppermute(shard, 'dp', [(i, i ^ bit) for i in range(peers)])  27.8 us
  transfers between devices with their start and end apart: 58, of which 17 were waited for; matrix products, arithmetic and copies ran while one was open for 11% of the time, Pallas kernels for 26%

profile of v4, /device:TPU:2, one launch (start us, length us, event | category | flops | bytes accessed | tf_op | source)
XLA Modules:
  0.0 810.2 jit_solution(10932660371544202316)
XLA Ops:
  9.9 7.4 all-reduce.2
  25.1 16.5 %all-gather.1 = f32[2048,62]{0,1:T(8,128)S(1)} all-gather(f32[512,62]{0,1:T(8,128)S(1)} %concatenate.27), channel_id=4, replica_groups=mesh['dp'=8,'stream'=4] {'stream'}, dimensions={0}, use_global_device_ids=true | all-gather | bytes 634880 | tf_op jit(solution)/shard_map/all_gather | solution.py:938
  48.0 5.6 collective-permute-done.1.refs_2_
  54.3 22.6 %make_streams.1 = (bf16[4,512,2048]{2,1,0:T(8,128)(2,1)}, bf16[4,512,2048]{2,1,0:T(8,128)(2,1)}, f32[512,4]{1,0:T(8,128)}, f32[512,2048]{1,0:T(8,128)}) custom-call(bf16[8,512,2048]{2,1,0:T(8,128)(2,1)} %hist.2, f32[512,32]{1,0:T(8,128)} %copy.63.mix, f32[4,2048]{1,0:T(4,128)} %get-tuple-element.191.gain, f32[4,2048]{1,0:T(4,128)} %get-tuple-element.190.bias), custom_call_target="tpu_custom_call" | custom-call | flops 19800000512 | bytes 66000000 | tf_op jit(solution)/shard_map/make_streams/pallas_call | solution.py:266
  77.8 5.5 put_together.4.w
  83.3 8.8 %project.1 = bf16[8,3,256,128]{3,2,1,0:T(8,128)(2,1)} custom-call(bf16[4,512,2048]{2,1,0:T(8,128)(2,1)} %get-tuple-element.75.x, bf16[8,3,256,512]{3,2,1,0:T(8,128)(2,1)} %put_together.4.w, f32[3,512,128]{2,1,0:T(8,128)} %get-tuple-element.170.table), custom_call_target="tpu_custom_call" | custom-call | flops 8099999744 | bytes 27000000 | tf_op jit(solution)/shard_map/project/pallas_call | solution.py:316
  92.1 25.1 %all_to_all.30.mine = bf16[8,3,256,128]{3,2,1,0:T(8,128)(2,1)S(1)} all-to-all(bf16[8,3,256,128]{3,2,1,0:T(8,128)(2,1)} %project.1), channel_id=1, replica_groups=mesh['dp'=8,'stream'=4] {'dp'}, dimensions={0} | all-to-all | bytes 3145728 | tf_op jit(solution)/shard_map/all_to_all | solution.py:967
  124.4 27.5 %attend.1 = (bf16[8,256,128]{2,1,0:T(8,128)(2,1)}, f32[8,256,128]{2,1,0:T(8,128)}, f32[8,256,1]{2,1,0:T(8,128)}) custom-call(s32[8]{0:T(128)} %subtract_maximum_fusion.first, s32[1]{0:T(128)} %bitcast.1.part, bf16[8,3,256,128]{3,2,1,0:T(8,128)(2,1)} %copy-done.7, bf16[8,2,256,128]{3,2,1,0:T(8,128)(2,1)} %collective-permute-done.9.theirs), custom_call_target="tpu_custom_call" | custom-call | flops 14400000000 | bytes 48000000 | tf_op jit(solution)/shard_map/attend/pallas_call | solution.py:375
  151.9 5.0 collective-permute-done.25.refs_2_
  167.0 5.9 collective-permute-done.26.refs_3_
  175.5 4.9 all-to-all-start.1
  183.2 5.7 collective-permute-done.11.refs_4_
  188.9 3.2 slice_bitcast_fusion.1.x_ref
  197.3 6.5 put_together.5
  203.8 10.0 %hidden_units.1 = (bf16[512,2048]{1,0:T(8,128)(2,1)}, bf16[512,2048]{1,0:T(8,128)(2,1)}) custom-call(bf16[512,2048]{1,0:T(8,128)(2,1)} %slice_bitcast_fusion.1.x_ref, bf16[2048,2048]{1,0:T(8,128)(2,1)} %bitcast.107), custom_call_target="tpu_custom_call" | custom-call | flops 8099999744 | bytes 27000000 | tf_op jit(solution)/shard_map/hidden_units/pallas_call | solution.py:802
  214.7 6.5 put_together.7.wd.refs_1_
  221.2 12.6 %merge_branches.1 = bf16[4,512,512]{2,1,0:T(8,128)(2,1)} custom-call(bf16[512,512]{1,0:T(8,128)(2,1)} %bitcast.98, bf16[512,2048]{1,0:T(8,128)(2,1)} %get-tuple-element.84.h, bf16[8,512,256]{2,1,0:T(8,128)(2,1)} %put_together.6.wm.refs_1_, bf16[8,2048,256]{2,1,0:T(8,128)(2,1)} %put_together.7.wd.refs_1_, f32[512,2048]{1,0:T(8,128)} %get-tuple-element.94.st, ...), custom_call_target="tpu_custom_call" | custom-call | flops 11699999744 | bytes 39000000 | tf_op jit(solution)/shard_map/merge_branches/pallas_call | solution.py:830
  233.8 53.5 %all_to_all.31 = bf16[4,512,512]{2,1,0:T(8,128)(2,1)S(1)} all-to-all(bf16[4,512,512]{2,1,0:T(8,128)(2,1)} %merge_branches.1), channel_id=1, replica_groups=mesh['dp'=8,'stream'=4] {'stream'}, dimensions={0} | all-to-all | bytes 4194304 | tf_op jit(solution)/shard_map/all_to_all | solution.py:990
  288.9 43.6 %all-gather.8.cloned.1.call-done = bf16[512,2048]{1,0:T(8,128)(2,1)} async-done(((bf16[512,512]{1,0:T(8,128)(2,1)}), bf16[512,2048]{1,0:T(8,128)(2,1)}) %all-gather.8.cloned.1.call-update) | async-done | bytes 2097168 | tf_op jit(solution)/shard_map/all_gather | solution.py:992
  338.9 6.9 convolution_convert_fusion.1
  346.4 3.2 slice_bitcast_fusion.u
  349.6 14.7 %back_through.3 = bf16[512,2048]{1,0:T(8,128)(2,1)} custom-call(bf16[512,2048]{1,0:T(8,128)(2,1)} %copy-done.38, bf16[8,2048,256]{2,1,0:T(8,128)(2,1)} %put_together.7.wd.refs_1_, bf16[512,2048]{1,0:T(8,128)(2,1)} %get-tuple-element.95.refs_2_), custom_call_target="tpu_custom_call" | custom-call | flops 11699999744 | bytes 39000000 | tf_op jit(solution)/shard_map/back_through/pallas_call | solution.py:885
  364.3 7.3 back_through.2
  373.6 4.2 all-to-all-start.3
  378.0 9.8 %fusion.37.g = f32[512,2048]{1,0:T(8,128)} fusion(bf16[512,2048]{1,0:T(8,128)(2,1)S(1)} %copy-done.41, bf16[2048,2048]{1,0:T(8,128)(2,1)} %bitcast.108), kind=kOutput, calls=%fused_computation.98 | convolution fusion | flops 4294967296 | bytes 14680064 | tf_op jit(solution)/shard_map/dot_general | solution.py:72
  387.8 6.5 last_back.1
  396.8 35.8 %attend_back.1 = (bf16[8,3,256,128]{3,2,1,0:T(8,128)(2,1)}, bf16[8,2,256,128]{3,2,1,0:T(8,128)(2,1)}) custom-call(s32[8]{0:T(128)} %subtract_maximum_fusion.first, s32[1]{0:T(128)} %bitcast.1.part, bf16[8,3,256,128]{3,2,1,0:T(8,128)(2,1)} %copy-done.7, bf16[8,2,256,128]{3,2,1,0:T(8,128)(2,1)} %collective-permute-done.9.theirs, ...), custom_call_target="tpu_custom_call" | custom-call | flops 19800000512 | bytes 66000000 | tf_op jit(solution)/shard_map/attend_back/pallas_call | solution.py:449
  432.7 4.6 collective-permute-start.33
  443.6 2.6 convolution_convert_fusion.2
  447.8 8.4 %convolution_convert_fusion = bf16[2048,2048]{1,0:T(8,128)(2,1)} fusion(bf16[512,2048]{1,0:T(8,128)(2,1)S(1)} %copy-done.42, bf16[4,512,2048]{2,1,0:T(8,128)(2,1)} %get-tuple-element.75.x), kind=kOutput, calls=%fused_computation | convolution fusion | flops 4299161600 | bytes 12582912 | tf_op jit(solution)/shard_map/dot_general | solution.py:68
  456.2 4.6 all-to-all-start.4
  461.1 3.7 add_convert_fusion
  464.8 2.7 convert_element_type.143
  467.5 18.6 %all-to-all-done.4.part = bf16[8,3,256,128]{3,2,1,0:T(8,128)(2,1)} async-done(((bf16[8,3,256,128]{3,2,1,0:T(8,128)(2,1)}), bf16[8,3,256,128]{3,2,1,0:T(8,128)(2,1)}, u32[]{:S(2)}, u32[]{:S(2)}) %all-to-all-start.4) | async-done | bytes 1572896 | tf_op jit(solution)/shard_map/all_to_all | solution.py:1039
  486.1 17.0 %heads_back.1 = (bf16[3,128,2048]{2,1,0:T(8,128)(2,1)}, bf16[3,128,2048]{2,1,0:T(8,128)(2,1)}, bf16[3,128,2048]{2,1,0:T(8,128)(2,1)}, bf16[3,128,2048]{2,1,0:T(8...) custom-call(bf16[8,3,256,128]{3,2,1,0:T(8,128)(2,1)} %all-to-all-done.4.part, ...), custom_call_target="tpu_custom_call" | custom-call | flops 2700000000 | bytes 9000000 | tf_op jit(solution)/shard_map/heads_back/pallas_call | solution.py:521
  503.1 3.4 collective-permute-start.36
  507.3 3.9 collective-permute-start.35
  511.2 10.5 %mixing_back.3 = f32[4,256,8]{2,1,0:T(8,128)} custom-call(bf16[3,512,2048]{2,1,0:T(8,128)(2,1)} %get-tuple-element.111.first, bf16[512,2048]{1,0:T(8,128)(2,1)} %get-tuple-element.98.last.refs_3_.refs_4_, bf16[8,512,2048]{2,1,0:T(8,128)(2,1)} %hist.2), custom_call_target="tpu_custom_call" | custom-call | flops 360000000 | bytes 1200000 | tf_op jit(solution)/shard_map/mixing_back/pallas_call | solution.py:615
  521.7 10.3 %mixing_back.2 = f32[4,256,8]{2,1,0:T(8,128)} custom-call(bf16[3,512,2048]{2,1,0:T(8,128)(2,1)} %get-tuple-element.111.first, bf16[512,2048]{1,0:T(8,128)(2,1)} %get-tuple-element.98.last.refs_3_.refs_4_, bf16[8,512,2048]{2,1,0:T(8,128)(2,1)} %hist.2), custom_call_target="tpu_custom_call" | custom-call | flops 360000000 | bytes 1200000 | tf_op jit(solution)/shard_map/mixing_back/pallas_call | solution.py:615
  532.1 8.4 %collective-permute-done.36.refs_2_ = bf16[3,128,2048]{2,1,0:T(8,128)(2,1)} collective-permute-done((bf16[3,128,2048]{2,1,0:T(8,128)(2,1)}, bf16[3,128,2048]{2,1,0:T(8,128)(2,1)}, u32[]{:S(2)}, u32[]{:S(2)}) %collective-permute-start.36) | collective-permute-done | bytes 1572896 | tf_op jit(solution)/shard_map/ppermute | solution.py:81
  540.4 3.9 add_convert_fusion.4
  546.2 7.0 collective-permute-start.40
  554.9 19.2 %collective-permute-done.35.refs_2_ = bf16[3,128,2048]{2,1,0:T(8,128)(2,1)} collective-permute-done((bf16[3,128,2048]{2,1,0:T(8,128)(2,1)}, bf16[3,128,2048]{2,1,0:T(8,128)(2,1)}, u32[]{:S(2)}, u32[]{:S(2)}) %collective-permute-start.35) | collective-permute-done | bytes 1572896 | tf_op jit(solution)/shard_map/ppermute | solution.py:81
  574.1 17.1 %collective-permute-start.38 = (bf16[3,128,2048]{2,1,0:T(8,128)(2,1)}, bf16[3,128,2048]{2,1,0:T(8,128)(2,1)}, u32[]{:S(2)}, u32[]{:S(2)}) collective-permute-start(bf16[3,128,2048]{2,1,0:T(8,128)(2,1)} %get-tuple-element.113.refs_1_), channel_id=1, source_target_pairs={{0,1},{3,2},{4,5},{7,6},{8,9},{11,10},{12,13},{15,14},{16,17},{19,... | collective-permute-start | bytes 4718600 | tf_op jit(solution)/shard_map/ppermute | solution.py:81
  594.4 4.1 mix_inward.4
  598.5 9.3 %collective-permute-done.40.refs_2_ = bf16[3,128,2048]{2,1,0:T(8,128)(2,1)} collective-permute-done((bf16[3,128,2048]{2,1,0:T(8,128)(2,1)}, bf16[3,128,2048]{2,1,0:T(8,128)(2,1)}, u32[]{:S(2)}, u32[]{:S(2)}) %collective-permute-start.40) | collective-permute-done | bytes 1572896 | tf_op jit(solution)/shard_map/ppermute | solution.py:81
  609.1 3.7 add_convert_fusion.1
  614.7 3.8 add_convert_fusion.2
  619.6 13.9 %collective-permute-done.41.refs_7_ = bf16[2,128,2048]{2,1,0:T(8,128)(2,1)} collective-permute-done((bf16[2,128,2048]{2,1,0:T(8,128)(2,1)}, bf16[2,128,2048]{2,1,0:T(8,128)(2,1)}, u32[]{:S(2)}, u32[]{:S(2)}) %collective-permute-start.41) | collective-permute-done | bytes 1048608 | tf_op jit(solution)/shard_map/ppermute | solution.py:81
  633.5 5.9 mix_final.4
  640.7 3.2 add_convert_fusion.3
  651.6 6.4 all-to-all-start.5
  659.2 63.5 %all-to-all-done.5 = f32[4,512,16]{1,2,0:T(8,128)S(1)} async-done(((f32[4,512,16]{1,2,0:T(8,128)}), f32[4,512,16]{1,2,0:T(8,128)S(1)}, u32[]{:S(2)}, u32[]{:S(2)}) %all-to-all-start.5) | async-done | bytes 131104 | tf_op jit(solution)/shard_map/all_to_all | solution.py:1079
  722.9 4.2 mix_inward.7
  729.5 4.2 mix_inward.6
  736.3 4.1 mix_inward.5
  741.9 9.9 %all-gather.2 = f32[4096,45]{0,1:T(8,128)S(1)} all-gather(f32[512,45]{0,1:T(8,128)S(1)} %pad_maximum_fusion.3), channel_id=5, replica_groups=mesh['dp'=8,'stream'=4] {'dp'}, dimensions={0}, use_global_device_ids=true | all-gather | bytes 829440 | tf_op jit(solution)/shard_map/all_gather | solution.py:1082
  756.3 2.8 convert_element_type.160
  759.1 5.8 mix_final.5
  764.9 12.7 %collective-permute-done.45.refs_7_ = bf16[2,128,2048]{2,1,0:T(8,128)(2,1)S(1)} collective-permute-done((bf16[2,128,2048]{2,1,0:T(8,128)(2,1)}, bf16[2,128,2048]{2,1,0:T(8,128)(2,1)S(1)}, u32[]{:S(2)}, u32[]{:S(2)}) %collective-permute-start.45) | collective-permute-done | bytes 1048608 | tf_op jit(solution)/shard_map/ppermute | solution.py:81
  778.6 5.8 mix_final.6
  784.4 2.5 convert_element_type.153
  786.9 9.2 %collective-permute-done.43.refs_7_ = bf16[2,128,2048]{2,1,0:T(8,128)(2,1)S(1)} collective-permute-done((bf16[2,128,2048]{2,1,0:T(8,128)(2,1)}, bf16[2,128,2048]{2,1,0:T(8,128)(2,1)S(1)}, u32[]{:S(2)}, u32[]{:S(2)}) %collective-permute-start.43) | collective-permute-done | bytes 1048608 | tf_op jit(solution)/shard_map/ppermute | solution.py:81
  797.1 5.8 mix_final.7
  (275 shorter events, 102.7 us)
Async XLA Ops:
  7.2 206.7 %all-gather.6.cloned.1.call-start = ((), (), s32[]{:S(2)}) async-start(), calls=%async_computation.10 | async-start | bytes 2621440 | tf_op jit(solution)/shard_map/all_gather | solution.py:959
  17.3 30.7 %collective-permute-start = (bf16[3,256,512]{2,1,0:T(8,128)(2,1)}, bf16[3,256,512]{2,1,0:T(8,128)(2,1)S(1)}, u32[]{:S(2)}, u32[]{:S(2)}) collective-permute-start(bf16[3,256,512]{2,1,0:T(8,128)(2,1)} %refs_0_), channel_id=1, source_target_pairs={{0,8},{4,12},{8,0},{12,4},{16,24},{20,28},{24,16},{28,20},{1,9},{5... | collective-permute-start | bytes 2359304 | tf_op jit(solution)/shard_map/ppermute | solution.py:77
  18.4 35.2 %collective-permute-start.1 = (bf16[3,256,512]{2,1,0:T(8,128)(2,1)}, bf16[3,256,512]{2,1,0:T(8,128)(2,1)S(1)}, u32[]{:S(2)}, u32[]{:S(2)}) collective-permute-start(bf16[3,256,512]{2,1,0:T(8,128)(2,1)} %refs_0_), channel_id=1, source_target_pairs={{0,16},{4,20},{8,24},{12,28},{16,0},{20,4},{24,8},{28,12},{1,17},{... | collective-permute-start | bytes 2359304 | tf_op jit(solution)/shard_map/ppermute | solution.py:77
  18.9 34.8 %collective-permute-start.2 = (bf16[3,256,512]{2,1,0:T(8,128)(2,1)}, bf16[3,256,512]{2,1,0:T(8,128)(2,1)}, u32[]{:S(2)}, u32[]{:S(2)}) collective-permute-start(bf16[3,256,512]{2,1,0:T(8,128)(2,1)} %refs_0_), channel_id=1, source_target_pairs={{0,24},{4,28},{8,16},{12,20},{16,8},{20,12},{24,0},{28,4},{1,25},{... | collective-permute-start | bytes 2359304 | tf_op jit(solution)/shard_map/ppermute | solution.py:77
  20.7 33.5 %collective-permute-start.5 = (bf16[3,256,512]{2,1,0:T(8,128)(2,1)}, bf16[3,256,512]{2,1,0:T(8,128)(2,1)}, u32[]{:S(2)}, u32[]{:S(2)}) collective-permute-start(bf16[3,256,512]{2,1,0:T(8,128)(2,1)} %refs_0_), channel_id=1, source_target_pairs={{0,4},{4,0},{8,12},{12,8},{16,20},{20,16},{24,28},{28,24},{1,5},{5... | collective-permute-start | bytes 2359304 | tf_op jit(solution)/shard_map/ppermute | solution.py:77
  41.9 246.9 %copy-start.9 = (f32[4,512,62]{1,0,2:T(4,128)}, f32[4,512,62]{1,0,2:T(4,128)S(1)}, u32[]{:S(2)}) copy-start(f32[4,512,62]{1,0,2:T(4,128)S(1)} %reshape.497) | copy-start | bytes 1523716
  48.0 28.9 %copy-start.25 = (bf16[3,256,512]{2,1,0:T(8,128)(2,1)}, bf16[3,256,512]{2,1,0:T(8,128)(2,1)S(1)}, u32[]{:S(2)}) copy-start(bf16[3,256,512]{2,1,0:T(8,128)(2,1)S(1)} %collective-permute-done.refs_1_) | copy-start | bytes 2359300
  53.6 23.3 %copy-start.26 = (bf16[3,256,512]{2,1,0:T(8,128)(2,1)}, bf16[3,256,512]{2,1,0:T(8,128)(2,1)S(1)}, u32[]{:S(2)}) copy-start(bf16[3,256,512]{2,1,0:T(8,128)(2,1)S(1)} %collective-permute-done.1.refs_2_) | copy-start | bytes 2359300
  53.6 29.7 %collective-permute-start.3 = (bf16[256,2048]{1,0:T(8,128)(2,1)}, bf16[256,2048]{1,0:T(8,128)(2,1)}, u32[]{:S(2)}, u32[]{:S(2)}) collective-permute-start(bf16[256,2048]{1,0:T(8,128)(2,1)} %refs_0_.1), channel_id=1, source_target_pairs={{0,8},{4,12},{8,0},{12,4},{16,24},{20,28},{24,16},{28,20},{1,9},{5... | collective-permute-start | bytes 3145736 | tf_op jit(solution)/shard_map/ppermute | solution.py:77
  53.6 29.7 %collective-permute-start.4 = (bf16[256,2048]{1,0:T(8,128)(2,1)}, bf16[256,2048]{1,0:T(8,128)(2,1)}, u32[]{:S(2)}, u32[]{:S(2)}) collective-permute-start(bf16[256,2048]{1,0:T(8,128)(2,1)} %refs_0_.1), channel_id=1, source_target_pairs={{0,16},{4,20},{8,24},{12,28},{16,0},{20,4},{24,8},{28,12},{1,17},{... | collective-permute-start | bytes 3145736 | tf_op jit(solution)/shard_map/ppermute | solution.py:77
  53.7 23.2 %collective-permute-start.6 = (bf16[3,256,512]{2,1,0:T(8,128)(2,1)S(1)}, bf16[3,256,512]{2,1,0:T(8,128)(2,1)S(1)}, u32[]{:S(2)}, u32[]{:S(2)}) collective-permute-start(bf16[3,256,512]{2,1,0:T(8,128)(2,1)S(1)} %collective-permute-done.refs_1_), channel_id=1, source_target_pairs={{0,4},{4,0},{8,12},{12,8},{16,20},{20,16},{24,28},{28,24},{1,5},{5... | collective-permute-start | bytes 2359304 | tf_op jit(solution)/shard_map/ppermute | solution.py:77
  53.7 23.2 %collective-permute-start.7 = (bf16[3,256,512]{2,1,0:T(8,128)(2,1)S(1)}, bf16[3,256,512]{2,1,0:T(8,128)(2,1)}, u32[]{:S(2)}, u32[]{:S(2)}) collective-permute-start(bf16[3,256,512]{2,1,0:T(8,128)(2,1)S(1)} %collective-permute-done.1.refs_2_), channel_id=1, source_target_pairs={{0,4},{4,0},{8,12},{12,8},{16,20},{20,16},{24,28},{28,24},{1,5},{5... | collective-permute-start | bytes 2359304 | tf_op jit(solution)/shard_map/ppermute | solution.py:77
  54.2 22.7 %collective-permute-start.8 = (bf16[3,256,512]{2,1,0:T(8,128)(2,1)}, bf16[3,256,512]{2,1,0:T(8,128)(2,1)}, u32[]{:S(2)}, u32[]{:S(2)}) collective-permute-start(bf16[3,256,512]{2,1,0:T(8,128)(2,1)} %collective-permute-done.2.refs_3_), channel_id=1, source_target_pairs={{0,4},{4,0},{8,12},{12,8},{16,20},{20,16},{24,28},{28,24},{1,5},{5... | collective-permute-start | bytes 2359304 | tf_op jit(solution)/shard_map/ppermute | solution.py:77
  92.1 26.7 %copy-start.32 = (bf16[512,256]{1,0:T(8,128)(2,1)S(1)}, bf16[512,256]{1,0:T(8,128)(2,1)}, u32[]{:S(2)}) copy-start(bf16[512,256]{1,0:T(8,128)(2,1)} %refs_0_.2) | copy-start | bytes 786436
  118.3 5.1 collective-permute-start.9
  118.8 39.8 %collective-permute-start.17 = (bf16[512,256]{1,0:T(8,128)(2,1)S(1)}, bf16[512,256]{1,0:T(8,128)(2,1)S(1)}, u32[]{:S(2)}, u32[]{:S(2)}) collective-permute-start(bf16[512,256]{1,0:T(8,128)(2,1)S(1)} %copy-done.32), channel_id=1, source_target_pairs={{0,8},{4,12},{8,0},{12,4},{16,24},{20,28},{24,16},{28,20},{1,9},{5... | collective-permute-start | bytes 786440 | tf_op jit(solution)/shard_map/ppermute | solution.py:77
  120.3 40.6 %collective-permute-start.18 = (bf16[512,256]{1,0:T(8,128)(2,1)S(1)}, bf16[512,256]{1,0:T(8,128)(2,1)}, u32[]{:S(2)}, u32[]{:S(2)}) collective-permute-start(bf16[512,256]{1,0:T(8,128)(2,1)S(1)} %copy-done.32), channel_id=1, source_target_pairs={{0,16},{4,20},{8,24},{12,28},{16,0},{20,4},{24,8},{28,12},{1,17},{... | collective-permute-start | bytes 786440 | tf_op jit(solution)/shard_map/ppermute | solution.py:77
  120.9 40.1 %collective-permute-start.19 = (bf16[512,256]{1,0:T(8,128)(2,1)S(1)}, bf16[512,256]{1,0:T(8,128)(2,1)}, u32[]{:S(2)}, u32[]{:S(2)}) collective-permute-start(bf16[512,256]{1,0:T(8,128)(2,1)S(1)} %copy-done.32), channel_id=1, source_target_pairs={{0,24},{4,28},{8,16},{12,20},{16,8},{20,12},{24,0},{28,4},{1,25},{... | collective-permute-start | bytes 786440 | tf_op jit(solution)/shard_map/ppermute | solution.py:77
  122.4 34.6 %collective-permute-start.25 = (bf16[2048,256]{1,0:T(8,128)(2,1)}, bf16[2048,256]{1,0:T(8,128)(2,1)}, u32[]{:S(2)}, u32[]{:S(2)}) collective-permute-start(bf16[2048,256]{1,0:T(8,128)(2,1)} %refs_0_.3), channel_id=1, source_target_pairs={{0,16},{4,20},{8,24},{12,28},{16,0},{20,4},{24,8},{28,12},{1,17},{... | collective-permute-start | bytes 3145736 | tf_op jit(solution)/shard_map/ppermute | solution.py:77
  123.4 35.3 %collective-permute-start.24 = (bf16[2048,256]{1,0:T(8,128)(2,1)}, bf16[2048,256]{1,0:T(8,128)(2,1)}, u32[]{:S(2)}, u32[]{:S(2)}) collective-permute-start(bf16[2048,256]{1,0:T(8,128)(2,1)} %refs_0_.3), channel_id=1, source_target_pairs={{0,8},{4,12},{8,0},{12,4},{16,24},{20,28},{24,16},{28,20},{1,9},{5... | collective-permute-start | bytes 3145736 | tf_op jit(solution)/shard_map/ppermute | solution.py:77
  158.0 14.9 %collective-permute-start.26 = (bf16[1024,256]{1,0:T(8,128)(2,1)S(1)}, bf16[1024,256]{1,0:T(8,128)(2,1)S(1)}, u32[]{:S(2)}, u32[]{:S(2)}) collective-permute-start(bf16[1024,256]{1,0:T(8,128)(2,1)S(1)} %slice.102), channel_id=1, source_target_pairs={{0,8},{4,12},{8,0},{12,4},{16,24},{20,28},{24,16},{28,20},{1,9},{5... | collective-permute-start | bytes 1572872 | tf_op jit(solution)/shard_map/ppermute | solution.py:77
  158.7 2.7 collective-permute-start.21
  159.8 14.9 %collective-permute-start.27 = (bf16[1024,256]{1,0:T(8,128)(2,1)S(1)}, bf16[1024,256]{1,0:T(8,128)(2,1)S(1)}, u32[]{:S(2)}, u32[]{:S(2)}) collective-permute-start(bf16[1024,256]{1,0:T(8,128)(2,1)S(1)} %slice.103), channel_id=1, source_target_pairs={{0,16},{4,20},{8,24},{12,28},{16,0},{20,4},{24,8},{28,12},{1,17},{... | collective-permute-start | bytes 1572872 | tf_op jit(solution)/shard_map/ppermute | solution.py:77
  160.9 3.5 collective-permute-start.22
  161.0 4.5 collective-permute-start.23
  162.1 4.9 collective-permute-start.20
  164.4 18.8 %collective-permute-start.10 = (bf16[128,2048]{1,0:T(8,128)(2,1)S(1)}, bf16[128,2048]{1,0:T(8,128)(2,1)}, u32[]{:S(2)}, u32[]{:S(2)}) collective-permute-start(bf16[128,2048]{1,0:T(8,128)(2,1)S(1)} %slice.100), channel_id=1, source_target_pairs={{0,8},{4,12},{8,0},{12,4},{16,24},{20,28},{24,16},{28,20},{1,9},{5... | collective-permute-start | bytes 1572872 | tf_op jit(solution)/shard_map/ppermute | solution.py:77
  165.5 23.3 %collective-permute-start.11 = (bf16[128,2048]{1,0:T(8,128)(2,1)S(1)}, bf16[128,2048]{1,0:T(8,128)(2,1)}, u32[]{:S(2)}, u32[]{:S(2)}) collective-permute-start(bf16[128,2048]{1,0:T(8,128)(2,1)S(1)} %slice.101), channel_id=1, source_target_pairs={{0,16},{4,20},{8,24},{12,28},{16,0},{20,4},{24,8},{28,12},{1,17},{... | collective-permute-start | bytes 1572872 | tf_op jit(solution)/shard_map/ppermute | solution.py:77
  167.0 29.3 %collective-permute-start.13 = (bf16[256,2048]{1,0:T(8,128)(2,1)}, bf16[256,2048]{1,0:T(8,128)(2,1)}, u32[]{:S(2)}, u32[]{:S(2)}) collective-permute-start(bf16[256,2048]{1,0:T(8,128)(2,1)} %collective-permute-done.3.refs_1_), channel_id=1, source_target_pairs={{0,4},{4,0},{8,12},{12,8},{16,20},{20,16},{24,28},{28,24},{1,5},{5... | collective-permute-start | bytes 3145736 | tf_op jit(solution)/shard_map/ppermute | solution.py:77
  172.9 23.9 %copy-start.28 = (bf16[1024,256]{1,0:T(8,128)(2,1)}, bf16[1024,256]{1,0:T(8,128)(2,1)S(1)}, u32[]{:S(2)}) copy-start(bf16[1024,256]{1,0:T(8,128)(2,1)S(1)} %collective-permute-done.26.refs_3_) | copy-start | bytes 1572868
  172.9 23.9 %collective-permute-start.14 = (bf16[256,2048]{1,0:T(8,128)(2,1)}, bf16[256,2048]{1,0:T(8,128)(2,1)}, u32[]{:S(2)}, u32[]{:S(2)}) collective-permute-start(bf16[256,2048]{1,0:T(8,128)(2,1)} %collective-permute-done.4.refs_2_), channel_id=1, source_target_pairs={{0,4},{4,0},{8,12},{12,8},{16,20},{20,16},{24,28},{28,24},{1,5},{5... | collective-permute-start | bytes 3145736 | tf_op jit(solution)/shard_map/ppermute | solution.py:77
  175.5 21.4 %collective-permute-start.12 = (bf16[256,2048]{1,0:T(8,128)(2,1)}, bf16[256,2048]{1,0:T(8,128)(2,1)}, u32[]{:S(2)}, u32[]{:S(2)}) collective-permute-start(bf16[256,2048]{1,0:T(8,128)(2,1)} %refs_0_.1), channel_id=1, source_target_pairs={{0,4},{4,0},{8,12},{12,8},{16,20},{20,16},{24,28},{28,24},{1,5},{5... | collective-permute-start | bytes 3145736 | tf_op jit(solution)/shard_map/ppermute | solution.py:77
  175.5 19.0 %all-to-all-start.1 = ((bf16[8,256,128]{2,1,0:T(8,128)(2,1)}), bf16[8,256,128]{2,1,0:T(8,128)(2,1)S(1)}, u32[]{:S(2)}, u32[]{:S(2)}) async-start(bf16[8,256,128]{2,1,0:T(8,128)(2,1)} %get-tuple-element.76), calls=%async_computation.1 | async-start | bytes 1048576 | tf_op jit(solution)/shard_map/all_to_all | solution.py:973
  180.4 152.2 %all-gather.8.cloned.1.call-start = ((), (), s32[]{:S(2)}) async-start(), calls=%async_computation.11 | async-start | bytes 2621440 | tf_op jit(solution)/shard_map/all_gather | solution.py:992
  183.2 12.6 %collective-permute-start.15 = (bf16[128,2048]{1,0:T(8,128)(2,1)}, bf16[128,2048]{1,0:T(8,128)(2,1)}, u32[]{:S(2)}, u32[]{:S(2)}) collective-permute-start(bf16[128,2048]{1,0:T(8,128)(2,1)} %collective-permute-done.10.refs_3_), channel_id=1, source_target_pairs={{0,4},{4,0},{8,12},{12,8},{16,20},{20,16},{24,28},{28,24},{1,5},{5... | collective-permute-start | bytes 1572872 | tf_op jit(solution)/shard_map/ppermute | solution.py:77
  188.9 7.4 collective-permute-start.16
  195.8 18.1 %collective-permute-start.30 = (bf16[2048,256]{1,0:T(8,128)(2,1)}, bf16[2048,256]{1,0:T(8,128)(2,1)}, u32[]{:S(2)}, u32[]{:S(2)}) collective-permute-start(bf16[2048,256]{1,0:T(8,128)(2,1)} %collective-permute-done.25.refs_2_), channel_id=1, source_target_pairs={{0,4},{4,0},{8,12},{12,8},{16,20},{20,16},{24,28},{28,24},{1,5},{5... | collective-permute-start | bytes 3145736 | tf_op jit(solution)/shard_map/ppermute | solution.py:77
  196.3 17.6 %collective-permute-start.29 = (bf16[2048,256]{1,0:T(8,128)(2,1)}, bf16[2048,256]{1,0:T(8,128)(2,1)}, u32[]{:S(2)}, u32[]{:S(2)}) collective-permute-start(bf16[2048,256]{1,0:T(8,128)(2,1)} %collective-permute-done.24.refs_1_), channel_id=1, source_target_pairs={{0,4},{4,0},{8,12},{12,8},{16,20},{20,16},{24,28},{28,24},{1,5},{5... | collective-permute-start | bytes 3145736 | tf_op jit(solution)/shard_map/ppermute | solution.py:77
  196.4 17.6 %collective-permute-start.28 = (bf16[2048,256]{1,0:T(8,128)(2,1)S(1)}, bf16[2048,256]{1,0:T(8,128)(2,1)}, u32[]{:S(2)}, u32[]{:S(2)}) collective-permute-start(bf16[2048,256]{1,0:T(8,128)(2,1)S(1)} %copy-done.24), channel_id=1, source_target_pairs={{0,4},{4,0},{8,12},{12,8},{16,20},{20,16},{24,28},{28,24},{1,5},{5... | collective-permute-start | bytes 3145736 | tf_op jit(solution)/shard_map/ppermute | solution.py:77
  196.8 17.1 %collective-permute-start.31 = (bf16[1024,256]{1,0:T(8,128)(2,1)S(1)}, bf16[1024,256]{1,0:T(8,128)(2,1)S(1)}, u32[]{:S(2)}, u32[]{:S(2)}) collective-permute-start(bf16[1024,256]{1,0:T(8,128)(2,1)S(1)} %collective-permute-done.26.refs_3_), channel_id=1, source_target_pairs={{0,4},{4,0},{8,12},{12,8},{16,20},{20,16},{24,28},{28,24},{1,5},{5... | collective-permute-start | bytes 1572872 | tf_op jit(solution)/shard_map/ppermute | solution.py:77
  196.9 17.0 %collective-permute-start.32 = (bf16[1024,256]{1,0:T(8,128)(2,1)S(1)}, bf16[1024,256]{1,0:T(8,128)(2,1)}, u32[]{:S(2)}, u32[]{:S(2)}) collective-permute-start(bf16[1024,256]{1,0:T(8,128)(2,1)S(1)} %copy-done.30), channel_id=1, source_target_pairs={{0,4},{4,0},{8,12},{12,8},{16,20},{20,16},{24,28},{28,24},{1,5},{5... | collective-permute-start | bytes 1572872 | tf_op jit(solution)/shard_map/ppermute | solution.py:77
  288.6 176.2 %reduce-scatter.5.cloned.1.call-start = ((), (), s32[]{:S(2)}) async-start(), calls=%async_computation.12 | async-start | bytes 9437184 | tf_op jit(solution)/shard_map/reduce_scatter | solution.py:1018
  373.6 22.4 %all-to-all-start.3 = ((bf16[8,256,128]{2,1,0:T(8,128)(2,1)}), bf16[8,256,128]{2,1,0:T(8,128)(2,1)S(1)}, u32[]{:S(2)}, u32[]{:S(2)}) async-start(bf16[8,256,128]{2,1,0:T(8,128)(2,1)} %bitcast.20), calls=%async_computation.3 | async-start | bytes 1048576 | tf_op jit(solution)/shard_map/all_to_all | solution.py:1029
  377.8 175.3 %reduce-scatter.7.cloned.1.call-start = ((), (), s32[]{:S(2)}) async-start(), calls=%async_computation.13 | async-start | bytes 2359296 | tf_op jit(solution)/shard_map/reduce_scatter | solution.py:1053
  394.3 48.3 %collective-permute-start.34 = (bf16[512,2048]{1,0:T(8,128)(2,1)}, bf16[512,2048]{1,0:T(8,128)(2,1)S(1)}, u32[]{:S(2)}, u32[]{:S(2)}) collective-permute-start(bf16[512,2048]{1,0:T(8,128)(2,1)} %get-tuple-element.98.last.refs_3_.refs_4_), channel_id=1, source_target_pairs={{0,1},{3,2},{4,5},{7,6},{8,9},{11,10},{12,13},{15,14},{16,17},{19,... | collective-permute-start | bytes 6291464 | tf_op jit(solution)/shard_map/ppermute | solution.py:81
  432.7 7.1 collective-permute-start.33
  446.3 310.0 %reduce-scatter.11.cloned.1.call-start = ((), (), s32[]{:S(2)}) async-start(), calls=%async_computation.15 | async-start | bytes 9437184 | tf_op jit(solution)/shard_map/reduce_scatter | solution.py:1055
  456.2 29.8 %all-to-all-start.4 = ((bf16[8,3,256,128]{3,2,1,0:T(8,128)(2,1)}), bf16[8,3,256,128]{3,2,1,0:T(8,128)(2,1)}, u32[]{:S(2)}, u32[]{:S(2)}) async-start(bf16[8,3,256,128]{3,2,1,0:T(8,128)(2,1)} %pad_maximum_fusion), calls=%async_computation.4 | async-start | bytes 3145728 | tf_op jit(solution)/shard_map/all_to_all | solution.py:1039
  460.8 323.6 %reduce-scatter.9.cloned.1.call-start = ((), (), s32[]{:S(2)}) async-start(), calls=%async_computation.14 | async-start | bytes 7077888 | tf_op jit(solution)/shard_map/reduce_scatter | solution.py:1054
  503.1 37.3 %collective-permute-start.36 = (bf16[3,128,2048]{2,1,0:T(8,128)(2,1)}, bf16[3,128,2048]{2,1,0:T(8,128)(2,1)}, u32[]{:S(2)}, u32[]{:S(2)}) collective-permute-start(bf16[3,128,2048]{2,1,0:T(8,128)(2,1)} %get-tuple-element.110.refs_1_), channel_id=1, source_target_pairs={{0,1},{3,2},{4,5},{7,6},{8,9},{11,10},{12,13},{15,14},{16,17},{19,... | collective-permute-start | bytes 4718600 | tf_op jit(solution)/shard_map/ppermute | solution.py:81
  506.5 86.5 %collective-permute-start.39 = (bf16[512,2048]{1,0:T(8,128)(2,1)}, bf16[512,2048]{1,0:T(8,128)(2,1)S(1)}, u32[]{:S(2)}, u32[]{:S(2)}) collective-permute-start(bf16[512,2048]{1,0:T(8,128)(2,1)} %add_convert_fusion), channel_id=1, source_target_pairs={{1,2},{2,1},{5,6},{6,5},{9,10},{10,9},{13,14},{14,13},{17,18},{18,... | collective-permute-start | bytes 6291464 | tf_op jit(solution)/shard_map/ppermute | solution.py:81
  507.3 66.8 %collective-permute-start.35 = (bf16[3,128,2048]{2,1,0:T(8,128)(2,1)}, bf16[3,128,2048]{2,1,0:T(8,128)(2,1)}, u32[]{:S(2)}, u32[]{:S(2)}) collective-permute-start(bf16[3,128,2048]{2,1,0:T(8,128)(2,1)} %get-tuple-element.109.refs_1_), channel_id=1, source_target_pairs={{0,1},{3,2},{4,5},{7,6},{8,9},{11,10},{12,13},{15,14},{16,17},{19,... | collective-permute-start | bytes 4718600 | tf_op jit(solution)/shard_map/ppermute | solution.py:81
  532.1 59.2 %copy-start.19 = (f32[4,512,8]{1,0,2:T(4,128)S(1)}, f32[4,512,8]{1,0,2:T(4,128)}, u32[]{:S(2)}) copy-start(f32[4,512,8]{1,0,2:T(4,128)} %get-tuple-element.166) | copy-start | bytes 196612
  544.4 29.8 %collective-permute-start.37 = (bf16[3,128,2048]{2,1,0:T(8,128)(2,1)}, bf16[3,128,2048]{2,1,0:T(8,128)(2,1)}, u32[]{:S(2)}, u32[]{:S(2)}) collective-permute-start(bf16[3,128,2048]{2,1,0:T(8,128)(2,1)} %add_convert_fusion.4), channel_id=1, source_target_pairs={{1,2},{2,1},{5,6},{6,5},{9,10},{10,9},{13,14},{14,13},{17,18},{18,... | collective-permute-start | bytes 4718600 | tf_op jit(solution)/shard_map/ppermute | solution.py:81
  546.2 61.7 %collective-permute-start.40 = (bf16[3,128,2048]{2,1,0:T(8,128)(2,1)}, bf16[3,128,2048]{2,1,0:T(8,128)(2,1)}, u32[]{:S(2)}, u32[]{:S(2)}) collective-permute-start(bf16[3,128,2048]{2,1,0:T(8,128)(2,1)} %get-tuple-element.115.refs_1_), channel_id=1, source_target_pairs={{0,1},{3,2},{4,5},{7,6},{8,9},{11,10},{12,13},{15,14},{16,17},{19,... | collective-permute-start | bytes 4718600 | tf_op jit(solution)/shard_map/ppermute | solution.py:81
  574.1 66.5 %collective-permute-start.38 = (bf16[3,128,2048]{2,1,0:T(8,128)(2,1)}, bf16[3,128,2048]{2,1,0:T(8,128)(2,1)}, u32[]{:S(2)}, u32[]{:S(2)}) collective-permute-start(bf16[3,128,2048]{2,1,0:T(8,128)(2,1)} %get-tuple-element.113.refs_1_), channel_id=1, source_target_pairs={{0,1},{3,2},{4,5},{7,6},{8,9},{11,10},{12,13},{15,14},{16,17},{19,... | collective-permute-start | bytes 4718600 | tf_op jit(solution)/shard_map/ppermute | solution.py:81
  607.9 25.7 %collective-permute-start.41 = (bf16[2,128,2048]{2,1,0:T(8,128)(2,1)}, bf16[2,128,2048]{2,1,0:T(8,128)(2,1)}, u32[]{:S(2)}, u32[]{:S(2)}) collective-permute-start(bf16[2,128,2048]{2,1,0:T(8,128)(2,1)} %mix_inward.4), channel_id=1, source_target_pairs={{1,0},{2,3},{5,4},{6,7},{9,8},{10,11},{13,12},{14,15},{17,16},{18,... | collective-permute-start | bytes 3145736 | tf_op jit(solution)/shard_map/ppermute | solution.py:81
  612.8 110.0 %collective-permute-start.46 = (bf16[3,128,2048]{2,1,0:T(8,128)(2,1)}, bf16[3,128,2048]{2,1,0:T(8,128)(2,1)}, u32[]{:S(2)}, u32[]{:S(2)}) collective-permute-start(bf16[3,128,2048]{2,1,0:T(8,128)(2,1)} %add_convert_fusion.1), channel_id=1, source_target_pairs={{1,2},{2,1},{5,6},{6,5},{9,10},{10,9},{13,14},{14,13},{17,18},{18,... | collective-permute-start | bytes 4718600 | tf_op jit(solution)/shard_map/ppermute | solution.py:81
  618.5 109.8 %collective-permute-start.44 = (bf16[3,128,2048]{2,1,0:T(8,128)(2,1)}, bf16[3,128,2048]{2,1,0:T(8,128)(2,1)S(1)}, u32[]{:S(2)}, u32[]{:S(2)}) collective-permute-start(bf16[3,128,2048]{2,1,0:T(8,128)(2,1)} %add_convert_fusion.2), channel_id=1, source_target_pairs={{1,2},{2,1},{5,6},{6,5},{9,10},{10,9},{13,14},{14,13},{17,18},{18,... | collective-permute-start | bytes 4718600 | tf_op jit(solution)/shard_map/ppermute | solution.py:81
  643.8 91.3 %collective-permute-start.42 = (bf16[3,128,2048]{2,1,0:T(8,128)(2,1)}, bf16[3,128,2048]{2,1,0:T(8,128)(2,1)S(1)}, u32[]{:S(2)}, u32[]{:S(2)}) collective-permute-start(bf16[3,128,2048]{2,1,0:T(8,128)(2,1)} %add_convert_fusion.3), channel_id=1, source_target_pairs={{1,2},{2,1},{5,6},{6,5},{9,10},{10,9},{13,14},{14,13},{17,18},{18,... | collective-permute-start | bytes 4718600 | tf_op jit(solution)/shard_map/ppermute | solution.py:81
  651.6 71.1 %all-to-all-start.5 = ((f32[4,512,16]{1,2,0:T(8,128)}), f32[4,512,16]{1,2,0:T(8,128)S(1)}, u32[]{:S(2)}, u32[]{:S(2)}) async-start(f32[4,512,16]{1,2,0:T(8,128)} %maximum_maximum_fusion), calls=%async_computation.8 | async-start | bytes 262144 | tf_op jit(solution)/shard_map/all_to_all | solution.py:1079
  727.0 32.1 %collective-permute-start.47 = (bf16[2,128,2048]{2,1,0:T(8,128)(2,1)}, bf16[2,128,2048]{2,1,0:T(8,128)(2,1)}, u32[]{:S(2)}, u32[]{:S(2)}) collective-permute-start(bf16[2,128,2048]{2,1,0:T(8,128)(2,1)} %mix_inward.7), channel_id=1, source_target_pairs={{1,0},{2,3},{5,4},{6,7},{9,8},{10,11},{13,12},{14,15},{17,16},{18,... | collective-permute-start | bytes 3145736 | tf_op jit(solution)/shard_map/ppermute | solution.py:81
  733.6 44.0 %collective-permute-start.45 = (bf16[2,128,2048]{2,1,0:T(8,128)(2,1)}, bf16[2,128,2048]{2,1,0:T(8,128)(2,1)S(1)}, u32[]{:S(2)}, u32[]{:S(2)}) collective-permute-start(bf16[2,128,2048]{2,1,0:T(8,128)(2,1)} %mix_inward.6), channel_id=1, source_target_pairs={{1,0},{2,3},{5,4},{6,7},{9,8},{10,11},{13,12},{14,15},{17,16},{18,... | collective-permute-start | bytes 3145736 | tf_op jit(solution)/shard_map/ppermute | solution.py:81
  740.4 55.7 %collective-permute-start.43 = (bf16[2,128,2048]{2,1,0:T(8,128)(2,1)}, bf16[2,128,2048]{2,1,0:T(8,128)(2,1)S(1)}, u32[]{:S(2)}, u32[]{:S(2)}) collective-permute-start(bf16[2,128,2048]{2,1,0:T(8,128)(2,1)} %mix_inward.5), channel_id=1, source_target_pairs={{1,0},{2,3},{5,4},{6,7},{9,8},{10,11},{13,12},{14,15},{17,16},{18,... | collective-permute-start | bytes 3145736 | tf_op jit(solution)/shard_map/ppermute | solution.py:81
  (38 other events, 166.8 us)
Sparse Core Ops, SparseCore 0:
  122.5 46.1 all-gather.5
  288.7 43.7 all-gather.7
  345.9 75.6 reduce-scatter.4
  446.4 50.9 reduce-scatter.6
  500.7 71.4 reduce-scatter.10
  575.4 61.6 reduce-scatter.8
